TPU v7x, 512 devices: a whole 4x8x8 slice. The times are simulated.
512 devices in a mesh: gx: 32 (over y, x), gy: 16 (over z, core).
Axes of the slice: x: 4, y: 8, z: 8, core: 2. Of those that a mesh axis runs over, the one named last changes fastest.
Arguments:
- right_side: float32 [128, 128, 512], P('gx', 'gy'), may hold values from -18 to 18
- labels: int32 [128, 128, 512], P('gx', 'gy'), may hold values from 0 to 2
- conduct_table: float32 [3], replicated, may hold values from 0.2 to 5
Outputs:
- correction: float32 [128, 128, 512], P('gx', 'gy')
All inputs are finite; a program needn't handle non-finite values.
Results may differ from a plain program's by a relative error of at most 0.0003.
Values sent between devices are 32-bit elements; how exact they have to be, the bound alone decides.
No kernel may reach another device: no remote copies, remote signals or barrier semaphores. Data moves between devices by JAX's collectives and lax.ppermute only.
A program may use at most 128 MiB of HBM per device.

v0:
```python
import jax
import jax.numpy as jnp
from jax import lax
from jax.sharding import PartitionSpec as P

SWEEPS = 8


OMEGA = 0.8


def extended(cells, sides, width):
    for axis, dim in sides:
        count = lax.axis_size(axis)
        ends = count - 1
        head = lax.slice_in_dim(cells, 0, width, axis=dim)
        tail = lax.slice_in_dim(cells, cells.shape[dim] - width, cells.shape[dim], axis=dim)
        cells = jnp.concatenate(
            [
                lax.ppermute(tail, axis, [(i, (i + 1) % count) for i in range(ends)]),
                cells,
                lax.ppermute(head, axis, [((i + 1) % count, i) for i in range(ends)]),
            ],
            axis=dim,
        )
    return cells


def lookup(labels, table):
    return jnp.where(labels == 0, table[0], jnp.where(labels == 1, table[1], table[2]))


def face_couplings(padded):
    own = padded[1:-1, 1:-1, 1:-1]
    own = jnp.where(own > 0.0, own, 1.0)

    def across(beside):
        beside = jnp.where(beside > 0.0, beside, own)
        return 2.0 * (own * beside) / (own + beside)

    return jnp.stack(
        [
            across(padded[:-2, 1:-1, 1:-1]),
            across(padded[2:, 1:-1, 1:-1]),
            across(padded[1:-1, :-2, 1:-1]),
            across(padded[1:-1, 2:, 1:-1]),
            across(padded[1:-1, 1:-1, :-2]),
            across(padded[1:-1, 1:-1, 2:]),
        ]
    )


def coupled(couplings, padded):
    total = couplings[0] * padded[:-2, 1:-1, 1:-1] + couplings[1] * padded[2:, 1:-1, 1:-1]
    total = total + couplings[2] * padded[1:-1, :-2, 1:-1] + couplings[3] * padded[1:-1, 2:, 1:-1]
    total = total + couplings[4] * padded[1:-1, 1:-1, :-2] + couplings[5] * padded[1:-1, 1:-1, 2:]
    return total


def relax(couplings, diagonal, source, field, padded):
    image = diagonal * field - coupled(couplings, padded)
    return field + OMEGA * (source - image) / diagonal


def residual_of(couplings, diagonal, source, field, padded):
    return source - (diagonal * field - coupled(couplings, padded))


def coarsen_couplings(couplings):
    extent = couplings.shape
    blocks = couplings.reshape(6, extent[1] // 2, 2, extent[2] // 2, 2, extent[3] // 2, 2)
    lower_one = jnp.sum(blocks[0][:, 0], axis=(2, 4))
    upper_one = jnp.sum(blocks[1][:, 1], axis=(2, 4))
    lower_two = jnp.sum(blocks[2][:, :, :, 0], axis=(1, 4))
    upper_two = jnp.sum(blocks[3][:, :, :, 1], axis=(1, 4))
    lower_three = jnp.sum(blocks[4][..., 0], axis=(1, 3))
    upper_three = jnp.sum(blocks[5][..., 1], axis=(1, 3))
    return jnp.stack([lower_one, upper_one, lower_two, upper_two, lower_three, upper_three])


def restrict(field):
    extent = field.shape
    return jnp.sum(
        field.reshape(extent[0] // 2, 2, extent[1] // 2, 2, extent[2] // 2, 2), axis=(1, 3, 5)
    )


def prolong(field):
    extent = field.shape
    spread = jnp.broadcast_to(
        field[:, None, :, None, :, None], (extent[0], 2, extent[1], 2, extent[2], 2)
    )
    return spread.reshape(2 * extent[0], 2 * extent[1], 2 * extent[2])


def pad_third(field):
    return jnp.pad(field, ((0, 0), (0, 0), (1, 1)))


def with_rim(field, level):
    if level == 0:
        padded = extended(field, (("gx", 0), ("gy", 1)), 1)
    elif level == 1:
        padded = extended(field, (("gx", 0), ("gy", 1)), 1)
    else:
        padded = extended(field, (("gx", 0), ("gy", 1)), 1)
    return pad_third(padded)


def from_zero(couplings, diagonal, source):
    empty = jnp.zeros_like(source)
    return relax(couplings, diagonal, source, empty, jnp.pad(empty, 1))


def shards(right_side, labels, conduct_table):
    conduct = lookup(labels, conduct_table)
    conduct_padded = extended(conduct, (("gx", 0), ("gy", 1)), 1)
    fine_couplings = face_couplings(pad_third(conduct_padded))
    fine_diagonal = jnp.sum(fine_couplings, axis=0)
    first_iterate = from_zero(fine_couplings, fine_diagonal, right_side)
    first_padded = pad_third(extended(first_iterate, (("gx", 0), ("gy", 1)), 1))
    fine_iterate = relax(fine_couplings, fine_diagonal, right_side, first_iterate, first_padded)
    fine_residual = residual_of(
        fine_couplings, fine_diagonal, right_side, fine_iterate, with_rim(fine_iterate, 0)
    )
    middle_source = restrict(fine_residual)
    middle_couplings = coarsen_couplings(fine_couplings)
    middle_diagonal = jnp.sum(middle_couplings, axis=0)
    middle_iterate = from_zero(middle_couplings, middle_diagonal, middle_source)
    middle_iterate = relax(
        middle_couplings,
        middle_diagonal,
        middle_source,
        middle_iterate,
        with_rim(middle_iterate, 1),
    )
    middle_residual = residual_of(
        middle_couplings,
        middle_diagonal,
        middle_source,
        middle_iterate,
        with_rim(middle_iterate, 1),
    )
    coarse_source = restrict(middle_residual)
    coarse_couplings = coarsen_couplings(middle_couplings)
    coarse_diagonal = jnp.sum(coarse_couplings, axis=0)
    coarse_iterate = from_zero(coarse_couplings, coarse_diagonal, coarse_source)
    for repeat in range(SWEEPS - 1):
        coarse_iterate = relax(
            coarse_couplings,
            coarse_diagonal,
            coarse_source,
            coarse_iterate,
            with_rim(coarse_iterate, 2),
        )
    middle_iterate = middle_iterate + prolong(coarse_iterate)
    middle_iterate = relax(
        middle_couplings,
        middle_diagonal,
        middle_source,
        middle_iterate,
        with_rim(middle_iterate, 1),
    )
    fine_iterate = fine_iterate + prolong(middle_iterate)
    return relax(fine_couplings, fine_diagonal, right_side, fine_iterate, with_rim(fine_iterate, 0))


def solution(mesh):
    in_specs = (P("gx", "gy", None), P("gx", "gy", None), P())
    out_specs = P("gx", "gy", None)
    return jax.shard_map(shards, mesh=mesh, in_specs=in_specs, out_specs=out_specs, check_vma=False)
```

profile of v0, /device:TPU:223, one launch (start us, length us, event | category | flops | bytes accessed | tf_op | source)
XLA Modules:
  0.0 334.9 jit_solution(735291682422212108)
XLA Ops:
  4.2 4.3 %collective-permute-start = (f32[1,8,512]{2,1,0:T(8,128)S(1)}, f32[1,8,512]{2,1,0:T(8,128)S(1)}, u32[]{:S(2)}, u32[]{:S(2)}) collective-permute-start(f32[1,8,512]{2,1,0:T(8,128)S(1)} %get-tuple-element.26), channel_id=1, source_target_pairs={{0,16},{16,32},{32,48},{48,64},{64,80},{80,96},{96,112},{112,128},... | collective-permute-start | bytes 49160 | tf_op jit(solution)/shard_map/ppermute | solution.py:20
  10.4 5.9 %collective-permute-done.1 = f32[1,8,512]{2,1,0:T(8,128)S(1)} collective-permute-done((f32[1,8,512]{2,1,0:T(8,128)S(1)}, f32[1,8,512]{2,1,0:T(8,128)S(1)}, u32[]{:S(2)}, u32[]{:S(2)}) %collective-permute-start.1) | collective-permute-done | bytes 16416 | tf_op jit(solution)/shard_map/ppermute | solution.py:22
  16.3 7.2 %collective-permute-start.2 = (f32[6,1,512]{2,1,0:T(1,128)S(1)}, f32[6,1,512]{2,1,0:T(1,128)S(1)}, u32[]{:S(2)}, u32[]{:S(2)}) collective-permute-start(f32[6,1,512]{2,1,0:T(1,128)S(1)} %get-tuple-element.18), channel_id=1, source_target_pairs={{0,1},{1,2},{2,3},{3,4},{4,5},{5,6},{6,7},{7,8},{8,9},{9,10},{10,1... | collective-permute-start | bytes 36872 | tf_op jit(solution)/shard_map/ppermute | solution.py:20
  25.5 4.3 %collective-permute-done.3 = f32[6,1,512]{2,1,0:T(1,128)S(1)} collective-permute-done((f32[6,1,512]{2,1,0:T(1,128)S(1)}, f32[6,1,512]{2,1,0:T(1,128)S(1)}, u32[]{:S(2)}, u32[]{:S(2)}) %collective-permute-start.3) | collective-permute-done | bytes 12320 | tf_op jit(solution)/shard_map/ppermute | solution.py:22
  31.0 5.6 %squeeze.64 = f32[2,2,4,2,256,2]{5,4,3,2,1,0:T(8,128)} reshape(f32[4,8,512]{2,1,0:T(8,128)S(1)} %get-tuple-element.7) | data formatting | bytes 131072 | tf_op jit(solution)/shard_map/squeeze | solution.py:76
  36.6 5.5 %squeeze.65 = f32[2,2,4,2,256,2]{5,4,3,2,1,0:T(8,128)} reshape(f32[4,8,512]{2,1,0:T(8,128)S(1)} %get-tuple-element.6) | data formatting | bytes 131072 | tf_op jit(solution)/shard_map/squeeze | solution.py:77
  42.2 5.5 %squeeze.62 = f32[2,2,4,2,256,2]{5,4,3,2,1,0:T(8,128)} reshape(f32[4,8,512]{2,1,0:T(8,128)S(1)} %get-tuple-element.9) | data formatting | bytes 131072 | tf_op jit(solution)/shard_map/squeeze | solution.py:74
  47.7 5.6 %squeeze.63 = f32[2,2,4,2,256,2]{5,4,3,2,1,0:T(8,128)} reshape(f32[4,8,512]{2,1,0:T(8,128)S(1)} %get-tuple-element.8) | data formatting | bytes 131072 | tf_op jit(solution)/shard_map/squeeze | solution.py:75
  55.2 3.6 %collective-permute-start.5 = (f32[1,8,512]{2,1,0:T(8,128)S(1)}, f32[1,8,512]{2,1,0:T(8,128)S(1)}, u32[]{:S(2)}, u32[]{:S(2)}) collective-permute-start(f32[1,8,512]{2,1,0:T(8,128)S(1)} %get-tuple-element.25), channel_id=1, source_target_pairs={{16,0},{32,16},{48,32},{64,48},{80,64},{96,80},{112,96},{128,112},... | collective-permute-start | bytes 49160 | tf_op jit(solution)/shard_map/ppermute | solution.py:22
  58.8 5.2 %slice_reduce_fusion = (f32[2,4,256]{2,1,0:T(4,128)S(1)}, f32[2,4,256]{2,1,0:T(4,128)S(1)}) fusion(f32[2,2,4,2,256,2]{5,4,3,2,1,0:T(8,128)} %squeeze.65, f32[2,2,4,2,256,2]{5,4,3,2,1,0:T(8,128)} %squeeze.64), kind=kLoop, calls=%fused_computation | loop fusion | flops 12288 | bytes 81920 | tf_op jit(solution)/shard_map/reduce_sum | solution.py:77
  64.6 5.6 %squeeze.60 = f32[2,2,4,2,256,2]{5,4,3,2,1,0:T(8,128)} reshape(f32[4,8,512]{2,1,0:T(8,128)S(1)} %get-tuple-element.11) | data formatting | bytes 131072 | tf_op jit(solution)/shard_map/squeeze | solution.py:72
  70.2 5.5 %squeeze.61 = f32[2,2,4,2,256,2]{5,4,3,2,1,0:T(8,128)} reshape(f32[4,8,512]{2,1,0:T(8,128)S(1)} %get-tuple-element.10) | data formatting | bytes 131072 | tf_op jit(solution)/shard_map/squeeze | solution.py:73
  84.9 5.0 %collective-permute-start.8 = (f32[1,8,512]{2,1,0:T(8,128)S(1)}, f32[1,8,512]{2,1,0:T(8,128)S(1)}, u32[]{:S(2)}, u32[]{:S(2)}) collective-permute-start(f32[1,8,512]{2,1,0:T(8,128)S(1)} %get-tuple-element.22), channel_id=1, source_target_pairs={{0,16},{16,32},{32,48},{48,64},{64,80},{80,96},{96,112},{112,128},... | collective-permute-start | bytes 49160 | tf_op jit(solution)/shard_map/ppermute | solution.py:20
  92.7 5.4 %collective-permute-done.9 = f32[1,8,512]{2,1,0:T(8,128)S(1)} collective-permute-done((f32[1,8,512]{2,1,0:T(8,128)S(1)}, f32[1,8,512]{2,1,0:T(8,128)S(1)}, u32[]{:S(2)}, u32[]{:S(2)}) %collective-permute-start.9) | collective-permute-done | bytes 16416 | tf_op jit(solution)/shard_map/ppermute | solution.py:22
  98.1 4.9 %collective-permute-start.10 = (f32[6,1,512]{2,1,0:T(1,128)S(1)}, f32[6,1,512]{2,1,0:T(1,128)S(1)}, u32[]{:S(2)}, u32[]{:S(2)}) collective-permute-start(f32[6,1,512]{2,1,0:T(1,128)S(1)} %get-tuple-element.14), channel_id=1, source_target_pairs={{0,1},{1,2},{2,3},{3,4},{4,5},{5,6},{6,7},{7,8},{8,9},{9,10},{10,1... | collective-permute-start | bytes 36872 | tf_op jit(solution)/shard_map/ppermute | solution.py:20
  105.5 3.7 %collective-permute-done.11 = f32[6,1,512]{2,1,0:T(1,128)S(1)} collective-permute-done((f32[6,1,512]{2,1,0:T(1,128)S(1)}, f32[6,1,512]{2,1,0:T(1,128)S(1)}, u32[]{:S(2)}, u32[]{:S(2)}) %collective-permute-start.11) | collective-permute-done | bytes 12320 | tf_op jit(solution)/shard_map/ppermute | solution.py:22
  109.5 5.5 %reshape.181 = f32[2,2,4,2,256,2]{5,4,3,2,1,0:T(8,128)} reshape(f32[4,8,512]{2,1,0:T(8,128)S(1)} %fusion.56) | data formatting | bytes 131072 | tf_op jit(solution)/shard_map/reshape | solution.py:84
  119.7 3.4 %collective-permute-start.13 = (f32[1,4,256]{2,1,0:T(4,128)S(1)}, f32[1,4,256]{2,1,0:T(4,128)S(1)}, u32[]{:S(2)}, u32[]{:S(2)}) collective-permute-start(f32[1,4,256]{2,1,0:T(4,128)S(1)} %get-tuple-element.39), channel_id=1, source_target_pairs={{16,0},{32,16},{48,32},{64,48},{80,64},{96,80},{112,96},{128,112},... | collective-permute-start | bytes 12296 | tf_op jit(solution)/shard_map/ppermute | solution.py:22
  123.6 3.7 %collective-permute-done.13 = f32[1,4,256]{2,1,0:T(4,128)S(1)} collective-permute-done((f32[1,4,256]{2,1,0:T(4,128)S(1)}, f32[1,4,256]{2,1,0:T(4,128)S(1)}, u32[]{:S(2)}, u32[]{:S(2)}) %collective-permute-start.13) | collective-permute-done | bytes 4128 | tf_op jit(solution)/shard_map/ppermute | solution.py:22
  133.0 3.6 %collective-permute-done.15 = f32[4,1,256]{2,1,0:T(1,128)S(1)} collective-permute-done((f32[4,1,256]{2,1,0:T(1,128)S(1)}, f32[4,1,256]{2,1,0:T(1,128)S(1)}, u32[]{:S(2)}, u32[]{:S(2)}) %collective-permute-start.15) | collective-permute-done | bytes 4128 | tf_op jit(solution)/shard_map/ppermute | solution.py:22
  138.7 3.4 %collective-permute-start.17 = (f32[1,4,256]{2,1,0:T(4,128)S(1)}, f32[1,4,256]{2,1,0:T(4,128)S(1)}, u32[]{:S(2)}, u32[]{:S(2)}) collective-permute-start(f32[1,4,256]{2,1,0:T(4,128)S(1)} %get-tuple-element.37), channel_id=1, source_target_pairs={{16,0},{32,16},{48,32},{64,48},{80,64},{96,80},{112,96},{128,112},... | collective-permute-start | bytes 12296 | tf_op jit(solution)/shard_map/ppermute | solution.py:22
  142.7 3.7 %collective-permute-done.17 = f32[1,4,256]{2,1,0:T(4,128)S(1)} collective-permute-done((f32[1,4,256]{2,1,0:T(4,128)S(1)}, f32[1,4,256]{2,1,0:T(4,128)S(1)}, u32[]{:S(2)}, u32[]{:S(2)}) %collective-permute-start.17) | collective-permute-done | bytes 4128 | tf_op jit(solution)/shard_map/ppermute | solution.py:22
  151.6 4.1 %collective-permute-done.19 = f32[4,1,256]{2,1,0:T(1,128)S(1)} collective-permute-done((f32[4,1,256]{2,1,0:T(1,128)S(1)}, f32[4,1,256]{2,1,0:T(1,128)S(1)}, u32[]{:S(2)}, u32[]{:S(2)}) %collective-permute-start.19) | collective-permute-done | bytes 4128 | tf_op jit(solution)/shard_map/ppermute | solution.py:22
  158.2 3.4 %collective-permute-start.21 = (f32[1,2,128]{2,1,0:T(2,128)S(1)}, f32[1,2,128]{2,1,0:T(2,128)S(1)}, u32[]{:S(2)}, u32[]{:S(2)}) collective-permute-start(f32[1,2,128]{2,1,0:T(2,128)S(1)} %fusion.206), channel_id=1, source_target_pairs={{16,0},{32,16},{48,32},{64,48},{80,64},{96,80},{112,96},{128,112},... | collective-permute-start | bytes 3080 | tf_op jit(solution)/shard_map/ppermute | solution.py:22
  161.6 4.3 %collective-permute-done.21 = f32[1,2,128]{2,1,0:T(2,128)S(1)} collective-permute-done((f32[1,2,128]{2,1,0:T(2,128)S(1)}, f32[1,2,128]{2,1,0:T(2,128)S(1)}, u32[]{:S(2)}, u32[]{:S(2)}) %collective-permute-start.21) | collective-permute-done | bytes 1056 | tf_op jit(solution)/shard_map/ppermute | solution.py:22
  170.9 4.2 %collective-permute-done.23 = f32[3,1,128]{2,1,0:T(1,128)S(1)} collective-permute-done((f32[3,1,128]{2,1,0:T(1,128)S(1)}, f32[3,1,128]{2,1,0:T(1,128)S(1)}, u32[]{:S(2)}, u32[]{:S(2)}) %collective-permute-start.23) | collective-permute-done | bytes 1568 | tf_op jit(solution)/shard_map/ppermute | solution.py:22
  177.1 3.4 %collective-permute-start.25 = (f32[1,2,128]{2,1,0:T(2,128)S(1)}, f32[1,2,128]{2,1,0:T(2,128)S(1)}, u32[]{:S(2)}, u32[]{:S(2)}) collective-permute-start(f32[1,2,128]{2,1,0:T(2,128)S(1)} %divide_add_fusion.5), channel_id=1, source_target_pairs={{16,0},{32,16},{48,32},{64,48},{80,64},{96,80},{112,96},{128,112},... | collective-permute-start | bytes 3080 | tf_op jit(solution)/shard_map/ppermute | solution.py:22
  180.5 4.3 %collective-permute-done.25 = f32[1,2,128]{2,1,0:T(2,128)S(1)} collective-permute-done((f32[1,2,128]{2,1,0:T(2,128)S(1)}, f32[1,2,128]{2,1,0:T(2,128)S(1)}, u32[]{:S(2)}, u32[]{:S(2)}) %collective-permute-start.25) | collective-permute-done | bytes 1056 | tf_op jit(solution)/shard_map/ppermute | solution.py:22
  189.8 4.2 %collective-permute-done.27 = f32[3,1,128]{2,1,0:T(1,128)S(1)} collective-permute-done((f32[3,1,128]{2,1,0:T(1,128)S(1)}, f32[3,1,128]{2,1,0:T(1,128)S(1)}, u32[]{:S(2)}, u32[]{:S(2)}) %collective-permute-start.27) | collective-permute-done | bytes 1568 | tf_op jit(solution)/shard_map/ppermute | solution.py:22
  196.1 3.4 %collective-permute-start.29 = (f32[1,2,128]{2,1,0:T(2,128)S(1)}, f32[1,2,128]{2,1,0:T(2,128)S(1)}, u32[]{:S(2)}, u32[]{:S(2)}) collective-permute-start(f32[1,2,128]{2,1,0:T(2,128)S(1)} %divide_add_fusion.4), channel_id=1, source_target_pairs={{16,0},{32,16},{48,32},{64,48},{80,64},{96,80},{112,96},{128,112},... | collective-permute-start | bytes 3080 | tf_op jit(solution)/shard_map/ppermute | solution.py:22
  199.5 4.3 %collective-permute-done.29 = f32[1,2,128]{2,1,0:T(2,128)S(1)} collective-permute-done((f32[1,2,128]{2,1,0:T(2,128)S(1)}, f32[1,2,128]{2,1,0:T(2,128)S(1)}, u32[]{:S(2)}, u32[]{:S(2)}) %collective-permute-start.29) | collective-permute-done | bytes 1056 | tf_op jit(solution)/shard_map/ppermute | solution.py:22
  208.8 4.2 %collective-permute-done.31 = f32[3,1,128]{2,1,0:T(1,128)S(1)} collective-permute-done((f32[3,1,128]{2,1,0:T(1,128)S(1)}, f32[3,1,128]{2,1,0:T(1,128)S(1)}, u32[]{:S(2)}, u32[]{:S(2)}) %collective-permute-start.31) | collective-permute-done | bytes 1568 | tf_op jit(solution)/shard_map/ppermute | solution.py:22
  215.0 3.4 %collective-permute-start.33 = (f32[1,2,128]{2,1,0:T(2,128)S(1)}, f32[1,2,128]{2,1,0:T(2,128)S(1)}, u32[]{:S(2)}, u32[]{:S(2)}) collective-permute-start(f32[1,2,128]{2,1,0:T(2,128)S(1)} %divide_add_fusion.3), channel_id=1, source_target_pairs={{16,0},{32,16},{48,32},{64,48},{80,64},{96,80},{112,96},{128,112},... | collective-permute-start | bytes 3080 | tf_op jit(solution)/shard_map/ppermute | solution.py:22
  218.4 4.3 %collective-permute-done.33 = f32[1,2,128]{2,1,0:T(2,128)S(1)} collective-permute-done((f32[1,2,128]{2,1,0:T(2,128)S(1)}, f32[1,2,128]{2,1,0:T(2,128)S(1)}, u32[]{:S(2)}, u32[]{:S(2)}) %collective-permute-start.33) | collective-permute-done | bytes 1056 | tf_op jit(solution)/shard_map/ppermute | solution.py:22
  227.7 4.2 %collective-permute-done.35 = f32[3,1,128]{2,1,0:T(1,128)S(1)} collective-permute-done((f32[3,1,128]{2,1,0:T(1,128)S(1)}, f32[3,1,128]{2,1,0:T(1,128)S(1)}, u32[]{:S(2)}, u32[]{:S(2)}) %collective-permute-start.35) | collective-permute-done | bytes 1568 | tf_op jit(solution)/shard_map/ppermute | solution.py:22
  234.0 3.4 %collective-permute-start.37 = (f32[1,2,128]{2,1,0:T(2,128)S(1)}, f32[1,2,128]{2,1,0:T(2,128)S(1)}, u32[]{:S(2)}, u32[]{:S(2)}) collective-permute-start(f32[1,2,128]{2,1,0:T(2,128)S(1)} %divide_add_fusion.2), channel_id=1, source_target_pairs={{16,0},{32,16},{48,32},{64,48},{80,64},{96,80},{112,96},{128,112},... | collective-permute-start | bytes 3080 | tf_op jit(solution)/shard_map/ppermute | solution.py:22
  237.4 4.3 %collective-permute-done.37 = f32[1,2,128]{2,1,0:T(2,128)S(1)} collective-permute-done((f32[1,2,128]{2,1,0:T(2,128)S(1)}, f32[1,2,128]{2,1,0:T(2,128)S(1)}, u32[]{:S(2)}, u32[]{:S(2)}) %collective-permute-start.37) | collective-permute-done | bytes 1056 | tf_op jit(solution)/shard_map/ppermute | solution.py:22
  246.7 4.2 %collective-permute-done.39 = f32[3,1,128]{2,1,0:T(1,128)S(1)} collective-permute-done((f32[3,1,128]{2,1,0:T(1,128)S(1)}, f32[3,1,128]{2,1,0:T(1,128)S(1)}, u32[]{:S(2)}, u32[]{:S(2)}) %collective-permute-start.39) | collective-permute-done | bytes 1568 | tf_op jit(solution)/shard_map/ppermute | solution.py:22
  253.0 3.4 %collective-permute-start.41 = (f32[1,2,128]{2,1,0:T(2,128)S(1)}, f32[1,2,128]{2,1,0:T(2,128)S(1)}, u32[]{:S(2)}, u32[]{:S(2)}) collective-permute-start(f32[1,2,128]{2,1,0:T(2,128)S(1)} %divide_add_fusion.1), channel_id=1, source_target_pairs={{16,0},{32,16},{48,32},{64,48},{80,64},{96,80},{112,96},{128,112},... | collective-permute-start | bytes 3080 | tf_op jit(solution)/shard_map/ppermute | solution.py:22
  256.3 4.3 %collective-permute-done.41 = f32[1,2,128]{2,1,0:T(2,128)S(1)} collective-permute-done((f32[1,2,128]{2,1,0:T(2,128)S(1)}, f32[1,2,128]{2,1,0:T(2,128)S(1)}, u32[]{:S(2)}, u32[]{:S(2)}) %collective-permute-start.41) | collective-permute-done | bytes 1056 | tf_op jit(solution)/shard_map/ppermute | solution.py:22
  265.7 4.2 %collective-permute-done.43 = f32[3,1,128]{2,1,0:T(1,128)S(1)} collective-permute-done((f32[3,1,128]{2,1,0:T(1,128)S(1)}, f32[3,1,128]{2,1,0:T(1,128)S(1)}, u32[]{:S(2)}, u32[]{:S(2)}) %collective-permute-start.43) | collective-permute-done | bytes 1568 | tf_op jit(solution)/shard_map/ppermute | solution.py:22
  275.3 4.3 %collective-permute-done.45 = f32[1,2,128]{2,1,0:T(2,128)S(1)} collective-permute-done((f32[1,2,128]{2,1,0:T(2,128)S(1)}, f32[1,2,128]{2,1,0:T(2,128)S(1)}, u32[]{:S(2)}, u32[]{:S(2)}) %collective-permute-start.45) | collective-permute-done | bytes 1056 | tf_op jit(solution)/shard_map/ppermute | solution.py:22
  284.6 4.2 %collective-permute-done.47 = f32[3,1,128]{2,1,0:T(1,128)S(1)} collective-permute-done((f32[3,1,128]{2,1,0:T(1,128)S(1)}, f32[3,1,128]{2,1,0:T(1,128)S(1)}, u32[]{:S(2)}, u32[]{:S(2)}) %collective-permute-start.47) | collective-permute-done | bytes 1568 | tf_op jit(solution)/shard_map/ppermute | solution.py:22
  294.6 4.3 %collective-permute-done.49 = f32[1,4,256]{2,1,0:T(4,128)S(1)} collective-permute-done((f32[1,4,256]{2,1,0:T(4,128)S(1)}, f32[1,4,256]{2,1,0:T(4,128)S(1)}, u32[]{:S(2)}, u32[]{:S(2)}) %collective-permute-start.49) | collective-permute-done | bytes 4128 | tf_op jit(solution)/shard_map/ppermute | solution.py:22
  303.9 4.2 %collective-permute-done.51 = f32[4,1,256]{2,1,0:T(1,128)S(1)} collective-permute-done((f32[4,1,256]{2,1,0:T(1,128)S(1)}, f32[4,1,256]{2,1,0:T(1,128)S(1)}, u32[]{:S(2)}, u32[]{:S(2)}) %collective-permute-start.51) | collective-permute-done | bytes 4128 | tf_op jit(solution)/shard_map/ppermute | solution.py:22
  310.9 4.0 %reshape.182 = f32[4,8,512]{2,1,0:T(8,128)S(1)} reshape(f32[2,2,4,2,256,2]{5,4,3,2,1,0:T(8,128)} %broadcast_in_dim.50) | data formatting | bytes 131072 | tf_op jit(solution)/shard_map/reshape | solution.py:93
  320.2 4.4 %collective-permute-done.53 = f32[1,8,512]{2,1,0:T(8,128)S(1)} collective-permute-done((f32[1,8,512]{2,1,0:T(8,128)S(1)}, f32[1,8,512]{2,1,0:T(8,128)S(1)}, u32[]{:S(2)}, u32[]{:S(2)}) %collective-permute-start.53) | collective-permute-done | bytes 16416 | tf_op jit(solution)/shard_map/ppermute | solution.py:22
  329.7 4.3 %collective-permute-done.55 = f32[6,1,512]{2,1,0:T(1,128)S(1)} collective-permute-done((f32[6,1,512]{2,1,0:T(1,128)S(1)}, f32[6,1,512]{2,1,0:T(1,128)S(1)}, u32[]{:S(2)}, u32[]{:S(2)}) %collective-permute-start.55) | collective-permute-done | bytes 12320 | tf_op jit(solution)/shard_map/ppermute | solution.py:22
  (165 shorter events, 123.5 us)
Async XLA Ops:
  4.2 6.3 %collective-permute-start = (f32[1,8,512]{2,1,0:T(8,128)S(1)}, f32[1,8,512]{2,1,0:T(8,128)S(1)}, u32[]{:S(2)}, u32[]{:S(2)}) collective-permute-start(f32[1,8,512]{2,1,0:T(8,128)S(1)} %get-tuple-element.26), channel_id=1, source_target_pairs={{0,16},{16,32},{32,48},{48,64},{64,80},{80,96},{96,112},{112,128},... | collective-permute-start | bytes 49160 | tf_op jit(solution)/shard_map/ppermute | solution.py:20
  8.5 7.8 %collective-permute-start.1 = (f32[1,8,512]{2,1,0:T(8,128)S(1)}, f32[1,8,512]{2,1,0:T(8,128)S(1)}, u32[]{:S(2)}, u32[]{:S(2)}) collective-permute-start(f32[1,8,512]{2,1,0:T(8,128)S(1)} %get-tuple-element.27), channel_id=1, source_target_pairs={{16,0},{32,16},{48,32},{64,48},{80,64},{96,80},{112,96},{128,112},... | collective-permute-start | bytes 49160 | tf_op jit(solution)/shard_map/ppermute | solution.py:22
  16.3 9.1 %collective-permute-start.2 = (f32[6,1,512]{2,1,0:T(1,128)S(1)}, f32[6,1,512]{2,1,0:T(1,128)S(1)}, u32[]{:S(2)}, u32[]{:S(2)}) collective-permute-start(f32[6,1,512]{2,1,0:T(1,128)S(1)} %get-tuple-element.18), channel_id=1, source_target_pairs={{0,1},{1,2},{2,3},{3,4},{4,5},{5,6},{6,7},{7,8},{8,9},{9,10},{10,1... | collective-permute-start | bytes 36872 | tf_op jit(solution)/shard_map/ppermute | solution.py:20
  23.5 6.2 %collective-permute-start.3 = (f32[6,1,512]{2,1,0:T(1,128)S(1)}, f32[6,1,512]{2,1,0:T(1,128)S(1)}, u32[]{:S(2)}, u32[]{:S(2)}) collective-permute-start(f32[6,1,512]{2,1,0:T(1,128)S(1)} %get-tuple-element.19), channel_id=1, source_target_pairs={{1,0},{2,1},{3,2},{4,3},{5,4},{6,5},{7,6},{8,7},{9,8},{10,9},{11,1... | collective-permute-start | bytes 36872 | tf_op jit(solution)/shard_map/ppermute | solution.py:22
  53.2 22.5 %collective-permute-start.4 = (f32[1,8,512]{2,1,0:T(8,128)S(1)}, f32[1,8,512]{2,1,0:T(8,128)S(1)}, u32[]{:S(2)}, u32[]{:S(2)}) collective-permute-start(f32[1,8,512]{2,1,0:T(8,128)S(1)} %get-tuple-element.24), channel_id=1, source_target_pairs={{0,16},{16,32},{32,48},{48,64},{64,80},{80,96},{96,112},{112,128},... | collective-permute-start | bytes 49160 | tf_op jit(solution)/shard_map/ppermute | solution.py:20
  55.2 20.6 %collective-permute-start.5 = (f32[1,8,512]{2,1,0:T(8,128)S(1)}, f32[1,8,512]{2,1,0:T(8,128)S(1)}, u32[]{:S(2)}, u32[]{:S(2)}) collective-permute-start(f32[1,8,512]{2,1,0:T(8,128)S(1)} %get-tuple-element.25), channel_id=1, source_target_pairs={{16,0},{32,16},{48,32},{64,48},{80,64},{96,80},{112,96},{128,112},... | collective-permute-start | bytes 49160 | tf_op jit(solution)/shard_map/ppermute | solution.py:22
  75.8 7.8 %collective-permute-start.6 = (f32[6,1,512]{2,1,0:T(1,128)S(1)}, f32[6,1,512]{2,1,0:T(1,128)S(1)}, u32[]{:S(2)}, u32[]{:S(2)}) collective-permute-start(f32[6,1,512]{2,1,0:T(1,128)S(1)} %get-tuple-element.16), channel_id=1, source_target_pairs={{0,1},{1,2},{2,3},{3,4},{4,5},{5,6},{6,7},{7,8},{8,9},{9,10},{10,1... | collective-permute-start | bytes 36872 | tf_op jit(solution)/shard_map/ppermute | solution.py:20
  78.3 6.2 %collective-permute-start.7 = (f32[6,1,512]{2,1,0:T(1,128)S(1)}, f32[6,1,512]{2,1,0:T(1,128)S(1)}, u32[]{:S(2)}, u32[]{:S(2)}) collective-permute-start(f32[6,1,512]{2,1,0:T(1,128)S(1)} %get-tuple-element.17), channel_id=1, source_target_pairs={{1,0},{2,1},{3,2},{4,3},{5,4},{6,5},{7,6},{8,7},{9,8},{10,9},{11,1... | collective-permute-start | bytes 36872 | tf_op jit(solution)/shard_map/ppermute | solution.py:22
  84.9 7.8 %collective-permute-start.8 = (f32[1,8,512]{2,1,0:T(8,128)S(1)}, f32[1,8,512]{2,1,0:T(8,128)S(1)}, u32[]{:S(2)}, u32[]{:S(2)}) collective-permute-start(f32[1,8,512]{2,1,0:T(8,128)S(1)} %get-tuple-element.22), channel_id=1, source_target_pairs={{0,16},{16,32},{32,48},{48,64},{64,80},{80,96},{96,112},{112,128},... | collective-permute-start | bytes 49160 | tf_op jit(solution)/shard_map/ppermute | solution.py:20
  89.8 8.3 %collective-permute-start.9 = (f32[1,8,512]{2,1,0:T(8,128)S(1)}, f32[1,8,512]{2,1,0:T(8,128)S(1)}, u32[]{:S(2)}, u32[]{:S(2)}) collective-permute-start(f32[1,8,512]{2,1,0:T(8,128)S(1)} %get-tuple-element.23), channel_id=1, source_target_pairs={{16,0},{32,16},{48,32},{64,48},{80,64},{96,80},{112,96},{128,112},... | collective-permute-start | bytes 49160 | tf_op jit(solution)/shard_map/ppermute | solution.py:22
  98.1 7.4 %collective-permute-start.10 = (f32[6,1,512]{2,1,0:T(1,128)S(1)}, f32[6,1,512]{2,1,0:T(1,128)S(1)}, u32[]{:S(2)}, u32[]{:S(2)}) collective-permute-start(f32[6,1,512]{2,1,0:T(1,128)S(1)} %get-tuple-element.14), channel_id=1, source_target_pairs={{0,1},{1,2},{2,3},{3,4},{4,5},{5,6},{6,7},{7,8},{8,9},{9,10},{10,1... | collective-permute-start | bytes 36872 | tf_op jit(solution)/shard_map/ppermute | solution.py:20
  103.0 6.2 %collective-permute-start.11 = (f32[6,1,512]{2,1,0:T(1,128)S(1)}, f32[6,1,512]{2,1,0:T(1,128)S(1)}, u32[]{:S(2)}, u32[]{:S(2)}) collective-permute-start(f32[6,1,512]{2,1,0:T(1,128)S(1)} %get-tuple-element.15), channel_id=1, source_target_pairs={{1,0},{2,1},{3,2},{4,3},{5,4},{6,5},{7,6},{8,7},{9,8},{10,9},{11,1... | collective-permute-start | bytes 36872 | tf_op jit(solution)/shard_map/ppermute | solution.py:22
  117.7 5.9 %collective-permute-start.12 = (f32[1,4,256]{2,1,0:T(4,128)S(1)}, f32[1,4,256]{2,1,0:T(4,128)S(1)}, u32[]{:S(2)}, u32[]{:S(2)}) collective-permute-start(f32[1,4,256]{2,1,0:T(4,128)S(1)} %get-tuple-element.38), channel_id=1, source_target_pairs={{0,16},{16,32},{32,48},{48,64},{64,80},{80,96},{96,112},{112,128},... | collective-permute-start | bytes 12296 | tf_op jit(solution)/shard_map/ppermute | solution.py:20
  119.7 7.7 %collective-permute-start.13 = (f32[1,4,256]{2,1,0:T(4,128)S(1)}, f32[1,4,256]{2,1,0:T(4,128)S(1)}, u32[]{:S(2)}, u32[]{:S(2)}) collective-permute-start(f32[1,4,256]{2,1,0:T(4,128)S(1)} %get-tuple-element.39), channel_id=1, source_target_pairs={{16,0},{32,16},{48,32},{64,48},{80,64},{96,80},{112,96},{128,112},... | collective-permute-start | bytes 12296 | tf_op jit(solution)/shard_map/ppermute | solution.py:22
  127.3 5.6 %collective-permute-start.14 = (f32[4,1,256]{2,1,0:T(1,128)S(1)}, f32[4,1,256]{2,1,0:T(1,128)S(1)}, u32[]{:S(2)}, u32[]{:S(2)}) collective-permute-start(f32[4,1,256]{2,1,0:T(1,128)S(1)} %get-tuple-element.32), channel_id=1, source_target_pairs={{0,1},{1,2},{2,3},{3,4},{4,5},{5,6},{6,7},{7,8},{8,9},{9,10},{10,1... | collective-permute-start | bytes 12296 | tf_op jit(solution)/shard_map/ppermute | solution.py:20
  130.4 6.1 %collective-permute-start.15 = (f32[4,1,256]{2,1,0:T(1,128)S(1)}, f32[4,1,256]{2,1,0:T(1,128)S(1)}, u32[]{:S(2)}, u32[]{:S(2)}) collective-permute-start(f32[4,1,256]{2,1,0:T(1,128)S(1)} %get-tuple-element.33), channel_id=1, source_target_pairs={{1,0},{2,1},{3,2},{4,3},{5,4},{6,5},{7,6},{8,7},{9,8},{10,9},{11,1... | collective-permute-start | bytes 12296 | tf_op jit(solution)/shard_map/ppermute | solution.py:22
  136.8 5.9 %collective-permute-start.16 = (f32[1,4,256]{2,1,0:T(4,128)S(1)}, f32[1,4,256]{2,1,0:T(4,128)S(1)}, u32[]{:S(2)}, u32[]{:S(2)}) collective-permute-start(f32[1,4,256]{2,1,0:T(4,128)S(1)} %get-tuple-element.36), channel_id=1, source_target_pairs={{0,16},{16,32},{32,48},{48,64},{64,80},{80,96},{96,112},{112,128},... | collective-permute-start | bytes 12296 | tf_op jit(solution)/shard_map/ppermute | solution.py:20
  138.7 7.7 %collective-permute-start.17 = (f32[1,4,256]{2,1,0:T(4,128)S(1)}, f32[1,4,256]{2,1,0:T(4,128)S(1)}, u32[]{:S(2)}, u32[]{:S(2)}) collective-permute-start(f32[1,4,256]{2,1,0:T(4,128)S(1)} %get-tuple-element.37), channel_id=1, source_target_pairs={{16,0},{32,16},{48,32},{64,48},{80,64},{96,80},{112,96},{128,112},... | collective-permute-start | bytes 12296 | tf_op jit(solution)/shard_map/ppermute | solution.py:22
  146.4 5.1 %collective-permute-start.18 = (f32[4,1,256]{2,1,0:T(1,128)S(1)}, f32[4,1,256]{2,1,0:T(1,128)S(1)}, u32[]{:S(2)}, u32[]{:S(2)}) collective-permute-start(f32[4,1,256]{2,1,0:T(1,128)S(1)} %get-tuple-element.30), channel_id=1, source_target_pairs={{0,1},{1,2},{2,3},{3,4},{4,5},{5,6},{6,7},{7,8},{8,9},{9,10},{10,1... | collective-permute-start | bytes 12296 | tf_op jit(solution)/shard_map/ppermute | solution.py:20
  149.5 6.1 %collective-permute-start.19 = (f32[4,1,256]{2,1,0:T(1,128)S(1)}, f32[4,1,256]{2,1,0:T(1,128)S(1)}, u32[]{:S(2)}, u32[]{:S(2)}) collective-permute-start(f32[4,1,256]{2,1,0:T(1,128)S(1)} %get-tuple-element.31), channel_id=1, source_target_pairs={{1,0},{2,1},{3,2},{4,3},{5,4},{6,5},{7,6},{8,7},{9,8},{10,9},{11,1... | collective-permute-start | bytes 12296 | tf_op jit(solution)/shard_map/ppermute | solution.py:22
  156.3 5.3 %collective-permute-start.20 = (f32[1,2,128]{2,1,0:T(2,128)S(1)}, f32[1,2,128]{2,1,0:T(2,128)S(1)}, u32[]{:S(2)}, u32[]{:S(2)}) collective-permute-start(f32[1,2,128]{2,1,0:T(2,128)S(1)} %fusion.206), channel_id=1, source_target_pairs={{0,16},{16,32},{32,48},{48,64},{64,80},{80,96},{96,112},{112,128},... | collective-permute-start | bytes 3080 | tf_op jit(solution)/shard_map/ppermute | solution.py:20
  158.2 7.6 %collective-permute-start.21 = (f32[1,2,128]{2,1,0:T(2,128)S(1)}, f32[1,2,128]{2,1,0:T(2,128)S(1)}, u32[]{:S(2)}, u32[]{:S(2)}) collective-permute-start(f32[1,2,128]{2,1,0:T(2,128)S(1)} %fusion.206), channel_id=1, source_target_pairs={{16,0},{32,16},{48,32},{64,48},{80,64},{96,80},{112,96},{128,112},... | collective-permute-start | bytes 3080 | tf_op jit(solution)/shard_map/ppermute | solution.py:22
  168.9 6.1 %collective-permute-start.23 = (f32[3,1,128]{2,1,0:T(1,128)S(1)}, f32[3,1,128]{2,1,0:T(1,128)S(1)}, u32[]{:S(2)}, u32[]{:S(2)}) collective-permute-start(f32[3,1,128]{2,1,0:T(1,128)S(1)} %get-tuple-element.53), channel_id=1, source_target_pairs={{1,0},{2,1},{3,2},{4,3},{5,4},{6,5},{7,6},{8,7},{9,8},{10,9},{11,1... | collective-permute-start | bytes 4616 | tf_op jit(solution)/shard_map/ppermute | solution.py:22
  175.2 5.3 %collective-permute-start.24 = (f32[1,2,128]{2,1,0:T(2,128)S(1)}, f32[1,2,128]{2,1,0:T(2,128)S(1)}, u32[]{:S(2)}, u32[]{:S(2)}) collective-permute-start(f32[1,2,128]{2,1,0:T(2,128)S(1)} %divide_add_fusion.5), channel_id=1, source_target_pairs={{0,16},{16,32},{32,48},{48,64},{64,80},{80,96},{96,112},{112,128},... | collective-permute-start | bytes 3080 | tf_op jit(solution)/shard_map/ppermute | solution.py:20
  177.1 7.6 %collective-permute-start.25 = (f32[1,2,128]{2,1,0:T(2,128)S(1)}, f32[1,2,128]{2,1,0:T(2,128)S(1)}, u32[]{:S(2)}, u32[]{:S(2)}) collective-permute-start(f32[1,2,128]{2,1,0:T(2,128)S(1)} %divide_add_fusion.5), channel_id=1, source_target_pairs={{16,0},{32,16},{48,32},{64,48},{80,64},{96,80},{112,96},{128,112},... | collective-permute-start | bytes 3080 | tf_op jit(solution)/shard_map/ppermute | solution.py:22
  187.9 6.1 %collective-permute-start.27 = (f32[3,1,128]{2,1,0:T(1,128)S(1)}, f32[3,1,128]{2,1,0:T(1,128)S(1)}, u32[]{:S(2)}, u32[]{:S(2)}) collective-permute-start(f32[3,1,128]{2,1,0:T(1,128)S(1)} %get-tuple-element.51), channel_id=1, source_target_pairs={{1,0},{2,1},{3,2},{4,3},{5,4},{6,5},{7,6},{8,7},{9,8},{10,9},{11,1... | collective-permute-start | bytes 4616 | tf_op jit(solution)/shard_map/ppermute | solution.py:22
  194.2 5.3 %collective-permute-start.28 = (f32[1,2,128]{2,1,0:T(2,128)S(1)}, f32[1,2,128]{2,1,0:T(2,128)S(1)}, u32[]{:S(2)}, u32[]{:S(2)}) collective-permute-start(f32[1,2,128]{2,1,0:T(2,128)S(1)} %divide_add_fusion.4), channel_id=1, source_target_pairs={{0,16},{16,32},{32,48},{48,64},{64,80},{80,96},{96,112},{112,128},... | collective-permute-start | bytes 3080 | tf_op jit(solution)/shard_map/ppermute | solution.py:20
  196.1 7.6 %collective-permute-start.29 = (f32[1,2,128]{2,1,0:T(2,128)S(1)}, f32[1,2,128]{2,1,0:T(2,128)S(1)}, u32[]{:S(2)}, u32[]{:S(2)}) collective-permute-start(f32[1,2,128]{2,1,0:T(2,128)S(1)} %divide_add_fusion.4), channel_id=1, source_target_pairs={{16,0},{32,16},{48,32},{64,48},{80,64},{96,80},{112,96},{128,112},... | collective-permute-start | bytes 3080 | tf_op jit(solution)/shard_map/ppermute | solution.py:22
  206.8 6.1 %collective-permute-start.31 = (f32[3,1,128]{2,1,0:T(1,128)S(1)}, f32[3,1,128]{2,1,0:T(1,128)S(1)}, u32[]{:S(2)}, u32[]{:S(2)}) collective-permute-start(f32[3,1,128]{2,1,0:T(1,128)S(1)} %get-tuple-element.49), channel_id=1, source_target_pairs={{1,0},{2,1},{3,2},{4,3},{5,4},{6,5},{7,6},{8,7},{9,8},{10,9},{11,1... | collective-permute-start | bytes 4616 | tf_op jit(solution)/shard_map/ppermute | solution.py:22
  213.1 5.3 %collective-permute-start.32 = (f32[1,2,128]{2,1,0:T(2,128)S(1)}, f32[1,2,128]{2,1,0:T(2,128)S(1)}, u32[]{:S(2)}, u32[]{:S(2)}) collective-permute-start(f32[1,2,128]{2,1,0:T(2,128)S(1)} %divide_add_fusion.3), channel_id=1, source_target_pairs={{0,16},{16,32},{32,48},{48,64},{64,80},{80,96},{96,112},{112,128},... | collective-permute-start | bytes 3080 | tf_op jit(solution)/shard_map/ppermute | solution.py:20
  215.0 7.6 %collective-permute-start.33 = (f32[1,2,128]{2,1,0:T(2,128)S(1)}, f32[1,2,128]{2,1,0:T(2,128)S(1)}, u32[]{:S(2)}, u32[]{:S(2)}) collective-permute-start(f32[1,2,128]{2,1,0:T(2,128)S(1)} %divide_add_fusion.3), channel_id=1, source_target_pairs={{16,0},{32,16},{48,32},{64,48},{80,64},{96,80},{112,96},{128,112},... | collective-permute-start | bytes 3080 | tf_op jit(solution)/shard_map/ppermute | solution.py:22
  225.8 6.1 %collective-permute-start.35 = (f32[3,1,128]{2,1,0:T(1,128)S(1)}, f32[3,1,128]{2,1,0:T(1,128)S(1)}, u32[]{:S(2)}, u32[]{:S(2)}) collective-permute-start(f32[3,1,128]{2,1,0:T(1,128)S(1)} %get-tuple-element.47), channel_id=1, source_target_pairs={{1,0},{2,1},{3,2},{4,3},{5,4},{6,5},{7,6},{8,7},{9,8},{10,9},{11,1... | collective-permute-start | bytes 4616 | tf_op jit(solution)/shard_map/ppermute | solution.py:22
  232.1 5.3 %collective-permute-start.36 = (f32[1,2,128]{2,1,0:T(2,128)S(1)}, f32[1,2,128]{2,1,0:T(2,128)S(1)}, u32[]{:S(2)}, u32[]{:S(2)}) collective-permute-start(f32[1,2,128]{2,1,0:T(2,128)S(1)} %divide_add_fusion.2), channel_id=1, source_target_pairs={{0,16},{16,32},{32,48},{48,64},{64,80},{80,96},{96,112},{112,128},... | collective-permute-start | bytes 3080 | tf_op jit(solution)/shard_map/ppermute | solution.py:20
  234.0 7.6 %collective-permute-start.37 = (f32[1,2,128]{2,1,0:T(2,128)S(1)}, f32[1,2,128]{2,1,0:T(2,128)S(1)}, u32[]{:S(2)}, u32[]{:S(2)}) collective-permute-start(f32[1,2,128]{2,1,0:T(2,128)S(1)} %divide_add_fusion.2), channel_id=1, source_target_pairs={{16,0},{32,16},{48,32},{64,48},{80,64},{96,80},{112,96},{128,112},... | collective-permute-start | bytes 3080 | tf_op jit(solution)/shard_map/ppermute | solution.py:22
  244.8 6.1 %collective-permute-start.39 = (f32[3,1,128]{2,1,0:T(1,128)S(1)}, f32[3,1,128]{2,1,0:T(1,128)S(1)}, u32[]{:S(2)}, u32[]{:S(2)}) collective-permute-start(f32[3,1,128]{2,1,0:T(1,128)S(1)} %get-tuple-element.45), channel_id=1, source_target_pairs={{1,0},{2,1},{3,2},{4,3},{5,4},{6,5},{7,6},{8,7},{9,8},{10,9},{11,1... | collective-permute-start | bytes 4616 | tf_op jit(solution)/shard_map/ppermute | solution.py:22
  251.0 5.3 %collective-permute-start.40 = (f32[1,2,128]{2,1,0:T(2,128)S(1)}, f32[1,2,128]{2,1,0:T(2,128)S(1)}, u32[]{:S(2)}, u32[]{:S(2)}) collective-permute-start(f32[1,2,128]{2,1,0:T(2,128)S(1)} %divide_add_fusion.1), channel_id=1, source_target_pairs={{0,16},{16,32},{32,48},{48,64},{64,80},{80,96},{96,112},{112,128},... | collective-permute-start | bytes 3080 | tf_op jit(solution)/shard_map/ppermute | solution.py:20
  253.0 7.6 %collective-permute-start.41 = (f32[1,2,128]{2,1,0:T(2,128)S(1)}, f32[1,2,128]{2,1,0:T(2,128)S(1)}, u32[]{:S(2)}, u32[]{:S(2)}) collective-permute-start(f32[1,2,128]{2,1,0:T(2,128)S(1)} %divide_add_fusion.1), channel_id=1, source_target_pairs={{16,0},{32,16},{48,32},{64,48},{80,64},{96,80},{112,96},{128,112},... | collective-permute-start | bytes 3080 | tf_op jit(solution)/shard_map/ppermute | solution.py:22
  263.7 6.1 %collective-permute-start.43 = (f32[3,1,128]{2,1,0:T(1,128)S(1)}, f32[3,1,128]{2,1,0:T(1,128)S(1)}, u32[]{:S(2)}, u32[]{:S(2)}) collective-permute-start(f32[3,1,128]{2,1,0:T(1,128)S(1)} %get-tuple-element.43), channel_id=1, source_target_pairs={{1,0},{2,1},{3,2},{4,3},{5,4},{6,5},{7,6},{8,7},{9,8},{10,9},{11,1... | collective-permute-start | bytes 4616 | tf_op jit(solution)/shard_map/ppermute | solution.py:22
  270.0 5.3 %collective-permute-start.44 = (f32[1,2,128]{2,1,0:T(2,128)S(1)}, f32[1,2,128]{2,1,0:T(2,128)S(1)}, u32[]{:S(2)}, u32[]{:S(2)}) collective-permute-start(f32[1,2,128]{2,1,0:T(2,128)S(1)} %divide_add_fusion), channel_id=1, source_target_pairs={{0,16},{16,32},{32,48},{48,64},{64,80},{80,96},{96,112},{112,128},... | collective-permute-start | bytes 3080 | tf_op jit(solution)/shard_map/ppermute | solution.py:20
  271.9 7.6 %collective-permute-start.45 = (f32[1,2,128]{2,1,0:T(2,128)S(1)}, f32[1,2,128]{2,1,0:T(2,128)S(1)}, u32[]{:S(2)}, u32[]{:S(2)}) collective-permute-start(f32[1,2,128]{2,1,0:T(2,128)S(1)} %divide_add_fusion), channel_id=1, source_target_pairs={{16,0},{32,16},{48,32},{64,48},{80,64},{96,80},{112,96},{128,112},... | collective-permute-start | bytes 3080 | tf_op jit(solution)/shard_map/ppermute | solution.py:22
  282.7 6.1 %collective-permute-start.47 = (f32[3,1,128]{2,1,0:T(1,128)S(1)}, f32[3,1,128]{2,1,0:T(1,128)S(1)}, u32[]{:S(2)}, u32[]{:S(2)}) collective-permute-start(f32[3,1,128]{2,1,0:T(1,128)S(1)} %get-tuple-element.41), channel_id=1, source_target_pairs={{1,0},{2,1},{3,2},{4,3},{5,4},{6,5},{7,6},{8,7},{9,8},{10,9},{11,1... | collective-permute-start | bytes 4616 | tf_op jit(solution)/shard_map/ppermute | solution.py:22
  289.3 5.3 %collective-permute-start.48 = (f32[1,4,256]{2,1,0:T(4,128)S(1)}, f32[1,4,256]{2,1,0:T(4,128)S(1)}, u32[]{:S(2)}, u32[]{:S(2)}) collective-permute-start(f32[1,4,256]{2,1,0:T(4,128)S(1)} %get-tuple-element.34), channel_id=1, source_target_pairs={{0,16},{16,32},{32,48},{48,64},{64,80},{80,96},{96,112},{112,128},... | collective-permute-start | bytes 12296 | tf_op jit(solution)/shard_map/ppermute | solution.py:20
  291.2 7.7 %collective-permute-start.49 = (f32[1,4,256]{2,1,0:T(4,128)S(1)}, f32[1,4,256]{2,1,0:T(4,128)S(1)}, u32[]{:S(2)}, u32[]{:S(2)}) collective-permute-start(f32[1,4,256]{2,1,0:T(4,128)S(1)} %get-tuple-element.35), channel_id=1, source_target_pairs={{16,0},{32,16},{48,32},{64,48},{80,64},{96,80},{112,96},{128,112},... | collective-permute-start | bytes 12296 | tf_op jit(solution)/shard_map/ppermute | solution.py:22
  298.9 5.0 %collective-permute-start.50 = (f32[4,1,256]{2,1,0:T(1,128)S(1)}, f32[4,1,256]{2,1,0:T(1,128)S(1)}, u32[]{:S(2)}, u32[]{:S(2)}) collective-permute-start(f32[4,1,256]{2,1,0:T(1,128)S(1)} %get-tuple-element.28), channel_id=1, source_target_pairs={{0,1},{1,2},{2,3},{3,4},{4,5},{5,6},{6,7},{7,8},{8,9},{9,10},{10,1... | collective-permute-start | bytes 12296 | tf_op jit(solution)/shard_map/ppermute | solution.py:20
  302.0 6.1 %collective-permute-start.51 = (f32[4,1,256]{2,1,0:T(1,128)S(1)}, f32[4,1,256]{2,1,0:T(1,128)S(1)}, u32[]{:S(2)}, u32[]{:S(2)}) collective-permute-start(f32[4,1,256]{2,1,0:T(1,128)S(1)} %get-tuple-element.29), channel_id=1, source_target_pairs={{1,0},{2,1},{3,2},{4,3},{5,4},{6,5},{7,6},{8,7},{9,8},{10,9},{11,1... | collective-permute-start | bytes 12296 | tf_op jit(solution)/shard_map/ppermute | solution.py:22
  314.9 5.3 %collective-permute-start.52 = (f32[1,8,512]{2,1,0:T(8,128)S(1)}, f32[1,8,512]{2,1,0:T(8,128)S(1)}, u32[]{:S(2)}, u32[]{:S(2)}) collective-permute-start(f32[1,8,512]{2,1,0:T(8,128)S(1)} %get-tuple-element.20), channel_id=1, source_target_pairs={{0,16},{16,32},{32,48},{48,64},{64,80},{80,96},{96,112},{112,128},... | collective-permute-start | bytes 49160 | tf_op jit(solution)/shard_map/ppermute | solution.py:20
  316.9 7.8 %collective-permute-start.53 = (f32[1,8,512]{2,1,0:T(8,128)S(1)}, f32[1,8,512]{2,1,0:T(8,128)S(1)}, u32[]{:S(2)}, u32[]{:S(2)}) collective-permute-start(f32[1,8,512]{2,1,0:T(8,128)S(1)} %get-tuple-element.21), channel_id=1, source_target_pairs={{16,0},{32,16},{48,32},{64,48},{80,64},{96,80},{112,96},{128,112},... | collective-permute-start | bytes 49160 | tf_op jit(solution)/shard_map/ppermute | solution.py:22
  327.8 6.2 %collective-permute-start.55 = (f32[6,1,512]{2,1,0:T(1,128)S(1)}, f32[6,1,512]{2,1,0:T(1,128)S(1)}, u32[]{:S(2)}, u32[]{:S(2)}) collective-permute-start(f32[6,1,512]{2,1,0:T(1,128)S(1)} %get-tuple-element.13), channel_id=1, source_target_pairs={{1,0},{2,1},{3,2},{4,3},{5,4},{6,5},{7,6},{8,7},{9,8},{10,9},{11,1... | collective-permute-start | bytes 36872 | tf_op jit(solution)/shard_map/ppermute | solution.py:22
  (11 other events, 72.5 us)
where the time goes:
time: 338 us; the launch traced here: 335 us
  starting transfers between devices  152 us (45%)
  waiting for transfers between devices  111 us (33%)
  local copies, waits for them, and re-layouts  50.3 us (15%)
  other arithmetic  19.7 us (6%)
    ppermute x28, waiting for transfers between devices, extended(): lax.ppermute(head, axis, [((i + 1) % count, i) for i in range(ends)])  111 us
    ppermute x28, starting transfers between devices, extended(): lax.ppermute(tail, axis, [(i, (i + 1) % count) for i in range(ends)])  80.9 us
    ppermute x28, starting transfers between devices, extended(): lax.ppermute(head, axis, [((i + 1) % count, i) for i in range(ends)])  71.5 us
  transfers between devices with their start and end apart: 56, of which 27 were waited for; matrix products, arithmetic and copies ran while one was open for 7% of the time, Pallas kernels for 0%

commit v1 on v0

v1 whole, which is shorter than its diff:
```python
import jax
import jax.numpy as jnp
from jax import lax
from jax.experimental import pallas as pl
from jax.experimental.pallas import tpu as pltpu
from jax.sharding import PartitionSpec as P

F32 = jnp.float32
LANES = 128
ROWS = 24
REACH = 7
PLANES = 4 + 2 * REACH
WINDOW = 8
KEEP = 0.2
OMEGA = 0.8


def iota(shape, dim):
    return lax.broadcasted_iota(jnp.int32, shape, dim)


def pick(values, index):
    return jnp.take_along_axis(values, index, axis=1)


def lane_roll(value, shift):
    return pltpu.roll(value, shift % LANES, value.ndim - 1)


def row_roll(value, shift):
    return pltpu.roll(value, shift % value.shape[-2], value.ndim - 2)


def split_kernel(labels_ref, source_ref, out_ref):
    lane = iota((8, LANES), 1)
    for plane in range(4):
        labels = labels_ref[plane]
        code = jnp.where(labels == 0, 8.0, jnp.where(labels == 1, 9.0, 11.0)).astype(F32)
        source = source_ref[plane]
        for which, values in enumerate((code, source)):
            parts = [values[:, LANES * j : LANES * (j + 1)] for j in range(4)]
            for residue in range(4):
                index = 4 * (lane % 32) + residue
                moved = [pick(part, index) for part in parts]
                low = jnp.where(lane < 32, moved[0], moved[1])
                high = jnp.where(lane < 96, moved[2], moved[3])
                out_ref[plane, which, residue] = jnp.where(lane < 64, low, high)


def join_kernel(low_ref, own_ref, high_ref, all_ref, up_ref, down_ref):
    for plane in range(4):
        for which in range(2):
            for residue in range(4):
                for part, ref in enumerate((low_ref, own_ref, high_ref)):
                    rows = pl.ds(8 * part, 8)
                    value = ref[plane, which, residue]
                    all_ref[plane, which, residue, rows] = value
                    if plane > 0:
                        up_ref[plane - 1, which, residue, rows] = value
                    if plane < 3:
                        down_ref[plane, which, residue, rows] = value


def fine_sum(fx_up, fx_low, fy, fz, v_up, v_low, v):
    lane = iota((ROWS, LANES), 1)
    total = fx_up * v_up + fx_low * v_low
    total = total + fy * row_roll(v, -1) + row_roll(fy * v, 1)
    zv = fz * v
    last = jnp.where(lane == LANES - 1, 0.0, lane_roll(v[0], -1))
    first = jnp.where(lane == 0, 0.0, lane_roll(zv[3], 1))
    lower = [first, fz[0] * v[0], fz[1] * v[1], fz[2] * v[2]]
    upper = [fz[0] * v[1], fz[1] * v[2], fz[2] * v[3], fz[3] * last]
    return total + jnp.stack([lower[r] + upper[r] for r in range(4)])


def middle_sum(fx_up, fx_low, fy, fz, v_up, v_low, v):
    lane = iota((ROWS, LANES), 1)
    total = fx_up * v_up + fx_low * v_low
    total = total + fy * row_roll(v, -2) + row_roll(fy * v, 2)
    last = jnp.where(lane == LANES - 1, 0.0, lane_roll(v[0], -1))
    first = jnp.where(lane == 0, 0.0, lane_roll(fz[1] * v[1], 1))
    return total + jnp.stack([first + fz[0] * v[1], fz[0] * v[0] + fz[1] * last])


def both_rows(value, bit):
    row = iota(value.shape, value.ndim - 2)
    return value + jnp.where((row & bit) == 0, row_roll(value, -bit), row_roll(value, bit))


def upper_row(value, bit):
    row = iota(value.shape, value.ndim - 2)
    return jnp.where((row & bit) != 0, value, row_roll(value, -bit))


def pair_table(table_ref):
    lane = iota((8, LANES), 1)

    def at(*keys):
        hit = lane == keys[0]
        for key in keys[1:]:
            hit = hit | (lane == key)
        return hit

    one = jnp.where(at(8, 16, 17, 19), table_ref[0], jnp.where(at(9, 18, 20), table_ref[1], jnp.where(at(11, 22), table_ref[2], 1.0)))
    two = jnp.where(at(8, 16), table_ref[0], jnp.where(at(9, 17, 18), table_ref[1], jnp.where(at(11, 19, 20, 22), table_ref[2], 1.0)))
    return 2.0 * (one * two) / (one + two)


def up_kernel(
    spot_ref, table_ref, low2_ref, low1_ref, own_ref, high1_ref, high2_ref,
    chunk_ref, ends_ref, fx_out, fy_out, fz_out, w_out, s_out, v_out,
    fxm_out, fym_out, fzm_out, wm_out, sm_out, vm_out, root_out,
    code, source, fx, fy, fz, zlow, diag, weight, first, second,
    fxm, fym, fzm, zlowm, diagm, weightm, sourcem, firstm, secondm,
):
    x0 = 4 * spot_ref[0]
    y0 = 8 * spot_ref[1]
    nx = 4 * spot_ref[2]
    ny = 8 * spot_ref[3]
    table = pair_table(table_ref)
    at = 0
    for ref in (low2_ref, low1_ref, own_ref, high1_ref, high2_ref):
        for plane in range(ref.shape[0]):
            code[at] = ref[plane, 0].astype(jnp.int32)
            source[at] = ref[plane, 1]
            at += 1

    row = iota((ROWS, LANES), 0)
    lane = iota((ROWS, LANES), 1)
    y = y0 - 8 + row
    rowmask = jnp.where((y >= 0) & (y < ny), 1.0, 0.0)

    def planemask(x):
        return jnp.where((x >= 0) & (x < nx), 1.0, 0.0).astype(F32)

    def look(key):
        flat = key.reshape(-1, LANES)
        parts = [pick(table, flat[8 * k : 8 * k + 8]) for k in range(flat.shape[0] // 8)]
        return jnp.concatenate(parts, axis=0).reshape(key.shape)

    def faces(p, carry):
        here = code[p]
        fx[p] = look(here + code[p + 1])
        fy[p] = look(here + row_roll(here, -1))
        beyond = jnp.where(lane == LANES - 1, 0, lane_roll(here[0], -1))
        after = jnp.stack([here[1], here[2], here[3], beyond])
        fz_here = look(here + after)
        fz[p] = fz_here
        zlow[p] = jnp.where(lane == 0, look(here[0]), lane_roll(fz_here[3], 1))
        return carry

    lax.fori_loop(0, PLANES - 1, faces, 0)

    def start(p, carry):
        fy_here = fy[p]
        fz_here = fz[p]
        lower = jnp.stack([zlow[p], fz_here[0], fz_here[1], fz_here[2]])
        total = fx[p] + fx[p - 1] + fy_here + row_roll(fy_here, 1) + fz_here + lower
        diag[p] = total
        w = (OMEGA * planemask(x0 - REACH + p) * rowmask) / total
        weight[p] = w
        first[p] = w * source[p]
        return carry

    lax.fori_loop(1, PLANES - 1, start, 0)

    def sweep(p, carry):
        v = first[p]
        image = fine_sum(fx[p], fx[p - 1], fy[p], fz[p], first[p + 1], first[p - 1], v)
        second[p] = KEEP * v + weight[p] * (source[p] + image)
        return carry

    lax.fori_loop(2, PLANES - 2, sweep, 0)

    def halves(value):
        return jnp.stack([value[0] + value[1], value[2] + value[3]])

    def residual(p):
        v = second[p]
        image = fine_sum(fx[p], fx[p - 1], fy[p], fz[p], second[p + 1], second[p - 1], v)
        return source[p] - diag[p] * v + image

    def coarse_face(k, carry):
        fxm[k] = both_rows(halves(fx[2 + 2 * k]), 1)
        return carry

    lax.fori_loop(0, 7, coarse_face, 0)

    def middle(k, carry):
        pa = 1 + 2 * k
        pb = 2 + 2 * k
        sm = both_rows(halves(residual(pa) + residual(pb)), 1)
        fym_here = upper_row(halves(fy[pa] + fy[pb]), 1)
        fz_two = fz[pa] + fz[pb]
        fzm_here = both_rows(jnp.stack([fz_two[1], fz_two[3]]), 1)
        zlow_here = both_rows(zlow[pa] + zlow[pb], 1)
        lower = jnp.stack([zlow_here, fzm_here[0]])
        total = fxm[k] + fxm[k - 1] + fym_here + row_roll(fym_here, 2) + fzm_here + lower
        w = (OMEGA * planemask(x0 - REACH + pa) * rowmask) / total
        fym[k] = fym_here
        fzm[k] = fzm_here
        zlowm[k] = zlow_here
        diagm[k] = total
        weightm[k] = w
        sourcem[k] = sm
        firstm[k] = w * sm
        return carry

    lax.fori_loop(1, 7, middle, 0)

    def middle_sweep(k, carry):
        v = firstm[k]
        image = middle_sum(fxm[k], fxm[k - 1], fym[k], fzm[k], firstm[k + 1], firstm[k - 1], v)
        secondm[k] = KEEP * v + weightm[k] * (sourcem[k] + image)
        return carry

    lax.fori_loop(2, 6, middle_sweep, 0)

    coarse_source = jnp.zeros((ROWS, LANES), F32)
    for k in (3, 4):
        v = secondm[k]
        image = middle_sum(fxm[k], fxm[k - 1], fym[k], fzm[k], secondm[k + 1], secondm[k - 1], v)
        left = sourcem[k] - diagm[k] * v + image
        coarse_source = coarse_source + left[0] + left[1]
    coarse_source = both_rows(coarse_source, 2)

    def xface(big):
        value = fxm[2 * big + 4]
        return both_rows(value[0] + value[1], 2)

    xfaces = {big: xface(big) for big in (-2, -1, 0, 1)}
    roots = {}
    keep = None
    for big in (-1, 0, 1):
        ka = 2 * big + 3
        ysum = fym[ka] + fym[ka + 1]
        yface = upper_row(ysum[0] + ysum[1], 2)
        zsum = fzm[ka] + fzm[ka + 1]
        zface = both_rows(zsum[1], 2)
        zbelow = both_rows(zlowm[ka] + zlowm[ka + 1], 2)
        total = xfaces[big] + xfaces[big - 1] + yface + row_roll(yface, 4) + zface + zbelow
        root = lax.rsqrt(total) * (planemask(x0 + 4 * big) * rowmask)
        roots[big] = root
        root_out[big + 1] = root
        if big == 0:
            keep = (yface, zface)
    root = roots[0]
    cx = OMEGA * xfaces[0] * root * roots[1]
    cy = OMEGA * keep[0] * root * row_roll(root, -4)
    cz = OMEGA * keep[1] * root * jnp.where(lane == LANES - 1, 0.0, lane_roll(root, -1))
    lines = []
    for value in (OMEGA * root * coarse_source, cx, cy, cz):
        lines.append(value[8:9])
        lines.append(value[12:13])
    for at_row in (10, 12):
        for k in (3, 4):
            for half in range(2):
                lines.append(secondm[k, half, at_row : at_row + 1])
    chunk = jnp.concatenate(lines, axis=0)
    for peer in range(chunk_ref.shape[0]):
        chunk_ref[peer] = chunk
    for k in (3, 4):
        mids = [secondm[k, half, 8 + 2 * m : 9 + 2 * m] for half in range(2) for m in range(4)]
        ends_ref[k - 3] = jnp.concatenate(mids, axis=0)

    own_rows = pl.ds(8, 8)
    for k in range(5):
        fx_out[k] = fx[REACH - 1 + k, :, own_rows]
        fxm_out[k] = fxm[1 + k]
    for k in range(4):
        p = REACH + k
        fy_out[k] = fy[p]
        fz_out[k] = fz[p, :, own_rows]
        w_out[k] = weight[p, :, own_rows]
        s_out[k] = source[p, :, own_rows]
        fym_out[k] = fym[2 + k]
        fzm_out[k] = fzm[2 + k]
        wm_out[k] = weightm[2 + k]
        sm_out[k] = sourcem[2 + k]
        vm_out[k] = secondm[2 + k]
    for k in range(6):
        v_out[k] = second[REACH - 1 + k]


def window_kernel(spot_ref, got_ref, ends_ref, out_ref, chunk):
    mine = spot_ref[1]
    count = got_ref.shape[0]
    for step in range(9):
        block = mine + (step - 4)
        inside = jnp.where((block >= 0) & (block < count), 1.0, 0.0).astype(F32)
        value = got_ref[jnp.clip(block, 0, count - 1), pl.ds(0, 8)] * inside
        for which in range(4):
            chunk[pl.ds(18 * which + 2 * step, 2)] = value[2 * which : 2 * which + 2]
    body = chunk[...]
    low = ends_ref[0]
    high = ends_ref[1]
    for peer in range(out_ref.shape[0]):
        out_ref[peer, pl.ds(0, 72)] = body
        above = (spot_ref[0] < peer).astype(F32)
        out_ref[peer, pl.ds(72, 8)] = low * above + high * (1.0 - above)


def down_kernel(
    spot_ref, planes_ref, rows_ref, fx, fy, fz, w, s, v2,
    fxm, fym, fzm, wm, sm, vm, root,
    out_ref,
    parts, state, field, third, total,
):
    mine_x = spot_ref[0]
    mine_y = spot_ref[1]
    count_x = planes_ref.shape[0]
    count_y = rows_ref.shape[0]
    width = 2 * WINDOW + 1
    lane = iota((ROWS, LANES), 1)
    row = iota((ROWS, LANES), 0)

    def load(step, carry):
        plane = mine_x + (step - WINDOW)
        inside = jnp.where((plane >= 0) & (plane < count_x), 1.0, 0.0).astype(F32)
        spot = jnp.clip(plane, 0, count_x - 1)
        for which in range(4):
            value = planes_ref[spot, pl.ds(18 * which, ROWS)] if which < 3 else jnp.concatenate(
                [planes_ref[spot, pl.ds(54, 18)], jnp.zeros((ROWS - 18, LANES), F32)], axis=0)
            value = jnp.where(row < 18, value * inside, 0.0)
            parts[which, step] = value
            if which == 0:
                state[0, step] = value
        return carry

    lax.fori_loop(0, width, load, 0)

    for turn in range(1, WINDOW):
        old = (turn - 1) % 2
        new = turn % 2

        def sweep(step, carry):
            v = state[old, step]
            cy = parts[2, step]
            cz = parts[3, step]
            value = KEEP * v + parts[0, step]
            value = value + parts[1, step] * state[old, step + 1] + parts[1, step - 1] * state[old, step - 1]
            value = value + cy * row_roll(v, -1) + row_roll(cy * v, 1)
            value = value + cz * lane_roll(v, -1) + lane_roll(cz * v, 1)
            state[new, step] = value
            return carry

        lax.fori_loop(turn, width - turn, sweep, 0)

    last = (WINDOW - 1) % 2
    spread = []
    for big in range(3):
        value = state[last, WINDOW - 1 + big]
        picked = jnp.zeros((ROWS, LANES), F32)
        for k in range(4):
            line = jnp.broadcast_to(value[7 + k : 8 + k], (ROWS, LANES))
            picked = jnp.where((row >= 4 + 4 * k) & (row < 8 + 4 * k), line, picked)
        spread.append(picked * root[big])

    def line_block(ref, spot, inside, base):
        halves = []
        for half in range(2):
            rows = []
            for m in range(4):
                line = ref[spot, pl.ds(base + 4 * half + m, 1)] * inside
                rows += [line, line]
            pad = jnp.zeros((8, LANES), F32)
            halves.append(jnp.concatenate([pad] + [jnp.concatenate(rows, axis=0)] + [pad], axis=0))
        return jnp.stack(halves)

    below = jnp.where(mine_x > 0, 1.0, 0.0).astype(F32)
    above = jnp.where(mine_x < count_x - 1, 1.0, 0.0).astype(F32)
    field[0] = line_block(planes_ref, jnp.maximum(mine_x - 1, 0), below, 72) + spread[0]
    field[5] = line_block(planes_ref, jnp.minimum(mine_x + 1, count_x - 1), above, 72) + spread[2]
    field[1] = vm[0] + spread[0]
    field[4] = vm[3] + spread[2]
    left = jnp.where(mine_y > 0, 1.0, 0.0).astype(F32)
    right = jnp.where(mine_y < count_y - 1, 1.0, 0.0).astype(F32)
    left_spot = jnp.maximum(mine_y - 1, 0)
    right_spot = jnp.minimum(mine_y + 1, count_y - 1)
    for k in range(2):
        halves = []
        for half in range(2):
            value = vm[1 + k, half]
            lower = rows_ref[left_spot, pl.ds(12 + 2 * k + half, 1)] * left
            upper = rows_ref[right_spot, pl.ds(8 + 2 * k + half, 1)] * right
            value = jnp.where((row >= 4) & (row < 6), jnp.broadcast_to(lower, (ROWS, LANES)), value)
            value = jnp.where((row >= 18) & (row < 20), jnp.broadcast_to(upper, (ROWS, LANES)), value)
            halves.append(value)
        field[2 + k] = jnp.stack(halves) + spread[1]

    for k in range(4):
        v = field[k + 1]
        image = middle_sum(fxm[k + 1], fxm[k], fym[k], fzm[k], field[k + 2], field[k], v)
        third[k] = KEEP * v + wm[k] * (sm[k] + image)

    for p in range(6):
        mid = third[(p + 1) // 2]
        total[p] = v2[p] + jnp.stack([mid[0], mid[0], mid[1], mid[1]])

    lane8 = iota((8, LANES), 1)
    for p in range(4):
        up = total[p + 2, :, pl.ds(8, 8)]
        low = total[p, :, pl.ds(8, 8)]
        v = total[p + 1, :, pl.ds(8, 8)]
        image = fx[p + 1] * up + fx[p] * low
        image = image + fy[p, :, pl.ds(8, 8)] * total[p + 1, :, pl.ds(9, 8)]
        image = image + fy[p, :, pl.ds(7, 8)] * total[p + 1, :, pl.ds(7, 8)]
        zc = fz[p]
        end = jnp.where(lane8 == LANES - 1, 0.0, lane_roll(v[0], -1))
        begin = jnp.where(lane8 == 0, 0.0, lane_roll(zc[3] * v[3], 1))
        below_z = [begin, zc[0] * v[0], zc[1] * v[1], zc[2] * v[2]]
        above_z = [zc[0] * v[1], zc[1] * v[2], zc[2] * v[3], zc[3] * end]
        done = []
        for r in range(4):
            done.append(KEEP * v[r] + w[p, r] * (s[p, r] + image[r] + below_z[r] + above_z[r]))
        for j in range(4):
            index = 32 * j + lane8 // 4
            moved = [pick(done[r], index) for r in range(4)]
            odd = lane8 % 4
            low_pair = jnp.where(odd == 0, moved[0], moved[1])
            high_pair = jnp.where(odd == 2, moved[2], moved[3])
            out_ref[p, :, LANES * j : LANES * (j + 1)] = jnp.where(odd < 2, low_pair, high_pair)


VMEM = pl.BlockSpec(memory_space=pltpu.VMEM)
SMEM = pl.BlockSpec(memory_space=pltpu.SMEM)
PARAMS = pltpu.CompilerParams(vmem_limit_bytes=48 * 1024 * 1024)


def call(kernel, specs, outs, scratch, *args):
    return pl.pallas_call(
        kernel,
        in_specs=specs,
        out_specs=[VMEM] * len(outs),
        out_shape=[jax.ShapeDtypeStruct(shape, F32) for shape in outs],
        scratch_shapes=scratch,
        compiler_params=PARAMS,
    )(*args)


def shifted(value, axis, step):
    count = lax.axis_size(axis)
    if step > 0:
        pairs = [(i, i + step) for i in range(count - step)]
    else:
        pairs = [(i - step, i) for i in range(count + step)]
    return lax.ppermute(value, axis, pairs)


def shards(right_side, labels, conduct_table):
    nx = lax.axis_size("gx")
    ny = lax.axis_size("gy")
    spot = jnp.stack([lax.axis_index("gx"), lax.axis_index("gy"), jnp.int32(nx), jnp.int32(ny)]).astype(jnp.int32)
    (own,) = call(split_kernel, [VMEM] * 2, [(4, 2, 4, 8, LANES)], [], labels, right_side)
    low = shifted(own, "gy", 1)
    high = shifted(own, "gy", -1)
    wide, up, down = call(
        join_kernel,
        [VMEM] * 3,
        [(4, 2, 4, ROWS, LANES), (3, 2, 4, ROWS, LANES), (3, 2, 4, ROWS, LANES)],
        [],
        low, own, high,
    )
    low1 = shifted(wide, "gx", 1)
    high1 = shifted(wide, "gx", -1)
    low2 = shifted(up, "gx", 2)
    high2 = shifted(down, "gx", -2)

    fine = (4, ROWS, LANES)
    mid = (2, ROWS, LANES)
    tile = (4, 8, LANES)

    def room(*shape):
        return pltpu.VMEM(shape, F32)

    outs = call(
        up_kernel,
        [SMEM, SMEM] + [VMEM] * 5,
        [
            (ny, 16, LANES), (2, 8, LANES),
            (5,) + tile, (4,) + fine, (4,) + tile, (4,) + tile, (4,) + tile, (6,) + fine,
            (5,) + mid, (4,) + mid, (4,) + mid, (4,) + mid, (4,) + mid, (4,) + mid,
            (3, ROWS, LANES),
        ],
        [pltpu.VMEM((PLANES,) + fine, jnp.int32), room(PLANES, *fine)]
        + [room(PLANES, *fine)] * 3
        + [room(PLANES, ROWS, LANES)]
        + [room(PLANES, *fine)] * 4
        + [room(8, *mid)] * 3
        + [room(8, ROWS, LANES)]
        + [room(8, *mid)] * 5,
        spot, conduct_table, low2, low1, wide, high1, high2,
    )
    chunk, ends = outs[:2]
    rows = lax.all_to_all(chunk, "gy", 0, 0, tiled=True)
    (planes,) = call(window_kernel, [SMEM, VMEM, VMEM], [(nx, 80, LANES)], [room(72, LANES)], spot, rows, ends)
    planes = lax.all_to_all(planes, "gx", 0, 0, tiled=True)
    width = 2 * WINDOW + 1
    (correction,) = call(
        down_kernel,
        [SMEM] + [VMEM] * 15,
        [(4, 8, 4 * LANES)],
        [room(4, width, ROWS, LANES), room(2, width, ROWS, LANES), room(6, *mid), room(4, *mid), room(6, *fine)],
        spot, planes, rows, *outs[2:],
    )
    return correction


def solution(mesh):
    in_specs = (P("gx", "gy", None), P("gx", "gy", None), P())
    out_specs = P("gx", "gy", None)
    return jax.shard_map(shards, mesh=mesh, in_specs=in_specs, out_specs=out_specs, check_vma=False)
```

time: 338 us -> 123 us (0.36)
  the two profiles are of different devices: /device:TPU:223 before, /device:TPU:1 now
where the time goes in v1:
time: 123 us
  blocking collectives  66.8 us (54%)
  waiting for transfers between devices  20.5 us (17%)
  starting transfers between devices  18.6 us (15%)
  Pallas kernels  14.7 us (12%)
  local copies, waits for them, and re-layouts  2.33 us (2%)
    all_to_all x1, blocking collectives, shards(): planes = lax.all_to_all(planes, 'gx', 0, 0, tiled=True)  51.1 us
    ppermute x6, waiting for transfers between devices, shifted(): return lax.ppermute(value, axis, pairs)  20.5 us
    ppermute x6, starting transfers between devices, shifted(): return lax.ppermute(value, axis, pairs)  18.6 us
    all_to_all x1, blocking collectives, shards(): rows = lax.all_to_all(chunk, 'gy', 0, 0, tiled=True)  15.7 us
    pallas_call x5, Pallas kernels, call(): pl.pallas_call(kernel, in_specs=specs, out_specs=[VMEM] * len(outs), out_...  14.7 us
  transfers between devices with their start and end apart: 6, of which 2 were waited for; matrix products, arithmetic and copies ran while one was open for 0% of the time, Pallas kernels for 0%

profile of v1, /device:TPU:1, one launch (start us, length us, event | category | flops | bytes accessed | tf_op | source)
XLA Modules:
  0.0 123.1 jit_solution(14397842582793125952)
XLA Ops:
  0.0 0.0 copy-start
  0.0 0.8 copy-done
  0.8 0.0 copy-start.1
  0.8 0.8 copy-done.1
  1.7 0.3 shard_map.37.own_ref
  1.9 8.8 %collective-permute-start.1 = (f32[4,2,4,8,128]{4,3,2,1,0:T(8,128)S(1)}, f32[4,2,4,8,128]{4,3,2,1,0:T(8,128)S(1)}, u32[]{:S(2)}, u32[]{:S(2)}) collective-permute-start(f32[4,2,4,8,128]{4,3,2,1,0:T(8,128)S(1)} %shard_map.37.own_ref), channel_id=1, source_target_pairs={{1,0},{2,1},{3,2},{4,3},{5,4},{6,5},{7,6},{8,7},{9,8},{10,9},{11,1... | collective-permute-start | bytes 393224 | tf_op jit(solution)/shard_map/ppermute | solution.py:447
  10.7 1.9 %collective-permute-start = (f32[4,2,4,8,128]{4,3,2,1,0:T(8,128)S(1)}, f32[4,2,4,8,128]{4,3,2,1,0:T(8,128)S(1)}, u32[]{:S(2)}, u32[]{:S(2)}) collective-permute-start(f32[4,2,4,8,128]{4,3,2,1,0:T(8,128)S(1)} %shard_map.37.own_ref), channel_id=1, source_target_pairs={{0,1},{1,2},{2,3},{3,4},{4,5},{5,6},{6,7},{7,8},{8,9},{9,10},{10,1... | collective-permute-start | bytes 393224 | tf_op jit(solution)/shard_map/ppermute | solution.py:447
  12.7 0.0 collective-permute-done.1.high_ref
  12.7 1.9 %collective-permute-done.low_ref = f32[4,2,4,8,128]{4,3,2,1,0:T(8,128)S(1)} collective-permute-done((f32[4,2,4,8,128]{4,3,2,1,0:T(8,128)S(1)}, f32[4,2,4,8,128]{4,3,2,1,0:T(8,128)S(1)}, u32[]{:S(2)}, u32[]{:S(2)}) %collective-permute-start) | collective-permute-done | bytes 131104 | tf_op jit(solution)/shard_map/ppermute | solution.py:447
  14.6 0.1 shard_map.38
  14.7 1.3 %collective-permute-start.4 = (f32[4,2,4,24,128]{4,3,2,1,0:T(8,128)S(1)}, f32[4,2,4,24,128]{4,3,2,1,0:T(8,128)S(1)}, u32[]{:S(2)}, u32[]{:S(2)}) collective-permute-start(f32[4,2,4,24,128]{4,3,2,1,0:T(8,128)S(1)} %get-tuple-element.24.own_ref), channel_id=1, source_target_pairs={{16,0},{32,16},{48,32},{64,48},{80,64},{96,80},{112,96},{128,112},... | collective-permute-start | bytes 1179656 | tf_op jit(solution)/shard_map/ppermute | solution.py:447
  16.0 4.0 %collective-permute-start.3 = (f32[4,2,4,24,128]{4,3,2,1,0:T(8,128)S(1)}, f32[4,2,4,24,128]{4,3,2,1,0:T(8,128)S(1)}, u32[]{:S(2)}, u32[]{:S(2)}) collective-permute-start(f32[4,2,4,24,128]{4,3,2,1,0:T(8,128)S(1)} %get-tuple-element.24.own_ref), channel_id=1, source_target_pairs={{0,16},{16,32},{32,48},{48,64},{64,80},{80,96},{96,112},{112,128},... | collective-permute-start | bytes 1179656 | tf_op jit(solution)/shard_map/ppermute | solution.py:447
  20.0 1.3 %collective-permute-start.2 = (f32[3,2,4,24,128]{4,3,2,1,0:T(8,128)S(1)}, f32[3,2,4,24,128]{4,3,2,1,0:T(8,128)S(1)}, u32[]{:S(2)}, u32[]{:S(2)}) collective-permute-start(f32[3,2,4,24,128]{4,3,2,1,0:T(8,128)S(1)} %get-tuple-element.23), channel_id=1, source_target_pairs={{0,32},{16,48},{32,64},{48,80},{64,96},{80,112},{96,128},{112,144}... | collective-permute-start | bytes 884744 | tf_op jit(solution)/shard_map/ppermute | solution.py:447
  21.3 1.3 %collective-permute-start.5 = (f32[3,2,4,24,128]{4,3,2,1,0:T(8,128)S(1)}, f32[3,2,4,24,128]{4,3,2,1,0:T(8,128)S(1)}, u32[]{:S(2)}, u32[]{:S(2)}) collective-permute-start(f32[3,2,4,24,128]{4,3,2,1,0:T(8,128)S(1)} %get-tuple-element.25), channel_id=1, source_target_pairs={{32,0},{48,16},{64,32},{80,48},{96,64},{112,80},{128,96},{144,112}... | collective-permute-start | bytes 884744 | tf_op jit(solution)/shard_map/ppermute | solution.py:447
  22.6 0.1 pad_add_fusion.spot_ref
  22.7 18.6 %collective-permute-done.2.low2_ref = f32[3,2,4,24,128]{4,3,2,1,0:T(8,128)S(1)} collective-permute-done((f32[3,2,4,24,128]{4,3,2,1,0:T(8,128)S(1)}, f32[3,2,4,24,128]{4,3,2,1,0:T(8,128)S(1)}, u32[]{:S(2)}, u32[]{:S(2)}) %collective-permute-start.2) | collective-permute-done | bytes 294944 | tf_op jit(solution)/shard_map/ppermute | solution.py:447
  41.2 0.0 collective-permute-done.5.high2_ref
  41.2 0.0 collective-permute-done.4.high1_ref
  41.2 0.0 collective-permute-done.3.low1_ref
  41.2 0.0 copy-start.2
  41.3 0.6 copy-done.2
  41.9 7.2 %shard_map.39 = (f32[16,16,128]{2,1,0:T(8,128)S(1)}, f32[2,8,128]{2,1,0:T(8,128)S(1)}, f32[5,4,8,128]{3,2,1,0:T(8,128)S(1)}, f32[4,4,24,128]{3,2,1,0:T(8,128)S(1...) custom-call(s32[4]{0:T(128)S(1)} %pad_add_fusion.spot_ref, ...), custom_call_target="tpu_custom_call" | custom-call | tf_op jit(solution)/shard_map/pallas_call | solution.py:431
  49.1 15.7 %all_to_all.10.got_ref.rows_ref = f32[16,16,128]{2,1,0:T(8,128)S(1)} all-to-all(f32[16,16,128]{2,1,0:T(8,128)S(1)} %get-tuple-element.26), channel_id=1, replica_groups=mesh['gx'=32,'gy'=16] {'gy'}, dimensions={0} | all-to-all | bytes 262144 | tf_op jit(solution)/shard_map/all_to_all | solution.py:495
  64.7 0.7 shard_map.40
  65.4 51.1 %all_to_all.11.planes_ref = f32[32,80,128]{2,1,0:T(8,128)S(1)} all-to-all(f32[32,80,128]{2,1,0:T(8,128)S(1)} %shard_map.40), channel_id=1, replica_groups=mesh['gx'=32,'gy'=16] {'gx'}, dimensions={0} | all-to-all | bytes 2621440 | tf_op jit(solution)/shard_map/all_to_all | solution.py:497
  116.5 6.5 %shard_map.41 = f32[4,8,512]{2,1,0:T(8,128)} custom-call(s32[4]{0:T(128)S(1)} %pad_add_fusion.spot_ref, f32[32,80,128]{2,1,0:T(8,128)S(1)} %all_to_all.11.planes_ref, f32[16,16,128]{2,1,0:T(8,128)S(1)} %all_to_all.10.got_ref.rows_ref, f32[5,4,8,128]{3,2,1,0:T(8,128)S(1)} %get-tuple-element.28.fx, f32[4,4,24,128]{3,2,1,0:T(8,128)S(1)} %get-tuple-element.29.fy, ...), custom_call_target="tpu_custom_call" | custom-call | tf_op jit(solution)/shard_map/pallas_call | solution.py:431
Async XLA Ops:
  0.0 0.8 copy-start
  0.8 0.8 copy-start.1
  1.9 10.7 %collective-permute-start.1 = (f32[4,2,4,8,128]{4,3,2,1,0:T(8,128)S(1)}, f32[4,2,4,8,128]{4,3,2,1,0:T(8,128)S(1)}, u32[]{:S(2)}, u32[]{:S(2)}) collective-permute-start(f32[4,2,4,8,128]{4,3,2,1,0:T(8,128)S(1)} %shard_map.37.own_ref), channel_id=1, source_target_pairs={{1,0},{2,1},{3,2},{4,3},{5,4},{6,5},{7,6},{8,7},{9,8},{10,9},{11,1... | collective-permute-start | bytes 393224 | tf_op jit(solution)/shard_map/ppermute | solution.py:447
  10.7 3.9 %collective-permute-start = (f32[4,2,4,8,128]{4,3,2,1,0:T(8,128)S(1)}, f32[4,2,4,8,128]{4,3,2,1,0:T(8,128)S(1)}, u32[]{:S(2)}, u32[]{:S(2)}) collective-permute-start(f32[4,2,4,8,128]{4,3,2,1,0:T(8,128)S(1)} %shard_map.37.own_ref), channel_id=1, source_target_pairs={{0,1},{1,2},{2,3},{3,4},{4,5},{5,6},{6,7},{7,8},{8,9},{9,10},{10,1... | collective-permute-start | bytes 393224 | tf_op jit(solution)/shard_map/ppermute | solution.py:447
  14.7 26.6 %collective-permute-start.4 = (f32[4,2,4,24,128]{4,3,2,1,0:T(8,128)S(1)}, f32[4,2,4,24,128]{4,3,2,1,0:T(8,128)S(1)}, u32[]{:S(2)}, u32[]{:S(2)}) collective-permute-start(f32[4,2,4,24,128]{4,3,2,1,0:T(8,128)S(1)} %get-tuple-element.24.own_ref), channel_id=1, source_target_pairs={{16,0},{32,16},{48,32},{64,48},{80,64},{96,80},{112,96},{128,112},... | collective-permute-start | bytes 1179656 | tf_op jit(solution)/shard_map/ppermute | solution.py:447
  16.0 25.3 %collective-permute-start.3 = (f32[4,2,4,24,128]{4,3,2,1,0:T(8,128)S(1)}, f32[4,2,4,24,128]{4,3,2,1,0:T(8,128)S(1)}, u32[]{:S(2)}, u32[]{:S(2)}) collective-permute-start(f32[4,2,4,24,128]{4,3,2,1,0:T(8,128)S(1)} %get-tuple-element.24.own_ref), channel_id=1, source_target_pairs={{0,16},{16,32},{32,48},{48,64},{64,80},{80,96},{96,112},{112,128},... | collective-permute-start | bytes 1179656 | tf_op jit(solution)/shard_map/ppermute | solution.py:447
  20.0 21.3 %collective-permute-start.2 = (f32[3,2,4,24,128]{4,3,2,1,0:T(8,128)S(1)}, f32[3,2,4,24,128]{4,3,2,1,0:T(8,128)S(1)}, u32[]{:S(2)}, u32[]{:S(2)}) collective-permute-start(f32[3,2,4,24,128]{4,3,2,1,0:T(8,128)S(1)} %get-tuple-element.23), channel_id=1, source_target_pairs={{0,32},{16,48},{32,64},{48,80},{64,96},{80,112},{96,128},{112,144}... | collective-permute-start | bytes 884744 | tf_op jit(solution)/shard_map/ppermute | solution.py:447
  21.3 19.9 %collective-permute-start.5 = (f32[3,2,4,24,128]{4,3,2,1,0:T(8,128)S(1)}, f32[3,2,4,24,128]{4,3,2,1,0:T(8,128)S(1)}, u32[]{:S(2)}, u32[]{:S(2)}) collective-permute-start(f32[3,2,4,24,128]{4,3,2,1,0:T(8,128)S(1)} %get-tuple-element.25), channel_id=1, source_target_pairs={{32,0},{48,16},{64,32},{80,48},{96,64},{112,80},{128,96},{144,112}... | collective-permute-start | bytes 884744 | tf_op jit(solution)/shard_map/ppermute | solution.py:447
  41.2 0.7 copy-start.2

commit v2 on v1

--- a/solution.py
+++ b/solution.py
@@ -3,6 +3,7 @@
 from jax import lax
 from jax.experimental import pallas as pl
 from jax.experimental.pallas import tpu as pltpu
+from jax.sharding import Mesh
 from jax.sharding import PartitionSpec as P
 
 F32 = jnp.float32
@@ -31,7 +32,17 @@
     return pltpu.roll(value, shift % value.shape[-2], value.ndim - 2)
 
 
-def split_kernel(labels_ref, source_ref, out_ref):
+def split_kernel(table_hbm, labels_hbm, source_hbm, out_ref, pairs_ref, table_ref, labels_ref, source_ref, done):
+    copies = [
+        pltpu.make_async_copy(src, dst, done.at[k])
+        for k, (src, dst) in enumerate(
+            ((table_hbm, table_ref), (labels_hbm, labels_ref), (source_hbm, source_ref)))
+    ]
+    for copy in copies:
+        copy.start()
+    for copy in copies:
+        copy.wait()
+    pairs_ref[...] = pair_table(table_ref)
     lane = iota((8, LANES), 1)
     for plane in range(4):
         labels = labels_ref[plane]
@@ -55,10 +66,14 @@
                     rows = pl.ds(8 * part, 8)
                     value = ref[plane, which, residue]
                     all_ref[plane, which, residue, rows] = value
-                    if plane > 0:
-                        up_ref[plane - 1, which, residue, rows] = value
-                    if plane < 3:
-                        down_ref[plane, which, residue, rows] = value
+                    near = {0: (slice(4, 8), 0), 1: (slice(0, 8), 4), 2: (slice(0, 4), 12)}[part]
+                    size = near[0].stop - near[0].start
+                    if plane > which:
+                        at = plane - 1 if which == 0 else plane + 1
+                        up_ref[at, residue, pl.ds(near[1], size)] = value[near[0]]
+                    if plane < 3 - which:
+                        at = plane if which == 0 else plane + 3
+                        down_ref[at, residue, pl.ds(near[1], size)] = value[near[0]]
 
 
 def fine_sum(fx_up, fx_low, fy, fz, v_up, v_low, v):
@@ -107,7 +122,7 @@
 
 
 def up_kernel(
-    spot_ref, table_ref, low2_ref, low1_ref, own_ref, high1_ref, high2_ref,
+    spot_ref, pairs_ref, low2_ref, low1_ref, own_ref, high1_ref, high2_ref,
     chunk_ref, ends_ref, fx_out, fy_out, fz_out, w_out, s_out, v_out,
     fxm_out, fym_out, fzm_out, wm_out, sm_out, vm_out, root_out,
     code, source, fx, fy, fz, zlow, diag, weight, first, second,
@@ -117,13 +132,24 @@
     y0 = 8 * spot_ref[1]
     nx = 4 * spot_ref[2]
     ny = 8 * spot_ref[3]
-    table = pair_table(table_ref)
-    at = 0
-    for ref in (low2_ref, low1_ref, own_ref, high1_ref, high2_ref):
-        for plane in range(ref.shape[0]):
+    table = pairs_ref[...]
+    at = 3
+    for ref in (low1_ref, own_ref, high1_ref):
+        for plane in range(4):
             code[at] = ref[plane, 0].astype(jnp.int32)
             source[at] = ref[plane, 1]
             at += 1
+    blank = jnp.zeros((4, 4, LANES), F32)
+
+    def far(value):
+        return jnp.concatenate([blank, value, blank], axis=1)
+
+    for k in range(3):
+        code[k] = far(low2_ref[k]).astype(jnp.int32)
+        code[PLANES - 3 + k] = far(high2_ref[k]).astype(jnp.int32)
+    for k in range(2):
+        source[1 + k] = far(low2_ref[3 + k])
+        source[PLANES - 3 + k] = far(high2_ref[3 + k])
 
     row = iota((ROWS, LANES), 0)
     lane = iota((ROWS, LANES), 1)
@@ -149,7 +175,7 @@
         zlow[p] = jnp.where(lane == 0, look(here[0]), lane_roll(fz_here[3], 1))
         return carry
 
-    lax.fori_loop(0, PLANES - 1, faces, 0)
+    lax.fori_loop(0, PLANES - 1, faces, 0, unroll=True)
 
     def start(p, carry):
         fy_here = fy[p]
@@ -162,7 +188,7 @@
         first[p] = w * source[p]
         return carry
 
-    lax.fori_loop(1, PLANES - 1, start, 0)
+    lax.fori_loop(1, PLANES - 1, start, 0, unroll=True)
 
     def sweep(p, carry):
         v = first[p]
@@ -170,7 +196,7 @@
         second[p] = KEEP * v + weight[p] * (source[p] + image)
         return carry
 
-    lax.fori_loop(2, PLANES - 2, sweep, 0)
+    lax.fori_loop(2, PLANES - 2, sweep, 0, unroll=True)
 
     def halves(value):
         return jnp.stack([value[0] + value[1], value[2] + value[3]])
@@ -184,7 +210,7 @@
         fxm[k] = both_rows(halves(fx[2 + 2 * k]), 1)
         return carry
 
-    lax.fori_loop(0, 7, coarse_face, 0)
+    lax.fori_loop(0, 7, coarse_face, 0, unroll=True)
 
     def middle(k, carry):
         pa = 1 + 2 * k
@@ -206,7 +232,7 @@
         firstm[k] = w * sm
         return carry
 
-    lax.fori_loop(1, 7, middle, 0)
+    lax.fori_loop(1, 7, middle, 0, unroll=True)
 
     def middle_sweep(k, carry):
         v = firstm[k]
@@ -214,7 +240,7 @@
         secondm[k] = KEEP * v + weightm[k] * (sourcem[k] + image)
         return carry
 
-    lax.fori_loop(2, 6, middle_sweep, 0)
+    lax.fori_loop(2, 6, middle_sweep, 0, unroll=True)
 
     coarse_source = jnp.zeros((ROWS, LANES), F32)
     for k in (3, 4):
@@ -294,83 +320,75 @@
     body = chunk[...]
     low = ends_ref[0]
     high = ends_ref[1]
-    for peer in range(out_ref.shape[0]):
+    place = spot_ref[4]
+    size = out_ref.shape[0]
+    for peer in range(size):
         out_ref[peer, pl.ds(0, 72)] = body
-        above = (spot_ref[0] < peer).astype(F32)
-        out_ref[peer, pl.ds(72, 8)] = low * above + high * (1.0 - above)
+        ahead = (lax.rem(peer - place + size, size) == 1).astype(F32)
+        out_ref[peer, pl.ds(72, 8)] = low * ahead + high * (1.0 - ahead)
 
 
 def down_kernel(
-    spot_ref, planes_ref, rows_ref, fx, fy, fz, w, s, v2,
+    spot_ref, low2_ref, low1_ref, mid_ref, high1_ref, high2_ref, rows_ref, fx, fy, fz, w, s, v2,
     fxm, fym, fzm, wm, sm, vm, root,
     out_ref,
-    parts, state, field, third, total,
+    parts, state, ends, field, third, total,
 ):
-    mine_x = spot_ref[0]
     mine_y = spot_ref[1]
-    count_x = planes_ref.shape[0]
+    place = spot_ref[4]
     count_y = rows_ref.shape[0]
     width = 2 * WINDOW + 1
     lane = iota((ROWS, LANES), 1)
     row = iota((ROWS, LANES), 0)
 
-    def load(step, carry):
-        plane = mine_x + (step - WINDOW)
-        inside = jnp.where((plane >= 0) & (plane < count_x), 1.0, 0.0).astype(F32)
-        spot = jnp.clip(plane, 0, count_x - 1)
-        for which in range(4):
-            value = planes_ref[spot, pl.ds(18 * which, ROWS)] if which < 3 else jnp.concatenate(
-                [planes_ref[spot, pl.ds(54, 18)], jnp.zeros((ROWS - 18, LANES), F32)], axis=0)
-            value = jnp.where(row < 18, value * inside, 0.0)
-            parts[which, step] = value
-            if which == 0:
-                state[0, step] = value
-        return carry
-
-    lax.fori_loop(0, width, load, 0)
+    at = 0
+    for ref in (low2_ref, low1_ref, mid_ref, high1_ref, high2_ref):
+        for plane in range(ref.shape[0]):
+            for which in range(4):
+                value = jnp.where(row < 18, ref[plane, pl.ds(18 * which, ROWS)], 0.0)
+                parts[which, at] = value
+                if which == 0:
+                    state[0, at] = value
+            ends[at] = ref[plane, pl.ds(72, 8)]
+            at += 1
 
     for turn in range(1, WINDOW):
         old = (turn - 1) % 2
         new = turn % 2
-
-        def sweep(step, carry):
-            v = state[old, step]
-            cy = parts[2, step]
-            cz = parts[3, step]
-            value = KEEP * v + parts[0, step]
-            value = value + parts[1, step] * state[old, step + 1] + parts[1, step - 1] * state[old, step - 1]
+        for step in range(turn, width - turn):
+            here = place + step
+            v = state[old, here]
+            cy = parts[2, here]
+            cz = parts[3, here]
+            value = KEEP * v + parts[0, here]
+            value = value + parts[1, here] * state[old, here + 1] + parts[1, here - 1] * state[old, here - 1]
             value = value + cy * row_roll(v, -1) + row_roll(cy * v, 1)
             value = value + cz * lane_roll(v, -1) + lane_roll(cz * v, 1)
-            state[new, step] = value
-            return carry
-
-        lax.fori_loop(turn, width - turn, sweep, 0)
+            state[new, here] = value
 
     last = (WINDOW - 1) % 2
     spread = []
     for big in range(3):
-        value = state[last, WINDOW - 1 + big]
+        value = state[last, place + WINDOW - 1 + big]
         picked = jnp.zeros((ROWS, LANES), F32)
         for k in range(4):
             line = jnp.broadcast_to(value[7 + k : 8 + k], (ROWS, LANES))
             picked = jnp.where((row >= 4 + 4 * k) & (row < 8 + 4 * k), line, picked)
         spread.append(picked * root[big])
 
-    def line_block(ref, spot, inside, base):
+    def line_block(at):
         halves = []
         for half in range(2):
             rows = []
             for m in range(4):
-                line = ref[spot, pl.ds(base + 4 * half + m, 1)] * inside
+                line = ends[at, pl.ds(4 * half + m, 1)]
                 rows += [line, line]
             pad = jnp.zeros((8, LANES), F32)
             halves.append(jnp.concatenate([pad] + [jnp.concatenate(rows, axis=0)] + [pad], axis=0))
         return jnp.stack(halves)
 
-    below = jnp.where(mine_x > 0, 1.0, 0.0).astype(F32)
-    above = jnp.where(mine_x < count_x - 1, 1.0, 0.0).astype(F32)
-    field[0] = line_block(planes_ref, jnp.maximum(mine_x - 1, 0), below, 72) + spread[0]
-    field[5] = line_block(planes_ref, jnp.minimum(mine_x + 1, count_x - 1), above, 72) + spread[2]
+    field[0] = line_block(place + WINDOW - 1) + spread[0]
+    field[5] = line_block(place + WINDOW + 1) + spread[2]
     field[1] = vm[0] + spread[0]
     field[4] = vm[3] + spread[2]
     left = jnp.where(mine_y > 0, 1.0, 0.0).astype(F32)
@@ -424,7 +442,10 @@
 
 VMEM = pl.BlockSpec(memory_space=pltpu.VMEM)
 SMEM = pl.BlockSpec(memory_space=pltpu.SMEM)
+HBM = pl.BlockSpec(memory_space=pltpu.HBM)
 PARAMS = pltpu.CompilerParams(vmem_limit_bytes=48 * 1024 * 1024)
+GX = ("ya", "xa")
+GY = ("za", "ca")
 
 
 def call(kernel, specs, outs, scratch, *args):
@@ -448,23 +469,11 @@
 
 
 def shards(right_side, labels, conduct_table):
-    nx = lax.axis_size("gx")
-    ny = lax.axis_size("gy")
-    spot = jnp.stack([lax.axis_index("gx"), lax.axis_index("gy"), jnp.int32(nx), jnp.int32(ny)]).astype(jnp.int32)
-    (own,) = call(split_kernel, [VMEM] * 2, [(4, 2, 4, 8, LANES)], [], labels, right_side)
-    low = shifted(own, "gy", 1)
-    high = shifted(own, "gy", -1)
-    wide, up, down = call(
-        join_kernel,
-        [VMEM] * 3,
-        [(4, 2, 4, ROWS, LANES), (3, 2, 4, ROWS, LANES), (3, 2, 4, ROWS, LANES)],
-        [],
-        low, own, high,
-    )
-    low1 = shifted(wide, "gx", 1)
-    high1 = shifted(wide, "gx", -1)
-    low2 = shifted(up, "gx", 2)
-    high2 = shifted(down, "gx", -2)
+    nx = lax.axis_size(GX)
+    ny = lax.axis_size(GY)
+    block = lax.axis_size("xa")
+    numbers = [lax.axis_index(GX), lax.axis_index(GY), jnp.int32(nx), jnp.int32(ny), lax.axis_index("xa")]
+    spot = jnp.stack(numbers).astype(jnp.int32)
 
     fine = (4, ROWS, LANES)
     mid = (2, ROWS, LANES)
@@ -473,9 +482,27 @@
     def room(*shape):
         return pltpu.VMEM(shape, F32)
 
+    own, pairs = call(
+        split_kernel, [HBM] * 3, [(4, 2, 4, 8, LANES), (8, LANES)],
+        [
+            pltpu.SMEM(conduct_table.shape, F32), pltpu.VMEM(labels.shape, jnp.int32), room(*right_side.shape),
+            pltpu.SemaphoreType.DMA((3,)),
+        ],
+        conduct_table, labels, right_side,
+    )
+    low = shifted(own, GY, 1)
+    high = shifted(own, GY, -1)
+    wide, up, down = call(
+        join_kernel, [VMEM] * 3, [(4, 2) + fine, (5, 4, 16, LANES), (5, 4, 16, LANES)], [], low, own, high
+    )
+    low1 = shifted(wide, GX, 1)
+    high1 = shifted(wide, GX, -1)
+    low2 = shifted(up, GX, 2)
+    high2 = shifted(down, GX, -2)
+
     outs = call(
         up_kernel,
-        [SMEM, SMEM] + [VMEM] * 5,
+        [SMEM] + [VMEM] * 6,
         [
             (ny, 16, LANES), (2, 8, LANES),
             (5,) + tile, (4,) + fine, (4,) + tile, (4,) + tile, (4,) + tile, (6,) + fine,
@@ -489,24 +516,27 @@
         + [room(8, *mid)] * 3
         + [room(8, ROWS, LANES)]
         + [room(8, *mid)] * 5,
-        spot, conduct_table, low2, low1, wide, high1, high2,
+        spot, pairs, low2, low1, wide, high1, high2,
     )
     chunk, ends = outs[:2]
-    rows = lax.all_to_all(chunk, "gy", 0, 0, tiled=True)
-    (planes,) = call(window_kernel, [SMEM, VMEM, VMEM], [(nx, 80, LANES)], [room(72, LANES)], spot, rows, ends)
-    planes = lax.all_to_all(planes, "gx", 0, 0, tiled=True)
-    width = 2 * WINDOW + 1
+    rows = lax.all_to_all(chunk, GY, 0, 0, tiled=True)
+    (planes,) = call(window_kernel, [SMEM, VMEM, VMEM], [(block, 80, LANES)], [room(72, LANES)], spot, rows, ends)
+    planes = lax.all_to_all(planes, "xa", 0, 0, tiled=True)
+    blocks = [shifted(planes, "ya", 2), shifted(planes, "ya", 1), planes, shifted(planes, "ya", -1), shifted(planes, "ya", -2)]
     (correction,) = call(
         down_kernel,
-        [SMEM] + [VMEM] * 15,
+        [SMEM] + [VMEM] * 19,
         [(4, 8, 4 * LANES)],
-        [room(4, width, ROWS, LANES), room(2, width, ROWS, LANES), room(6, *mid), room(4, *mid), room(6, *fine)],
-        spot, planes, rows, *outs[2:],
+        [
+            room(4, 5 * block, ROWS, LANES), room(2, 5 * block, ROWS, LANES), room(5 * block, 8, LANES),
+            room(6, *mid), room(4, *mid), room(6, *fine),
+        ],
+        spot, *blocks, rows, *outs[2:],
     )
     return correction
 
 
 def solution(mesh):
-    in_specs = (P("gx", "gy", None), P("gx", "gy", None), P())
-    out_specs = P("gx", "gy", None)
-    return jax.shard_map(shards, mesh=mesh, in_specs=in_specs, out_specs=out_specs, check_vma=False)
+    mesh = Mesh(mesh.devices.reshape(-1, 4, mesh.devices.shape[1] // 2, 2), GX + GY)
+    spec = P(GX, GY, None)
+    return jax.shard_map(shards, mesh=mesh, in_specs=(spec, spec, P()), out_specs=spec, check_vma=False)

time: 123 us -> 95.8 us (0.78)
  the two profiles are of different devices: /device:TPU:1 before, /device:TPU:48 now
where the time goes in v2:
time: 95.8 us; the launch traced here: 95.3 us
  blocking collectives  32 us (33%)
  starting transfers between devices  31.8 us (33%)
  waiting for transfers between devices  20.8 us (22%)
  Pallas kernels  8.09 us (8%)
  local copies, waits for them, and re-layouts  2.42 us (3%)
    ppermute x10, starting transfers between devices, shifted(): return lax.ppermute(value, axis, pairs)  31.8 us
    all_to_all x1, blocking collectives, shards(): rows = lax.all_to_all(chunk, GY, 0, 0, tiled=True)  22.8 us
    ppermute x10, waiting for transfers between devices, shifted(): return lax.ppermute(value, axis, pairs)  20.8 us
    all_to_all x1, blocking collectives, shards(): planes = lax.all_to_all(planes, 'xa', 0, 0, tiled=True)  9.25 us
    pallas_call x5, Pallas kernels, call(): pl.pallas_call(kernel, in_specs=specs, out_specs=[VMEM] * len(outs), out_...  8.09 us
    unnamed x6, local copies, waits for them, and re-layouts  2.33 us
  transfers between devices with their start and end apart: 10, of which 6 were waited for; matrix products, arithmetic and copies ran while one was open for 0% of the time, Pallas kernels for 0%

profile of v2, /device:TPU:48, one launch (start us, length us, event | category | flops | bytes accessed | tf_op | source)
XLA Modules:
  0.0 95.3 jit_solution(17115994273089882017)
XLA Ops:
  0.0 0.0 copy-start
  0.0 0.8 copy-done
  0.8 0.0 copy-start.1
  0.8 0.8 copy-done.1
  1.7 0.0 copy-start.2
  1.7 0.7 copy-done.2
  2.3 0.8 shard_map.37
  3.2 1.3 %collective-permute-start.1 = (f32[4,2,4,8,128]{4,3,2,1,0:T(8,128)S(1)}, f32[4,2,4,8,128]{4,3,2,1,0:T(8,128)S(1)}, u32[]{:S(2)}, u32[]{:S(2)}) collective-permute-start(f32[4,2,4,8,128]{4,3,2,1,0:T(8,128)S(1)} %get-tuple-element.26.own_ref), channel_id=1, source_target_pairs={{1,0},{2,1},{3,2},{4,3},{5,4},{6,5},{7,6},{8,7},{9,8},{10,9},{11,1... | collective-permute-start | bytes 393224 | tf_op jit(solution)/shard_map/ppermute | solution.py:468
  4.5 3.0 %collective-permute-start = (f32[4,2,4,8,128]{4,3,2,1,0:T(8,128)S(1)}, f32[4,2,4,8,128]{4,3,2,1,0:T(8,128)S(1)}, u32[]{:S(2)}, u32[]{:S(2)}) collective-permute-start(f32[4,2,4,8,128]{4,3,2,1,0:T(8,128)S(1)} %get-tuple-element.26.own_ref), channel_id=1, source_target_pairs={{0,1},{1,2},{2,3},{3,4},{4,5},{5,6},{6,7},{7,8},{8,9},{9,10},{10,1... | collective-permute-start | bytes 393224 | tf_op jit(solution)/shard_map/ppermute | solution.py:468
  7.5 0.0 collective-permute-done.1.high_ref
  7.5 1.0 collective-permute-done.low_ref
  8.5 0.1 shard_map.38
  8.5 5.5 %collective-permute-start.4 = (f32[4,2,4,24,128]{4,3,2,1,0:T(8,128)S(1)}, f32[4,2,4,24,128]{4,3,2,1,0:T(8,128)S(1)}, u32[]{:S(2)}, u32[]{:S(2)}) collective-permute-start(f32[4,2,4,24,128]{4,3,2,1,0:T(8,128)S(1)} %get-tuple-element.28.own_ref), channel_id=1, source_target_pairs={{16,0},{32,16},{48,32},{64,48},{80,64},{96,80},{112,96},{128,112},... | collective-permute-start | bytes 1179656 | tf_op jit(solution)/shard_map/ppermute | solution.py:468
  14.0 1.9 %collective-permute-start.3 = (f32[4,2,4,24,128]{4,3,2,1,0:T(8,128)S(1)}, f32[4,2,4,24,128]{4,3,2,1,0:T(8,128)S(1)}, u32[]{:S(2)}, u32[]{:S(2)}) collective-permute-start(f32[4,2,4,24,128]{4,3,2,1,0:T(8,128)S(1)} %get-tuple-element.28.own_ref), channel_id=1, source_target_pairs={{0,16},{16,32},{32,48},{48,64},{64,80},{80,96},{96,112},{112,128},... | collective-permute-start | bytes 1179656 | tf_op jit(solution)/shard_map/ppermute | solution.py:468
  15.9 3.4 %collective-permute-start.2 = (f32[5,4,16,128]{3,2,1,0:T(8,128)S(1)}, f32[5,4,16,128]{3,2,1,0:T(8,128)S(1)}, u32[]{:S(2)}, u32[]{:S(2)}) collective-permute-start(f32[5,4,16,128]{3,2,1,0:T(8,128)S(1)} %get-tuple-element.27), channel_id=1, source_target_pairs={{0,32},{16,48},{32,64},{48,80},{64,96},{80,112},{96,128},{112,144}... | collective-permute-start | bytes 491528 | tf_op jit(solution)/shard_map/ppermute | solution.py:468
  19.3 4.8 %collective-permute-start.5 = (f32[5,4,16,128]{3,2,1,0:T(8,128)S(1)}, f32[5,4,16,128]{3,2,1,0:T(8,128)S(1)}, u32[]{:S(2)}, u32[]{:S(2)}) collective-permute-start(f32[5,4,16,128]{3,2,1,0:T(8,128)S(1)} %get-tuple-element.29), channel_id=1, source_target_pairs={{32,0},{48,16},{64,32},{80,48},{96,64},{112,80},{128,96},{144,112}... | collective-permute-start | bytes 491528 | tf_op jit(solution)/shard_map/ppermute | solution.py:468
  24.2 0.1 stack.15.spot_ref
  24.3 6.1 %collective-permute-done.2.low2_ref = f32[5,4,16,128]{3,2,1,0:T(8,128)S(1)} collective-permute-done((f32[5,4,16,128]{3,2,1,0:T(8,128)S(1)}, f32[5,4,16,128]{3,2,1,0:T(8,128)S(1)}, u32[]{:S(2)}, u32[]{:S(2)}) %collective-permute-start.2) | collective-permute-done | bytes 163872 | tf_op jit(solution)/shard_map/ppermute | solution.py:468
  30.4 3.6 %collective-permute-done.5.high2_ref = f32[5,4,16,128]{3,2,1,0:T(8,128)S(1)} collective-permute-done((f32[5,4,16,128]{3,2,1,0:T(8,128)S(1)}, f32[5,4,16,128]{3,2,1,0:T(8,128)S(1)}, u32[]{:S(2)}, u32[]{:S(2)}) %collective-permute-start.5) | collective-permute-done | bytes 163872 | tf_op jit(solution)/shard_map/ppermute | solution.py:468
  34.0 0.0 collective-permute-done.4.high1_ref
  34.0 0.0 collective-permute-done.3.low1_ref
  34.0 4.4 %shard_map.39 = (f32[16,16,128]{2,1,0:T(8,128)S(1)}, f32[2,8,128]{2,1,0:T(8,128)S(1)}, f32[5,4,8,128]{3,2,1,0:T(8,128)S(1)}, f32[4,4,24,128]{3,2,1,0:T(8,128)S(1...) custom-call(s32[5]{0:T(128)S(1)} %stack.15.spot_ref, ...), custom_call_target="tpu_custom_call" | custom-call | tf_op jit(solution)/shard_map/pallas_call | solution.py:452
  38.4 22.8 %all_to_all.10.got_ref.rows_ref = f32[16,16,128]{2,1,0:T(8,128)S(1)} all-to-all(f32[16,16,128]{2,1,0:T(8,128)S(1)} %get-tuple-element.30), channel_id=1, replica_groups=mesh['ya'=8,'xa'=4,'za'=8,'ca'=2] {'za','ca'}, dimensions={0} | all-to-all | bytes 262144 | tf_op jit(solution)/shard_map/all_to_all | solution.py:522
  61.2 0.6 shard_map.40
  61.8 9.3 %all_to_all.11.mid_ref = f32[4,80,128]{2,1,0:T(8,128)S(1)} all-to-all(f32[4,80,128]{2,1,0:T(8,128)S(1)} %shard_map.40), channel_id=1, replica_groups=mesh['ya'=8,'xa'=4,'za'=8,'ca'=2] {'xa'}, dimensions={0} | all-to-all | bytes 327680 | tf_op jit(solution)/shard_map/all_to_all | solution.py:524
  71.0 4.7 %collective-permute-start.9 = (f32[4,80,128]{2,1,0:T(8,128)S(1)}, f32[4,80,128]{2,1,0:T(8,128)S(1)}, u32[]{:S(2)}, u32[]{:S(2)}) collective-permute-start(f32[4,80,128]{2,1,0:T(8,128)S(1)} %all_to_all.11.mid_ref), channel_id=1, source_target_pairs={{128,0},{192,64},{256,128},{320,192},{384,256},{448,320},{129,1},{... | collective-permute-start | bytes 491528 | tf_op jit(solution)/shard_map/ppermute | solution.py:468
  75.8 1.9 %collective-permute-start.8 = (f32[4,80,128]{2,1,0:T(8,128)S(1)}, f32[4,80,128]{2,1,0:T(8,128)S(1)}, u32[]{:S(2)}, u32[]{:S(2)}) collective-permute-start(f32[4,80,128]{2,1,0:T(8,128)S(1)} %all_to_all.11.mid_ref), channel_id=1, source_target_pairs={{64,0},{128,64},{192,128},{256,192},{320,256},{384,320},{448,384},... | collective-permute-start | bytes 491528 | tf_op jit(solution)/shard_map/ppermute | solution.py:468
  77.7 3.9 %collective-permute-start.7 = (f32[4,80,128]{2,1,0:T(8,128)S(1)}, f32[4,80,128]{2,1,0:T(8,128)S(1)}, u32[]{:S(2)}, u32[]{:S(2)}) collective-permute-start(f32[4,80,128]{2,1,0:T(8,128)S(1)} %all_to_all.11.mid_ref), channel_id=1, source_target_pairs={{0,64},{64,128},{128,192},{192,256},{256,320},{320,384},{384,448},... | collective-permute-start | bytes 491528 | tf_op jit(solution)/shard_map/ppermute | solution.py:468
  81.6 1.3 %collective-permute-start.6 = (f32[4,80,128]{2,1,0:T(8,128)S(1)}, f32[4,80,128]{2,1,0:T(8,128)S(1)}, u32[]{:S(2)}, u32[]{:S(2)}) collective-permute-start(f32[4,80,128]{2,1,0:T(8,128)S(1)} %all_to_all.11.mid_ref), channel_id=1, source_target_pairs={{0,128},{64,192},{128,256},{192,320},{256,384},{320,448},{1,129},{... | collective-permute-start | bytes 491528 | tf_op jit(solution)/shard_map/ppermute | solution.py:468
  82.9 0.0 collective-permute-done.9.high2_ref
  82.9 2.8 %collective-permute-done.8.high1_ref = f32[4,80,128]{2,1,0:T(8,128)S(1)} collective-permute-done((f32[4,80,128]{2,1,0:T(8,128)S(1)}, f32[4,80,128]{2,1,0:T(8,128)S(1)}, u32[]{:S(2)}, u32[]{:S(2)}) %collective-permute-start.8) | collective-permute-done | bytes 163872 | tf_op jit(solution)/shard_map/ppermute | solution.py:468
  85.7 2.3 %collective-permute-done.7.low1_ref = f32[4,80,128]{2,1,0:T(8,128)S(1)} collective-permute-done((f32[4,80,128]{2,1,0:T(8,128)S(1)}, f32[4,80,128]{2,1,0:T(8,128)S(1)}, u32[]{:S(2)}, u32[]{:S(2)}) %collective-permute-start.7) | collective-permute-done | bytes 163872 | tf_op jit(solution)/shard_map/ppermute | solution.py:468
  88.0 5.1 %collective-permute-done.6.low2_ref = f32[4,80,128]{2,1,0:T(8,128)S(1)} collective-permute-done((f32[4,80,128]{2,1,0:T(8,128)S(1)}, f32[4,80,128]{2,1,0:T(8,128)S(1)}, u32[]{:S(2)}, u32[]{:S(2)}) %collective-permute-start.6) | collective-permute-done | bytes 163872 | tf_op jit(solution)/shard_map/ppermute | solution.py:468
  93.1 2.2 %shard_map.41 = f32[4,8,512]{2,1,0:T(8,128)} custom-call(s32[5]{0:T(128)S(1)} %stack.15.spot_ref, f32[4,80,128]{2,1,0:T(8,128)S(1)} %collective-permute-done.6.low2_ref, f32[4,80,128]{2,1,0:T(8,128)S(1)} %collective-permute-done.7.low1_ref, f32[4,80,128]{2,1,0:T(8,128)S(1)} %all_to_all.11.mid_ref, f32[4,80,128]{2,1,0:T(8,128)S(1)} %collective-permute-done.8.high1_ref, ...), custom_call_target="tpu_custom_call" | custom-call | tf_op jit(solution)/shard_map/pallas_call | solution.py:452
Async XLA Ops:
  0.0 0.8 copy-start
  0.8 0.8 copy-start.1
  1.7 0.7 copy-start.2
  3.2 4.3 %collective-permute-start.1 = (f32[4,2,4,8,128]{4,3,2,1,0:T(8,128)S(1)}, f32[4,2,4,8,128]{4,3,2,1,0:T(8,128)S(1)}, u32[]{:S(2)}, u32[]{:S(2)}) collective-permute-start(f32[4,2,4,8,128]{4,3,2,1,0:T(8,128)S(1)} %get-tuple-element.26.own_ref), channel_id=1, source_target_pairs={{1,0},{2,1},{3,2},{4,3},{5,4},{6,5},{7,6},{8,7},{9,8},{10,9},{11,1... | collective-permute-start | bytes 393224 | tf_op jit(solution)/shard_map/ppermute | solution.py:468
  4.5 4.0 %collective-permute-start = (f32[4,2,4,8,128]{4,3,2,1,0:T(8,128)S(1)}, f32[4,2,4,8,128]{4,3,2,1,0:T(8,128)S(1)}, u32[]{:S(2)}, u32[]{:S(2)}) collective-permute-start(f32[4,2,4,8,128]{4,3,2,1,0:T(8,128)S(1)} %get-tuple-element.26.own_ref), channel_id=1, source_target_pairs={{0,1},{1,2},{2,3},{3,4},{4,5},{5,6},{6,7},{7,8},{8,9},{9,10},{10,1... | collective-permute-start | bytes 393224 | tf_op jit(solution)/shard_map/ppermute | solution.py:468
  8.5 25.5 %collective-permute-start.4 = (f32[4,2,4,24,128]{4,3,2,1,0:T(8,128)S(1)}, f32[4,2,4,24,128]{4,3,2,1,0:T(8,128)S(1)}, u32[]{:S(2)}, u32[]{:S(2)}) collective-permute-start(f32[4,2,4,24,128]{4,3,2,1,0:T(8,128)S(1)} %get-tuple-element.28.own_ref), channel_id=1, source_target_pairs={{16,0},{32,16},{48,32},{64,48},{80,64},{96,80},{112,96},{128,112},... | collective-permute-start | bytes 1179656 | tf_op jit(solution)/shard_map/ppermute | solution.py:468
  14.0 20.0 %collective-permute-start.3 = (f32[4,2,4,24,128]{4,3,2,1,0:T(8,128)S(1)}, f32[4,2,4,24,128]{4,3,2,1,0:T(8,128)S(1)}, u32[]{:S(2)}, u32[]{:S(2)}) collective-permute-start(f32[4,2,4,24,128]{4,3,2,1,0:T(8,128)S(1)} %get-tuple-element.28.own_ref), channel_id=1, source_target_pairs={{0,16},{16,32},{32,48},{48,64},{64,80},{80,96},{96,112},{112,128},... | collective-permute-start | bytes 1179656 | tf_op jit(solution)/shard_map/ppermute | solution.py:468
  15.9 14.5 %collective-permute-start.2 = (f32[5,4,16,128]{3,2,1,0:T(8,128)S(1)}, f32[5,4,16,128]{3,2,1,0:T(8,128)S(1)}, u32[]{:S(2)}, u32[]{:S(2)}) collective-permute-start(f32[5,4,16,128]{3,2,1,0:T(8,128)S(1)} %get-tuple-element.27), channel_id=1, source_target_pairs={{0,32},{16,48},{32,64},{48,80},{64,96},{80,112},{96,128},{112,144}... | collective-permute-start | bytes 491528 | tf_op jit(solution)/shard_map/ppermute | solution.py:468
  19.3 14.7 %collective-permute-start.5 = (f32[5,4,16,128]{3,2,1,0:T(8,128)S(1)}, f32[5,4,16,128]{3,2,1,0:T(8,128)S(1)}, u32[]{:S(2)}, u32[]{:S(2)}) collective-permute-start(f32[5,4,16,128]{3,2,1,0:T(8,128)S(1)} %get-tuple-element.29), channel_id=1, source_target_pairs={{32,0},{48,16},{64,32},{80,48},{96,64},{112,80},{128,96},{144,112}... | collective-permute-start | bytes 491528 | tf_op jit(solution)/shard_map/ppermute | solution.py:468
  71.0 11.9 %collective-permute-start.9 = (f32[4,80,128]{2,1,0:T(8,128)S(1)}, f32[4,80,128]{2,1,0:T(8,128)S(1)}, u32[]{:S(2)}, u32[]{:S(2)}) collective-permute-start(f32[4,80,128]{2,1,0:T(8,128)S(1)} %all_to_all.11.mid_ref), channel_id=1, source_target_pairs={{128,0},{192,64},{256,128},{320,192},{384,256},{448,320},{129,1},{... | collective-permute-start | bytes 491528 | tf_op jit(solution)/shard_map/ppermute | solution.py:468
  75.8 10.0 %collective-permute-start.8 = (f32[4,80,128]{2,1,0:T(8,128)S(1)}, f32[4,80,128]{2,1,0:T(8,128)S(1)}, u32[]{:S(2)}, u32[]{:S(2)}) collective-permute-start(f32[4,80,128]{2,1,0:T(8,128)S(1)} %all_to_all.11.mid_ref), channel_id=1, source_target_pairs={{64,0},{128,64},{192,128},{256,192},{320,256},{384,320},{448,384},... | collective-permute-start | bytes 491528 | tf_op jit(solution)/shard_map/ppermute | solution.py:468
  77.7 10.3 %collective-permute-start.7 = (f32[4,80,128]{2,1,0:T(8,128)S(1)}, f32[4,80,128]{2,1,0:T(8,128)S(1)}, u32[]{:S(2)}, u32[]{:S(2)}) collective-permute-start(f32[4,80,128]{2,1,0:T(8,128)S(1)} %all_to_all.11.mid_ref), channel_id=1, source_target_pairs={{0,64},{64,128},{128,192},{192,256},{256,320},{320,384},{384,448},... | collective-permute-start | bytes 491528 | tf_op jit(solution)/shard_map/ppermute | solution.py:468
  81.6 11.5 %collective-permute-start.6 = (f32[4,80,128]{2,1,0:T(8,128)S(1)}, f32[4,80,128]{2,1,0:T(8,128)S(1)}, u32[]{:S(2)}, u32[]{:S(2)}) collective-permute-start(f32[4,80,128]{2,1,0:T(8,128)S(1)} %all_to_all.11.mid_ref), channel_id=1, source_target_pairs={{0,128},{64,192},{128,256},{192,320},{256,384},{320,448},{1,129},{... | collective-permute-start | bytes 491528 | tf_op jit(solution)/shard_map/ppermute | solution.py:468

commit v3 on v2

--- a/solution.py
+++ b/solution.py
@@ -58,22 +58,34 @@
                 out_ref[plane, which, residue] = jnp.where(lane < 64, low, high)
 
 
-def join_kernel(low_ref, own_ref, high_ref, all_ref, up_ref, down_ref):
+def layout(first, last):
+    spots = []
+    offset = 0
+    for which in range(2):
+        for distance in range(first, last + 1 - which * (last == REACH)):
+            reach = REACH - which - distance
+            spots.append((which, distance, 8 - reach, 8 + 2 * reach, offset))
+            offset += 8 + 2 * reach
+    return spots, offset
+
+
+NEAR, NEAR_ROWS = layout(1, 4)
+FAR, FAR_ROWS = layout(5, REACH)
+
+
+def join_kernel(low_ref, own_ref, high_ref, all_ref, up1_ref, down1_ref, up2_ref, down2_ref):
     for plane in range(4):
         for which in range(2):
             for residue in range(4):
                 for part, ref in enumerate((low_ref, own_ref, high_ref)):
-                    rows = pl.ds(8 * part, 8)
-                    value = ref[plane, which, residue]
-                    all_ref[plane, which, residue, rows] = value
-                    near = {0: (slice(4, 8), 0), 1: (slice(0, 8), 4), 2: (slice(0, 4), 12)}[part]
-                    size = near[0].stop - near[0].start
-                    if plane > which:
-                        at = plane - 1 if which == 0 else plane + 1
-                        up_ref[at, residue, pl.ds(near[1], size)] = value[near[0]]
-                    if plane < 3 - which:
-                        at = plane if which == 0 else plane + 3
-                        down_ref[at, residue, pl.ds(near[1], size)] = value[near[0]]
+                    all_ref[plane, which, residue, pl.ds(8 * part, 8)] = ref[plane, which, residue]
+    for spots, start, up_ref, down_ref in ((NEAR, 1, up1_ref, down1_ref), (FAR, 5, up2_ref, down2_ref)):
+        for which, distance, row, rows, offset in spots:
+            ahead = distance - start
+            for residue in range(4):
+                out = pl.ds(offset, rows)
+                down_ref[residue, out] = all_ref[ahead, which, residue, pl.ds(row, rows)]
+                up_ref[residue, out] = all_ref[3 - ahead, which, residue, pl.ds(row, rows)]
 
 
 def fine_sum(fx_up, fx_low, fy, fz, v_up, v_low, v):
@@ -133,23 +145,23 @@
     nx = 4 * spot_ref[2]
     ny = 8 * spot_ref[3]
     table = pairs_ref[...]
-    at = 3
-    for ref in (low1_ref, own_ref, high1_ref):
-        for plane in range(4):
-            code[at] = ref[plane, 0].astype(jnp.int32)
-            source[at] = ref[plane, 1]
-            at += 1
-    blank = jnp.zeros((4, 4, LANES), F32)
-
-    def far(value):
-        return jnp.concatenate([blank, value, blank], axis=1)
-
-    for k in range(3):
-        code[k] = far(low2_ref[k]).astype(jnp.int32)
-        code[PLANES - 3 + k] = far(high2_ref[k]).astype(jnp.int32)
-    for k in range(2):
-        source[1 + k] = far(low2_ref[3 + k])
-        source[PLANES - 3 + k] = far(high2_ref[3 + k])
+    blank = jnp.zeros((4, ROWS, LANES), F32)
+    for k in range(4):
+        code[REACH + k] = own_ref[k, 0].astype(jnp.int32)
+        source[REACH + k] = own_ref[k, 1]
+    for distance in range(1, REACH + 1):
+        for p in (REACH - distance, REACH + 3 + distance):
+            code[p] = blank.astype(jnp.int32)
+            source[p] = blank
+    for spots, low_ref, high_ref in ((NEAR, low1_ref, high1_ref), (FAR, low2_ref, high2_ref)):
+        for which, distance, row, rows, offset in spots:
+            for p, ref in ((REACH - distance, low_ref), (REACH + 3 + distance, high_ref)):
+                for residue in range(4):
+                    value = ref[residue, pl.ds(offset, rows)]
+                    if which == 0:
+                        code[p, residue, pl.ds(row, rows)] = value.astype(jnp.int32)
+                    else:
+                        source[p, residue, pl.ds(row, rows)] = value
 
     row = iota((ROWS, LANES), 0)
     lane = iota((ROWS, LANES), 1)
@@ -285,9 +297,12 @@
     chunk = jnp.concatenate(lines, axis=0)
     for peer in range(chunk_ref.shape[0]):
         chunk_ref[peer] = chunk
-    for k in (3, 4):
-        mids = [secondm[k, half, 8 + 2 * m : 9 + 2 * m] for half in range(2) for m in range(4)]
-        ends_ref[k - 3] = jnp.concatenate(mids, axis=0)
+    for k, other in ((3, 4), (4, 3)):
+        lines = [secondm[k, half, 8 + 2 * m : 9 + 2 * m] for half in range(2) for m in range(4)]
+        lines += [secondm[other, half, at_row : at_row + 1] for at_row in (6, 16) for half in range(2)]
+        lines += [root[at_row : at_row + 1] for at_row in (4, 16)]
+        lines += [jnp.zeros((2, LANES), F32)]
+        ends_ref[k - 3] = jnp.concatenate(lines, axis=0)
 
     own_rows = pl.ds(8, 8)
     for k in range(5):
@@ -325,7 +340,7 @@
     for peer in range(size):
         out_ref[peer, pl.ds(0, 72)] = body
         ahead = (lax.rem(peer - place + size, size) == 1).astype(F32)
-        out_ref[peer, pl.ds(72, 8)] = low * ahead + high * (1.0 - ahead)
+        out_ref[peer, pl.ds(72, 16)] = low * ahead + high * (1.0 - ahead)
 
 
 def down_kernel(
@@ -349,7 +364,7 @@
                 parts[which, at] = value
                 if which == 0:
                     state[0, at] = value
-            ends[at] = ref[plane, pl.ds(72, 8)]
+            ends[at] = ref[plane, pl.ds(72, 16)]
             at += 1
 
     for turn in range(1, WINDOW):
@@ -366,6 +381,16 @@
             value = value + cz * lane_roll(v, -1) + lane_roll(cz * v, 1)
             state[new, here] = value
 
+    def swap_rows(value, line, first, stop):
+        return jnp.where((row >= first) & (row < stop), jnp.broadcast_to(line, (ROWS, LANES)), value)
+
+    def corners(value, at):
+        halves = []
+        for half in range(2):
+            part = swap_rows(value[half], ends[at, pl.ds(8 + half, 1)], 6, 8)
+            halves.append(swap_rows(part, ends[at, pl.ds(10 + half, 1)], 16, 18))
+        return jnp.stack(halves)
+
     last = (WINDOW - 1) % 2
     spread = []
     for big in range(3):
@@ -374,7 +399,12 @@
         for k in range(4):
             line = jnp.broadcast_to(value[7 + k : 8 + k], (ROWS, LANES))
             picked = jnp.where((row >= 4 + 4 * k) & (row < 8 + 4 * k), line, picked)
-        spread.append(picked * root[big])
+        scale = root[big]
+        if big != 1:
+            beside = place + WINDOW - 1 + big
+            scale = swap_rows(scale, ends[beside, pl.ds(12, 1)], 4, 8)
+            scale = swap_rows(scale, ends[beside, pl.ds(13, 1)], 16, 20)
+        spread.append(picked * scale)
 
     def line_block(at):
         halves = []
@@ -389,8 +419,8 @@
 
     field[0] = line_block(place + WINDOW - 1) + spread[0]
     field[5] = line_block(place + WINDOW + 1) + spread[2]
-    field[1] = vm[0] + spread[0]
-    field[4] = vm[3] + spread[2]
+    field[1] = corners(vm[0], place + WINDOW - 1) + spread[0]
+    field[4] = corners(vm[3], place + WINDOW + 1) + spread[2]
     left = jnp.where(mine_y > 0, 1.0, 0.0).astype(F32)
     right = jnp.where(mine_y < count_y - 1, 1.0, 0.0).astype(F32)
     left_spot = jnp.maximum(mine_y - 1, 0)
@@ -401,9 +431,7 @@
             value = vm[1 + k, half]
             lower = rows_ref[left_spot, pl.ds(12 + 2 * k + half, 1)] * left
             upper = rows_ref[right_spot, pl.ds(8 + 2 * k + half, 1)] * right
-            value = jnp.where((row >= 4) & (row < 6), jnp.broadcast_to(lower, (ROWS, LANES)), value)
-            value = jnp.where((row >= 18) & (row < 20), jnp.broadcast_to(upper, (ROWS, LANES)), value)
-            halves.append(value)
+            halves.append(swap_rows(swap_rows(value, lower, 4, 6), upper, 18, 20))
         field[2 + k] = jnp.stack(halves) + spread[1]
 
     for k in range(4):
@@ -488,23 +516,25 @@
             pltpu.SMEM(conduct_table.shape, F32), pltpu.VMEM(labels.shape, jnp.int32), room(*right_side.shape),
             pltpu.SemaphoreType.DMA((3,)),
         ],
-        conduct_table, labels, right_side,
+        *(pltpu.with_memory_space_constraint(value, pltpu.HBM) for value in (conduct_table, labels, right_side)),
     )
     low = shifted(own, GY, 1)
     high = shifted(own, GY, -1)
-    wide, up, down = call(
-        join_kernel, [VMEM] * 3, [(4, 2) + fine, (5, 4, 16, LANES), (5, 4, 16, LANES)], [], low, own, high
+    near = (4, NEAR_ROWS, LANES)
+    far = (4, FAR_ROWS, LANES)
+    wide, up1, down1, up2, down2 = call(
+        join_kernel, [VMEM] * 3, [(4, 2) + fine, near, near, far, far], [], low, own, high
     )
-    low1 = shifted(wide, GX, 1)
-    high1 = shifted(wide, GX, -1)
-    low2 = shifted(up, GX, 2)
-    high2 = shifted(down, GX, -2)
+    low1 = shifted(up1, GX, 1)
+    high1 = shifted(down1, GX, -1)
+    low2 = shifted(up2, GX, 2)
+    high2 = shifted(down2, GX, -2)
 
     outs = call(
         up_kernel,
         [SMEM] + [VMEM] * 6,
         [
-            (ny, 16, LANES), (2, 8, LANES),
+            (ny, 16, LANES), (2, 16, LANES),
             (5,) + tile, (4,) + fine, (4,) + tile, (4,) + tile, (4,) + tile, (6,) + fine,
             (5,) + mid, (4,) + mid, (4,) + mid, (4,) + mid, (4,) + mid, (4,) + mid,
             (3, ROWS, LANES),
@@ -520,7 +550,7 @@
     )
     chunk, ends = outs[:2]
     rows = lax.all_to_all(chunk, GY, 0, 0, tiled=True)
-    (planes,) = call(window_kernel, [SMEM, VMEM, VMEM], [(block, 80, LANES)], [room(72, LANES)], spot, rows, ends)
+    (planes,) = call(window_kernel, [SMEM, VMEM, VMEM], [(block, 88, LANES)], [room(72, LANES)], spot, rows, ends)
     planes = lax.all_to_all(planes, "xa", 0, 0, tiled=True)
     blocks = [shifted(planes, "ya", 2), shifted(planes, "ya", 1), planes, shifted(planes, "ya", -1), shifted(planes, "ya", -2)]
     (correction,) = call(
@@ -528,7 +558,7 @@
         [SMEM] + [VMEM] * 19,
         [(4, 8, 4 * LANES)],
         [
-            room(4, 5 * block, ROWS, LANES), room(2, 5 * block, ROWS, LANES), room(5 * block, 8, LANES),
+            room(4, 5 * block, ROWS, LANES), room(2, 5 * block, ROWS, LANES), room(5 * block, 16, LANES),
             room(6, *mid), room(4, *mid), room(6, *fine),
         ],
         spot, *blocks, rows, *outs[2:],

time: 95.8 us -> 94.6 us (0.987)
  the two profiles are of different devices: /device:TPU:48 before, /device:TPU:56 now
where the time goes in v3:
time: 94.6 us; the launch traced here: 94.2 us
  starting transfers between devices  32.5 us (34%)
  blocking collectives  31.5 us (33%)
  waiting for transfers between devices  21.5 us (23%)
  Pallas kernels  8.48 us (9%)
    ppermute x10, starting transfers between devices, shifted(): return lax.ppermute(value, axis, pairs)  32.5 us
    all_to_all x1, blocking collectives, shards(): rows = lax.all_to_all(chunk, GY, 0, 0, tiled=True)  22.1 us
    ppermute x10, waiting for transfers between devices, shifted(): return lax.ppermute(value, axis, pairs)  21.5 us
    all_to_all x1, blocking collectives, shards(): planes = lax.all_to_all(planes, 'xa', 0, 0, tiled=True)  9.43 us
    pallas_call x5, Pallas kernels, call(): pl.pallas_call(kernel, in_specs=specs, out_specs=[VMEM] * len(outs), out_...  8.48 us
  transfers between devices with their start and end apart: 10, of which 6 were waited for; matrix products, arithmetic and copies ran while one was open for 0% of the time, Pallas kernels for 0%

profile of v3, /device:TPU:56, one launch (start us, length us, event | category | flops | bytes accessed | tf_op | source)
XLA Modules:
  0.0 94.2 jit_solution(3845050753128326706)
XLA Ops:
  0.0 1.2 %shard_map.37 = (f32[4,2,4,8,128]{4,3,2,1,0:T(8,128)S(1)}, f32[8,128]{1,0:T(8,128)S(1)}) custom-call(f32[3]{0:T(128)} %table_hbm.1, s32[4,8,512]{2,1,0:T(8,128)} %labels_hbm.1, f32[4,8,512]{2,1,0:T(8,128)} %source_hbm.1), custom_call_target="tpu_custom_call" | custom-call | tf_op jit(solution)/shard_map/pallas_call | solution.py:480
  1.2 1.3 %collective-permute-start.1 = (f32[4,2,4,8,128]{4,3,2,1,0:T(8,128)S(1)}, f32[4,2,4,8,128]{4,3,2,1,0:T(8,128)S(1)}, u32[]{:S(2)}, u32[]{:S(2)}) collective-permute-start(f32[4,2,4,8,128]{4,3,2,1,0:T(8,128)S(1)} %get-tuple-element.28.own_ref), channel_id=1, source_target_pairs={{1,0},{2,1},{3,2},{4,3},{5,4},{6,5},{7,6},{8,7},{9,8},{10,9},{11,1... | collective-permute-start | bytes 393224 | tf_op jit(solution)/shard_map/ppermute | solution.py:496
  2.5 3.0 %collective-permute-start = (f32[4,2,4,8,128]{4,3,2,1,0:T(8,128)S(1)}, f32[4,2,4,8,128]{4,3,2,1,0:T(8,128)S(1)}, u32[]{:S(2)}, u32[]{:S(2)}) collective-permute-start(f32[4,2,4,8,128]{4,3,2,1,0:T(8,128)S(1)} %get-tuple-element.28.own_ref), channel_id=1, source_target_pairs={{0,1},{1,2},{2,3},{3,4},{4,5},{5,6},{6,7},{7,8},{8,9},{9,10},{10,1... | collective-permute-start | bytes 393224 | tf_op jit(solution)/shard_map/ppermute | solution.py:496
  5.5 0.0 collective-permute-done.1.high_ref
  5.5 1.0 %collective-permute-done.low_ref = f32[4,2,4,8,128]{4,3,2,1,0:T(8,128)S(1)} collective-permute-done((f32[4,2,4,8,128]{4,3,2,1,0:T(8,128)S(1)}, f32[4,2,4,8,128]{4,3,2,1,0:T(8,128)S(1)}, u32[]{:S(2)}, u32[]{:S(2)}) %collective-permute-start) | collective-permute-done | bytes 131104 | tf_op jit(solution)/shard_map/ppermute | solution.py:496
  6.5 0.1 shard_map.38
  6.6 3.4 %collective-permute-start.3 = (f32[4,128,128]{2,1,0:T(8,128)S(1)}, f32[4,128,128]{2,1,0:T(8,128)S(1)}, u32[]{:S(2)}, u32[]{:S(2)}) collective-permute-start(f32[4,128,128]{2,1,0:T(8,128)S(1)} %get-tuple-element.30), channel_id=1, source_target_pairs={{0,16},{16,32},{32,48},{48,64},{64,80},{80,96},{96,112},{112,128},... | collective-permute-start | bytes 786440 | tf_op jit(solution)/shard_map/ppermute | solution.py:496
  10.0 4.6 %collective-permute-start.4 = (f32[4,128,128]{2,1,0:T(8,128)S(1)}, f32[4,128,128]{2,1,0:T(8,128)S(1)}, u32[]{:S(2)}, u32[]{:S(2)}) collective-permute-start(f32[4,128,128]{2,1,0:T(8,128)S(1)} %get-tuple-element.32), channel_id=1, source_target_pairs={{16,0},{32,16},{48,32},{64,48},{80,64},{96,80},{112,96},{128,112},... | collective-permute-start | bytes 786440 | tf_op jit(solution)/shard_map/ppermute | solution.py:496
  14.5 2.8 %collective-permute-start.2 = (f32[4,48,128]{2,1,0:T(8,128)S(1)}, f32[4,48,128]{2,1,0:T(8,128)S(1)}, u32[]{:S(2)}, u32[]{:S(2)}) collective-permute-start(f32[4,48,128]{2,1,0:T(8,128)S(1)} %get-tuple-element.29), channel_id=1, source_target_pairs={{0,32},{16,48},{32,64},{48,80},{64,96},{80,112},{96,128},{112,144}... | collective-permute-start | bytes 294920 | tf_op jit(solution)/shard_map/ppermute | solution.py:496
  17.4 5.4 %collective-permute-start.5 = (f32[4,48,128]{2,1,0:T(8,128)S(1)}, f32[4,48,128]{2,1,0:T(8,128)S(1)}, u32[]{:S(2)}, u32[]{:S(2)}) collective-permute-start(f32[4,48,128]{2,1,0:T(8,128)S(1)} %get-tuple-element.33), channel_id=1, source_target_pairs={{32,0},{48,16},{64,32},{80,48},{96,64},{112,80},{128,96},{144,112}... | collective-permute-start | bytes 294920 | tf_op jit(solution)/shard_map/ppermute | solution.py:496
  22.8 0.1 stack.15.spot_ref
  22.9 0.6 collective-permute-done.2.low2_ref
  23.5 2.9 %collective-permute-done.5.high2_ref = f32[4,48,128]{2,1,0:T(8,128)S(1)} collective-permute-done((f32[4,48,128]{2,1,0:T(8,128)S(1)}, f32[4,48,128]{2,1,0:T(8,128)S(1)}, u32[]{:S(2)}, u32[]{:S(2)}) %collective-permute-start.5) | collective-permute-done | bytes 98336 | tf_op jit(solution)/shard_map/ppermute | solution.py:496
  26.4 0.0 collective-permute-done.3.low1_ref
  26.4 0.0 collective-permute-done.4.high1_ref
  26.4 4.4 %shard_map.39 = (f32[16,16,128]{2,1,0:T(8,128)S(1)}, f32[2,16,128]{2,1,0:T(8,128)S(1)}, f32[5,4,8,128]{3,2,1,0:T(8,128)S(1)}, f32[4,4,24,128]{3,2,1,0:T(8,128)S(...) custom-call(s32[5]{0:T(128)S(1)} %stack.15.spot_ref, ...), custom_call_target="tpu_custom_call" | custom-call | tf_op jit(solution)/shard_map/pallas_call | solution.py:480
  30.8 22.1 %all_to_all.10.got_ref.rows_ref = f32[16,16,128]{2,1,0:T(8,128)S(1)} all-to-all(f32[16,16,128]{2,1,0:T(8,128)S(1)} %get-tuple-element.34), channel_id=1, replica_groups=mesh['ya'=8,'xa'=4,'za'=8,'ca'=2] {'za','ca'}, dimensions={0} | all-to-all | bytes 262144 | tf_op jit(solution)/shard_map/all_to_all | solution.py:552
  52.9 0.6 shard_map.40
  53.5 9.4 %all_to_all.11.mid_ref = f32[4,88,128]{2,1,0:T(8,128)S(1)} all-to-all(f32[4,88,128]{2,1,0:T(8,128)S(1)} %shard_map.40), channel_id=1, replica_groups=mesh['ya'=8,'xa'=4,'za'=8,'ca'=2] {'xa'}, dimensions={0} | all-to-all | bytes 360448 | tf_op jit(solution)/shard_map/all_to_all | solution.py:554
  62.9 6.1 %collective-permute-start.9 = (f32[4,88,128]{2,1,0:T(8,128)S(1)}, f32[4,88,128]{2,1,0:T(8,128)S(1)}, u32[]{:S(2)}, u32[]{:S(2)}) collective-permute-start(f32[4,88,128]{2,1,0:T(8,128)S(1)} %all_to_all.11.mid_ref), channel_id=1, source_target_pairs={{128,0},{192,64},{256,128},{320,192},{384,256},{448,320},{129,1},{... | collective-permute-start | bytes 540680 | tf_op jit(solution)/shard_map/ppermute | solution.py:496
  69.0 3.3 %collective-permute-start.8 = (f32[4,88,128]{2,1,0:T(8,128)S(1)}, f32[4,88,128]{2,1,0:T(8,128)S(1)}, u32[]{:S(2)}, u32[]{:S(2)}) collective-permute-start(f32[4,88,128]{2,1,0:T(8,128)S(1)} %all_to_all.11.mid_ref), channel_id=1, source_target_pairs={{64,0},{128,64},{192,128},{256,192},{320,256},{384,320},{448,384},... | collective-permute-start | bytes 540680 | tf_op jit(solution)/shard_map/ppermute | solution.py:496
  72.3 1.3 %collective-permute-start.7 = (f32[4,88,128]{2,1,0:T(8,128)S(1)}, f32[4,88,128]{2,1,0:T(8,128)S(1)}, u32[]{:S(2)}, u32[]{:S(2)}) collective-permute-start(f32[4,88,128]{2,1,0:T(8,128)S(1)} %all_to_all.11.mid_ref), channel_id=1, source_target_pairs={{0,64},{64,128},{128,192},{192,256},{256,320},{320,384},{384,448},... | collective-permute-start | bytes 540680 | tf_op jit(solution)/shard_map/ppermute | solution.py:496
  73.6 1.3 %collective-permute-start.6 = (f32[4,88,128]{2,1,0:T(8,128)S(1)}, f32[4,88,128]{2,1,0:T(8,128)S(1)}, u32[]{:S(2)}, u32[]{:S(2)}) collective-permute-start(f32[4,88,128]{2,1,0:T(8,128)S(1)} %all_to_all.11.mid_ref), channel_id=1, source_target_pairs={{0,128},{64,192},{128,256},{192,320},{256,384},{320,448},{1,129},{... | collective-permute-start | bytes 540680 | tf_op jit(solution)/shard_map/ppermute | solution.py:496
  74.9 0.0 collective-permute-done.9.high2_ref
  74.9 1.8 %collective-permute-done.8.high1_ref = f32[4,88,128]{2,1,0:T(8,128)S(1)} collective-permute-done((f32[4,88,128]{2,1,0:T(8,128)S(1)}, f32[4,88,128]{2,1,0:T(8,128)S(1)}, u32[]{:S(2)}, u32[]{:S(2)}) %collective-permute-start.8) | collective-permute-done | bytes 180256 | tf_op jit(solution)/shard_map/ppermute | solution.py:496
  76.6 6.9 %collective-permute-done.7.low1_ref = f32[4,88,128]{2,1,0:T(8,128)S(1)} collective-permute-done((f32[4,88,128]{2,1,0:T(8,128)S(1)}, f32[4,88,128]{2,1,0:T(8,128)S(1)}, u32[]{:S(2)}, u32[]{:S(2)}) %collective-permute-start.7) | collective-permute-done | bytes 180256 | tf_op jit(solution)/shard_map/ppermute | solution.py:496
  83.6 8.4 %collective-permute-done.6.low2_ref = f32[4,88,128]{2,1,0:T(8,128)S(1)} collective-permute-done((f32[4,88,128]{2,1,0:T(8,128)S(1)}, f32[4,88,128]{2,1,0:T(8,128)S(1)}, u32[]{:S(2)}, u32[]{:S(2)}) %collective-permute-start.6) | collective-permute-done | bytes 180256 | tf_op jit(solution)/shard_map/ppermute | solution.py:496
  92.0 2.2 %shard_map.41 = f32[4,8,512]{2,1,0:T(8,128)} custom-call(s32[5]{0:T(128)S(1)} %stack.15.spot_ref, f32[4,88,128]{2,1,0:T(8,128)S(1)} %collective-permute-done.6.low2_ref, f32[4,88,128]{2,1,0:T(8,128)S(1)} %collective-permute-done.7.low1_ref, f32[4,88,128]{2,1,0:T(8,128)S(1)} %all_to_all.11.mid_ref, f32[4,88,128]{2,1,0:T(8,128)S(1)} %collective-permute-done.8.high1_ref, ...), custom_call_target="tpu_custom_call" | custom-call | tf_op jit(solution)/shard_map/pallas_call | solution.py:480
Async XLA Ops:
  1.2 4.3 %collective-permute-start.1 = (f32[4,2,4,8,128]{4,3,2,1,0:T(8,128)S(1)}, f32[4,2,4,8,128]{4,3,2,1,0:T(8,128)S(1)}, u32[]{:S(2)}, u32[]{:S(2)}) collective-permute-start(f32[4,2,4,8,128]{4,3,2,1,0:T(8,128)S(1)} %get-tuple-element.28.own_ref), channel_id=1, source_target_pairs={{1,0},{2,1},{3,2},{4,3},{5,4},{6,5},{7,6},{8,7},{9,8},{10,9},{11,1... | collective-permute-start | bytes 393224 | tf_op jit(solution)/shard_map/ppermute | solution.py:496
  2.5 4.0 %collective-permute-start = (f32[4,2,4,8,128]{4,3,2,1,0:T(8,128)S(1)}, f32[4,2,4,8,128]{4,3,2,1,0:T(8,128)S(1)}, u32[]{:S(2)}, u32[]{:S(2)}) collective-permute-start(f32[4,2,4,8,128]{4,3,2,1,0:T(8,128)S(1)} %get-tuple-element.28.own_ref), channel_id=1, source_target_pairs={{0,1},{1,2},{2,3},{3,4},{4,5},{5,6},{6,7},{7,8},{8,9},{9,10},{10,1... | collective-permute-start | bytes 393224 | tf_op jit(solution)/shard_map/ppermute | solution.py:496
  6.6 19.8 %collective-permute-start.3 = (f32[4,128,128]{2,1,0:T(8,128)S(1)}, f32[4,128,128]{2,1,0:T(8,128)S(1)}, u32[]{:S(2)}, u32[]{:S(2)}) collective-permute-start(f32[4,128,128]{2,1,0:T(8,128)S(1)} %get-tuple-element.30), channel_id=1, source_target_pairs={{0,16},{16,32},{32,48},{48,64},{64,80},{80,96},{96,112},{112,128},... | collective-permute-start | bytes 786440 | tf_op jit(solution)/shard_map/ppermute | solution.py:496
  10.0 16.4 %collective-permute-start.4 = (f32[4,128,128]{2,1,0:T(8,128)S(1)}, f32[4,128,128]{2,1,0:T(8,128)S(1)}, u32[]{:S(2)}, u32[]{:S(2)}) collective-permute-start(f32[4,128,128]{2,1,0:T(8,128)S(1)} %get-tuple-element.32), channel_id=1, source_target_pairs={{16,0},{32,16},{48,32},{64,48},{80,64},{96,80},{112,96},{128,112},... | collective-permute-start | bytes 786440 | tf_op jit(solution)/shard_map/ppermute | solution.py:496
  14.5 8.9 %collective-permute-start.2 = (f32[4,48,128]{2,1,0:T(8,128)S(1)}, f32[4,48,128]{2,1,0:T(8,128)S(1)}, u32[]{:S(2)}, u32[]{:S(2)}) collective-permute-start(f32[4,48,128]{2,1,0:T(8,128)S(1)} %get-tuple-element.29), channel_id=1, source_target_pairs={{0,32},{16,48},{32,64},{48,80},{64,96},{80,112},{96,128},{112,144}... | collective-permute-start | bytes 294920 | tf_op jit(solution)/shard_map/ppermute | solution.py:496
  17.4 9.0 %collective-permute-start.5 = (f32[4,48,128]{2,1,0:T(8,128)S(1)}, f32[4,48,128]{2,1,0:T(8,128)S(1)}, u32[]{:S(2)}, u32[]{:S(2)}) collective-permute-start(f32[4,48,128]{2,1,0:T(8,128)S(1)} %get-tuple-element.33), channel_id=1, source_target_pairs={{32,0},{48,16},{64,32},{80,48},{96,64},{112,80},{128,96},{144,112}... | collective-permute-start | bytes 294920 | tf_op jit(solution)/shard_map/ppermute | solution.py:496
  62.9 12.0 %collective-permute-start.9 = (f32[4,88,128]{2,1,0:T(8,128)S(1)}, f32[4,88,128]{2,1,0:T(8,128)S(1)}, u32[]{:S(2)}, u32[]{:S(2)}) collective-permute-start(f32[4,88,128]{2,1,0:T(8,128)S(1)} %all_to_all.11.mid_ref), channel_id=1, source_target_pairs={{128,0},{192,64},{256,128},{320,192},{384,256},{448,320},{129,1},{... | collective-permute-start | bytes 540680 | tf_op jit(solution)/shard_map/ppermute | solution.py:496
  69.0 7.6 %collective-permute-start.8 = (f32[4,88,128]{2,1,0:T(8,128)S(1)}, f32[4,88,128]{2,1,0:T(8,128)S(1)}, u32[]{:S(2)}, u32[]{:S(2)}) collective-permute-start(f32[4,88,128]{2,1,0:T(8,128)S(1)} %all_to_all.11.mid_ref), channel_id=1, source_target_pairs={{64,0},{128,64},{192,128},{256,192},{320,256},{384,320},{448,384},... | collective-permute-start | bytes 540680 | tf_op jit(solution)/shard_map/ppermute | solution.py:496
  72.3 11.3 %collective-permute-start.7 = (f32[4,88,128]{2,1,0:T(8,128)S(1)}, f32[4,88,128]{2,1,0:T(8,128)S(1)}, u32[]{:S(2)}, u32[]{:S(2)}) collective-permute-start(f32[4,88,128]{2,1,0:T(8,128)S(1)} %all_to_all.11.mid_ref), channel_id=1, source_target_pairs={{0,64},{64,128},{128,192},{192,256},{256,320},{320,384},{384,448},... | collective-permute-start | bytes 540680 | tf_op jit(solution)/shard_map/ppermute | solution.py:496
  73.6 18.4 %collective-permute-start.6 = (f32[4,88,128]{2,1,0:T(8,128)S(1)}, f32[4,88,128]{2,1,0:T(8,128)S(1)}, u32[]{:S(2)}, u32[]{:S(2)}) collective-permute-start(f32[4,88,128]{2,1,0:T(8,128)S(1)} %all_to_all.11.mid_ref), channel_id=1, source_target_pairs={{0,128},{64,192},{128,256},{192,320},{256,384},{320,448},{1,129},{... | collective-permute-start | bytes 540680 | tf_op jit(solution)/shard_map/ppermute | solution.py:496

commit v4 on v3

--- a/solution.py
+++ b/solution.py
@@ -12,6 +12,7 @@
 REACH = 7
 PLANES = 4 + 2 * REACH
 WINDOW = 8
+SPAN = 20
 KEEP = 0.2
 OMEGA = 0.8
 
@@ -323,28 +324,31 @@
         v_out[k] = second[REACH - 1 + k]
 
 
-def window_kernel(spot_ref, got_ref, ends_ref, out_ref, chunk):
-    mine = spot_ref[1]
+def window_kernel(spot_ref, got_ref, ends_ref, other_ref, out_ref, chunk):
+    place = spot_ref[4]
+    core = spot_ref[5]
+    base = spot_ref[1] - core
     count = got_ref.shape[0]
-    for step in range(9):
-        block = mine + (step - 4)
+    for step in range(SPAN // 2):
+        block = base + (step - 4)
         inside = jnp.where((block >= 0) & (block < count), 1.0, 0.0).astype(F32)
         value = got_ref[jnp.clip(block, 0, count - 1), pl.ds(0, 8)] * inside
         for which in range(4):
-            chunk[pl.ds(18 * which + 2 * step, 2)] = value[2 * which : 2 * which + 2]
+            chunk[pl.ds(SPAN * which + 2 * step, 2)] = value[2 * which : 2 * which + 2]
     body = chunk[...]
-    low = ends_ref[0]
-    high = ends_ref[1]
-    place = spot_ref[4]
     size = out_ref.shape[0]
+    first = (core == 0).astype(F32)
     for peer in range(size):
-        out_ref[peer, pl.ds(0, 72)] = body
+        out_ref[peer, pl.ds(0, 4 * SPAN)] = body
         ahead = (lax.rem(peer - place + size, size) == 1).astype(F32)
-        out_ref[peer, pl.ds(72, 16)] = low * ahead + high * (1.0 - ahead)
+        mine = ends_ref[0] * ahead + ends_ref[1] * (1.0 - ahead)
+        other = other_ref[0] * ahead + other_ref[1] * (1.0 - ahead)
+        out_ref[peer, pl.ds(4 * SPAN, 16)] = mine * first + other * (1.0 - first)
+        out_ref[peer, pl.ds(4 * SPAN + 16, 16)] = other * first + mine * (1.0 - first)
 
 
 def down_kernel(
-    spot_ref, low2_ref, low1_ref, mid_ref, high1_ref, high2_ref, rows_ref, fx, fy, fz, w, s, v2,
+    spot_ref, took1_ref, took2_ref, mid_ref, gave1_ref, gave2_ref, rows_ref, fx, fy, fz, w, s, v2,
     fxm, fym, fzm, wm, sm, vm, root,
     out_ref,
     parts, state, ends, field, third, total,
@@ -356,16 +360,27 @@
     lane = iota((ROWS, LANES), 1)
     row = iota((ROWS, LANES), 0)
 
-    at = 0
-    for ref in (low2_ref, low1_ref, mid_ref, high1_ref, high2_ref):
-        for plane in range(ref.shape[0]):
+    lower_core = spot_ref[5] == 0
+    block = mid_ref.shape[0]
+    sources = (
+        (took2_ref, gave2_ref), (took1_ref, gave1_ref), (mid_ref, None), (gave1_ref, took1_ref), (gave2_ref, took2_ref)
+    )
+    for number, (one, two) in enumerate(sources):
+        for plane in range(block):
+            at = number * block + plane
+
+            def read(first, rows):
+                value = one[plane, pl.ds(first, rows)]
+                if two is not None:
+                    value = jnp.where(lower_core, value, two[plane, pl.ds(first, rows)])
+                return value
+
             for which in range(4):
-                value = jnp.where(row < 18, ref[plane, pl.ds(18 * which, ROWS)], 0.0)
+                value = jnp.where(row < SPAN, read(SPAN * which, ROWS), 0.0)
                 parts[which, at] = value
                 if which == 0:
                     state[0, at] = value
-            ends[at] = ref[plane, pl.ds(72, 16)]
-            at += 1
+            ends[at] = jnp.where(lower_core, read(4 * SPAN, 16), read(4 * SPAN + 16, 16))
 
     for turn in range(1, WINDOW):
         old = (turn - 1) % 2
@@ -397,7 +412,8 @@
         value = state[last, place + WINDOW - 1 + big]
         picked = jnp.zeros((ROWS, LANES), F32)
         for k in range(4):
-            line = jnp.broadcast_to(value[7 + k : 8 + k], (ROWS, LANES))
+            line = jnp.where(lower_core, value[7 + k : 8 + k], value[9 + k : 10 + k])
+            line = jnp.broadcast_to(line, (ROWS, LANES))
             picked = jnp.where((row >= 4 + 4 * k) & (row < 8 + 4 * k), line, picked)
         scale = root[big]
         if big != 1:
@@ -496,11 +512,23 @@
     return lax.ppermute(value, axis, pairs)
 
 
+def parted(value, step):
+    pairs = []
+    for i in range(lax.axis_size("ya") - step):
+        pairs.append((2 * i, 2 * (i + step)))
+        pairs.append((2 * (i + step) + 1, 2 * i + 1))
+    return lax.ppermute(value, ("ya", "ca"), pairs)
+
+
+def swapped(value):
+    return lax.ppermute(value, "ca", [(0, 1), (1, 0)])
+
+
 def shards(right_side, labels, conduct_table):
     nx = lax.axis_size(GX)
     ny = lax.axis_size(GY)
     block = lax.axis_size("xa")
-    numbers = [lax.axis_index(GX), lax.axis_index(GY), jnp.int32(nx), jnp.int32(ny), lax.axis_index("xa")]
+    numbers = [lax.axis_index(GX), lax.axis_index(GY), jnp.int32(nx), jnp.int32(ny), lax.axis_index("xa"), lax.axis_index("ca")]
     spot = jnp.stack(numbers).astype(jnp.int32)
 
     fine = (4, ROWS, LANES)
@@ -550,9 +578,15 @@
     )
     chunk, ends = outs[:2]
     rows = lax.all_to_all(chunk, GY, 0, 0, tiled=True)
-    (planes,) = call(window_kernel, [SMEM, VMEM, VMEM], [(block, 88, LANES)], [room(72, LANES)], spot, rows, ends)
+    other = swapped(ends)
+    window = (block, 4 * SPAN + 32, LANES)
+    (planes,) = call(
+        window_kernel, [SMEM] + [VMEM] * 3, [window], [room(4 * SPAN, LANES)], spot, rows, ends, other
+    )
     planes = lax.all_to_all(planes, "xa", 0, 0, tiled=True)
-    blocks = [shifted(planes, "ya", 2), shifted(planes, "ya", 1), planes, shifted(planes, "ya", -1), shifted(planes, "ya", -2)]
+    took1 = parted(planes, 1)
+    took2 = parted(planes, 2)
+    blocks = [took1, took2, planes, swapped(took1), swapped(took2)]
     (correction,) = call(
         down_kernel,
         [SMEM] + [VMEM] * 19,

time: 94.6 us -> 89.7 us (0.948)
  the two profiles are of different devices: /device:TPU:56 before, /device:TPU:1 now
where the time goes in v4:
time: 89.7 us; the launch traced here: 89.1 us
  starting transfers between devices  47.1 us (53%)
  waiting for transfers between devices  21.2 us (24%)
  blocking collectives  11.5 us (13%)
  Pallas kernels  9.15 us (10%)
    ppermute x6, starting transfers between devices, shifted(): return lax.ppermute(value, axis, pairs)  18.5 us
    all_to_all x1, starting transfers between devices, shards(): rows = lax.all_to_all(chunk, GY, 0, 0, tiled=True)  13.7 us
    ppermute x3, starting transfers between devices, swapped(): return lax.ppermute(value, 'ca', [(0, 1), (1, 0)])  12.3 us
    all_to_all x1, blocking collectives, shards(): planes = lax.all_to_all(planes, 'xa', 0, 0, tiled=True)  11.5 us
    pallas_call x5, Pallas kernels, call(): pl.pallas_call(kernel, in_specs=specs, out_specs=[VMEM] * len(outs), out_...  9.15 us
    ppermute x6, waiting for transfers between devices, shifted(): return lax.ppermute(value, axis, pairs)  7.78 us
    all_to_all x1, waiting for transfers between devices, shards(): rows = lax.all_to_all(chunk, GY, 0, 0, tiled=True)  6.1 us
    ppermute x2, waiting for transfers between devices, parted(): return lax.ppermute(value, ('ya', 'ca'), pairs)  5.17 us
  transfers between devices with their start and end apart: 12, of which 7 were waited for; matrix products, arithmetic and copies ran while one was open for 0% of the time, Pallas kernels for 0%

profile of v4, /device:TPU:1, one launch (start us, length us, event | category | flops | bytes accessed | tf_op | source)
XLA Modules:
  0.0 89.1 jit_solution(13321270335711352077)
XLA Ops:
  0.0 1.2 %shard_map.37 = (f32[4,2,4,8,128]{4,3,2,1,0:T(8,128)S(1)}, f32[8,128]{1,0:T(8,128)S(1)}) custom-call(f32[3]{0:T(128)} %table_hbm.1, s32[4,8,512]{2,1,0:T(8,128)} %labels_hbm.1, f32[4,8,512]{2,1,0:T(8,128)} %source_hbm.1), custom_call_target="tpu_custom_call" | custom-call | tf_op jit(solution)/shard_map/pallas_call | solution.py:496
  1.2 8.8 %collective-permute-start.1 = (f32[4,2,4,8,128]{4,3,2,1,0:T(8,128)S(1)}, f32[4,2,4,8,128]{4,3,2,1,0:T(8,128)S(1)}, u32[]{:S(2)}, u32[]{:S(2)}) collective-permute-start(f32[4,2,4,8,128]{4,3,2,1,0:T(8,128)S(1)} %get-tuple-element.28.own_ref), channel_id=1, source_target_pairs={{1,0},{2,1},{3,2},{4,3},{5,4},{6,5},{7,6},{8,7},{9,8},{10,9},{11,1... | collective-permute-start | bytes 393224 | tf_op jit(solution)/shard_map/ppermute | solution.py:512
  10.0 1.9 %collective-permute-start = (f32[4,2,4,8,128]{4,3,2,1,0:T(8,128)S(1)}, f32[4,2,4,8,128]{4,3,2,1,0:T(8,128)S(1)}, u32[]{:S(2)}, u32[]{:S(2)}) collective-permute-start(f32[4,2,4,8,128]{4,3,2,1,0:T(8,128)S(1)} %get-tuple-element.28.own_ref), channel_id=1, source_target_pairs={{0,1},{1,2},{2,3},{3,4},{4,5},{5,6},{6,7},{7,8},{8,9},{9,10},{10,1... | collective-permute-start | bytes 393224 | tf_op jit(solution)/shard_map/ppermute | solution.py:512
  11.9 0.0 collective-permute-done.1.high_ref
  11.9 1.9 %collective-permute-done.low_ref = f32[4,2,4,8,128]{4,3,2,1,0:T(8,128)S(1)} collective-permute-done((f32[4,2,4,8,128]{4,3,2,1,0:T(8,128)S(1)}, f32[4,2,4,8,128]{4,3,2,1,0:T(8,128)S(1)}, u32[]{:S(2)}, u32[]{:S(2)}) %collective-permute-start) | collective-permute-done | bytes 131104 | tf_op jit(solution)/shard_map/ppermute | solution.py:512
  13.8 0.1 shard_map.38
  13.9 1.3 %collective-permute-start.3 = (f32[4,128,128]{2,1,0:T(8,128)S(1)}, f32[4,128,128]{2,1,0:T(8,128)S(1)}, u32[]{:S(2)}, u32[]{:S(2)}) collective-permute-start(f32[4,128,128]{2,1,0:T(8,128)S(1)} %get-tuple-element.30), channel_id=1, source_target_pairs={{0,16},{16,32},{32,48},{48,64},{64,80},{80,96},{96,112},{112,128},... | collective-permute-start | bytes 786440 | tf_op jit(solution)/shard_map/ppermute | solution.py:512
  15.2 1.3 %collective-permute-start.4 = (f32[4,128,128]{2,1,0:T(8,128)S(1)}, f32[4,128,128]{2,1,0:T(8,128)S(1)}, u32[]{:S(2)}, u32[]{:S(2)}) collective-permute-start(f32[4,128,128]{2,1,0:T(8,128)S(1)} %get-tuple-element.32), channel_id=1, source_target_pairs={{16,0},{32,16},{48,32},{64,48},{80,64},{96,80},{112,96},{128,112},... | collective-permute-start | bytes 786440 | tf_op jit(solution)/shard_map/ppermute | solution.py:512
  16.5 3.9 %collective-permute-start.2 = (f32[4,48,128]{2,1,0:T(8,128)S(1)}, f32[4,48,128]{2,1,0:T(8,128)S(1)}, u32[]{:S(2)}, u32[]{:S(2)}) collective-permute-start(f32[4,48,128]{2,1,0:T(8,128)S(1)} %get-tuple-element.29), channel_id=1, source_target_pairs={{0,32},{16,48},{32,64},{48,80},{64,96},{80,112},{96,128},{112,144}... | collective-permute-start | bytes 294920 | tf_op jit(solution)/shard_map/ppermute | solution.py:512
  20.5 1.3 %collective-permute-start.5 = (f32[4,48,128]{2,1,0:T(8,128)S(1)}, f32[4,48,128]{2,1,0:T(8,128)S(1)}, u32[]{:S(2)}, u32[]{:S(2)}) collective-permute-start(f32[4,48,128]{2,1,0:T(8,128)S(1)} %get-tuple-element.33), channel_id=1, source_target_pairs={{32,0},{48,16},{64,32},{80,48},{96,64},{112,80},{128,96},{144,112}... | collective-permute-start | bytes 294920 | tf_op jit(solution)/shard_map/ppermute | solution.py:512
  21.8 0.1 stack.19.spot_ref
  21.9 1.3 %collective-permute-done.2.low2_ref = f32[4,48,128]{2,1,0:T(8,128)S(1)} collective-permute-done((f32[4,48,128]{2,1,0:T(8,128)S(1)}, f32[4,48,128]{2,1,0:T(8,128)S(1)}, u32[]{:S(2)}, u32[]{:S(2)}) %collective-permute-start.2) | collective-permute-done | bytes 98336 | tf_op jit(solution)/shard_map/ppermute | solution.py:512
  23.1 4.6 %collective-permute-done.5.high2_ref = f32[4,48,128]{2,1,0:T(8,128)S(1)} collective-permute-done((f32[4,48,128]{2,1,0:T(8,128)S(1)}, f32[4,48,128]{2,1,0:T(8,128)S(1)}, u32[]{:S(2)}, u32[]{:S(2)}) %collective-permute-start.5) | collective-permute-done | bytes 98336 | tf_op jit(solution)/shard_map/ppermute | solution.py:512
  27.7 0.0 collective-permute-done.3.low1_ref
  27.7 0.0 collective-permute-done.4.high1_ref
  27.7 5.1 %shard_map.39 = (f32[16,16,128]{2,1,0:T(8,128)}, f32[2,16,128]{2,1,0:T(8,128)S(1)}, f32[5,4,8,128]{3,2,1,0:T(8,128)S(1)}, f32[4,4,24,128]{3,2,1,0:T(8,128)S(1)},...) custom-call(s32[6]{0:T(128)S(1)} %stack.19.spot_ref, ...), custom_call_target="tpu_custom_call" | custom-call | tf_op jit(solution)/shard_map/pallas_call | solution.py:496
  32.8 13.7 %all-to-all-start = ((f32[16,16,128]{2,1,0:T(8,128)}), f32[16,16,128]{2,1,0:T(8,128)S(1)}, u32[]{:S(2)}, u32[]{:S(2)}) async-start(f32[16,16,128]{2,1,0:T(8,128)} %get-tuple-element.34), calls=%async_computation | async-start | bytes 262144 | tf_op jit(solution)/shard_map/all_to_all | solution.py:580
  46.5 2.0 %collective-permute-start.6 = (f32[2,16,128]{2,1,0:T(8,128)S(1)}, f32[2,16,128]{2,1,0:T(8,128)S(1)}, u32[]{:S(2)}, u32[]{:S(2)}) collective-permute-start(f32[2,16,128]{2,1,0:T(8,128)S(1)} %get-tuple-element.35.ends_ref), channel_id=1, source_target_pairs={{0,1},{1,0},{2,3},{3,2},{4,5},{5,4},{6,7},{7,6},{8,9},{9,8},{10,11... | collective-permute-start | bytes 49160 | tf_op jit(solution)/shard_map/ppermute | solution.py:524
  48.5 1.0 %collective-permute-done.6.other_ref = f32[2,16,128]{2,1,0:T(8,128)S(1)} collective-permute-done((f32[2,16,128]{2,1,0:T(8,128)S(1)}, f32[2,16,128]{2,1,0:T(8,128)S(1)}, u32[]{:S(2)}, u32[]{:S(2)}) %collective-permute-start.6) | collective-permute-done | bytes 16416 | tf_op jit(solution)/shard_map/ppermute | solution.py:524
  49.6 6.1 %all-to-all-done.got_ref.rows_ref = f32[16,16,128]{2,1,0:T(8,128)S(1)} async-done(((f32[16,16,128]{2,1,0:T(8,128)}), f32[16,16,128]{2,1,0:T(8,128)S(1)}, u32[]{:S(2)}, u32[]{:S(2)}) %all-to-all-start) | async-done | bytes 131104 | tf_op jit(solution)/shard_map/all_to_all | solution.py:580
  55.7 0.6 shard_map.40
  56.3 11.5 %all_to_all.10.mid_ref = f32[4,112,128]{2,1,0:T(8,128)S(1)} all-to-all(f32[4,112,128]{2,1,0:T(8,128)S(1)} %shard_map.40), channel_id=1, replica_groups=mesh['ya'=8,'xa'=4,'za'=8,'ca'=2] {'xa'}, dimensions={0} | all-to-all | bytes 458752 | tf_op jit(solution)/shard_map/all_to_all | solution.py:586
  67.7 1.3 %collective-permute-start.8 = (f32[4,112,128]{2,1,0:T(8,128)S(1)}, f32[4,112,128]{2,1,0:T(8,128)S(1)}, u32[]{:S(2)}, u32[]{:S(2)}) collective-permute-start(f32[4,112,128]{2,1,0:T(8,128)S(1)} %all_to_all.10.mid_ref), channel_id=1, source_target_pairs={{0,128},{129,1},{64,192},{193,65},{128,256},{257,129},{192,320},{3... | collective-permute-start | bytes 688136 | tf_op jit(solution)/shard_map/ppermute | solution.py:520
  69.0 1.3 %collective-permute-start.7 = (f32[4,112,128]{2,1,0:T(8,128)S(1)}, f32[4,112,128]{2,1,0:T(8,128)S(1)}, u32[]{:S(2)}, u32[]{:S(2)}) collective-permute-start(f32[4,112,128]{2,1,0:T(8,128)S(1)} %all_to_all.10.mid_ref), channel_id=1, source_target_pairs={{0,64},{65,1},{64,128},{129,65},{128,192},{193,129},{192,256},{257... | collective-permute-start | bytes 688136 | tf_op jit(solution)/shard_map/ppermute | solution.py:520
  70.3 5.2 %collective-permute-done.8.took2_ref = f32[4,112,128]{2,1,0:T(8,128)S(1)} collective-permute-done((f32[4,112,128]{2,1,0:T(8,128)S(1)}, f32[4,112,128]{2,1,0:T(8,128)S(1)}, u32[]{:S(2)}, u32[]{:S(2)}) %collective-permute-start.8) | collective-permute-done | bytes 229408 | tf_op jit(solution)/shard_map/ppermute | solution.py:520
  75.5 6.8 %collective-permute-start.10 = (f32[4,112,128]{2,1,0:T(8,128)S(1)}, f32[4,112,128]{2,1,0:T(8,128)S(1)}, u32[]{:S(2)}, u32[]{:S(2)}) collective-permute-start(f32[4,112,128]{2,1,0:T(8,128)S(1)} %collective-permute-done.8.took2_ref), channel_id=1, source_target_pairs={{0,1},{1,0},{2,3},{3,2},{4,5},{5,4},{6,7},{7,6},{8,9},{9,8},{10,11... | collective-permute-start | bytes 688136 | tf_op jit(solution)/shard_map/ppermute | solution.py:524
  82.3 0.0 collective-permute-done.7.took1_ref
  82.3 3.5 %collective-permute-start.9 = (f32[4,112,128]{2,1,0:T(8,128)S(1)}, f32[4,112,128]{2,1,0:T(8,128)S(1)}, u32[]{:S(2)}, u32[]{:S(2)}) collective-permute-start(f32[4,112,128]{2,1,0:T(8,128)S(1)} %collective-permute-done.7.took1_ref), channel_id=1, source_target_pairs={{0,1},{1,0},{2,3},{3,2},{4,5},{5,4},{6,7},{7,6},{8,9},{9,8},{10,11... | collective-permute-start | bytes 688136 | tf_op jit(solution)/shard_map/ppermute | solution.py:524
  85.8 0.0 collective-permute-done.10.gave2_ref
  85.8 1.1 %collective-permute-done.9.gave1_ref = f32[4,112,128]{2,1,0:T(8,128)S(1)} collective-permute-done((f32[4,112,128]{2,1,0:T(8,128)S(1)}, f32[4,112,128]{2,1,0:T(8,128)S(1)}, u32[]{:S(2)}, u32[]{:S(2)}) %collective-permute-start.9) | collective-permute-done | bytes 229408 | tf_op jit(solution)/shard_map/ppermute | solution.py:524
  86.9 2.2 %shard_map.41 = f32[4,8,512]{2,1,0:T(8,128)} custom-call(s32[6]{0:T(128)S(1)} %stack.19.spot_ref, f32[4,112,128]{2,1,0:T(8,128)S(1)} %collective-permute-done.7.took1_ref, f32[4,112,128]{2,1,0:T(8,128)S(1)} %collective-permute-done.8.took2_ref, f32[4,112,128]{2,1,0:T(8,128)S(1)} %all_to_all.10.mid_ref, f32[4,112,128]{2,1,0:T(8,128)S(1)} %collective-permute-done.9.gave1_ref, ...), custom_call_target="tpu_custom_call" | custom-call | tf_op jit(solution)/shard_map/pallas_call | solution.py:496
Async XLA Ops:
  1.2 10.7 %collective-permute-start.1 = (f32[4,2,4,8,128]{4,3,2,1,0:T(8,128)S(1)}, f32[4,2,4,8,128]{4,3,2,1,0:T(8,128)S(1)}, u32[]{:S(2)}, u32[]{:S(2)}) collective-permute-start(f32[4,2,4,8,128]{4,3,2,1,0:T(8,128)S(1)} %get-tuple-element.28.own_ref), channel_id=1, source_target_pairs={{1,0},{2,1},{3,2},{4,3},{5,4},{6,5},{7,6},{8,7},{9,8},{10,9},{11,1... | collective-permute-start | bytes 393224 | tf_op jit(solution)/shard_map/ppermute | solution.py:512
  10.0 3.9 %collective-permute-start = (f32[4,2,4,8,128]{4,3,2,1,0:T(8,128)S(1)}, f32[4,2,4,8,128]{4,3,2,1,0:T(8,128)S(1)}, u32[]{:S(2)}, u32[]{:S(2)}) collective-permute-start(f32[4,2,4,8,128]{4,3,2,1,0:T(8,128)S(1)} %get-tuple-element.28.own_ref), channel_id=1, source_target_pairs={{0,1},{1,2},{2,3},{3,4},{4,5},{5,6},{6,7},{7,8},{8,9},{9,10},{10,1... | collective-permute-start | bytes 393224 | tf_op jit(solution)/shard_map/ppermute | solution.py:512
  13.9 13.8 %collective-permute-start.3 = (f32[4,128,128]{2,1,0:T(8,128)S(1)}, f32[4,128,128]{2,1,0:T(8,128)S(1)}, u32[]{:S(2)}, u32[]{:S(2)}) collective-permute-start(f32[4,128,128]{2,1,0:T(8,128)S(1)} %get-tuple-element.30), channel_id=1, source_target_pairs={{0,16},{16,32},{32,48},{48,64},{64,80},{80,96},{96,112},{112,128},... | collective-permute-start | bytes 786440 | tf_op jit(solution)/shard_map/ppermute | solution.py:512
  15.2 12.5 %collective-permute-start.4 = (f32[4,128,128]{2,1,0:T(8,128)S(1)}, f32[4,128,128]{2,1,0:T(8,128)S(1)}, u32[]{:S(2)}, u32[]{:S(2)}) collective-permute-start(f32[4,128,128]{2,1,0:T(8,128)S(1)} %get-tuple-element.32), channel_id=1, source_target_pairs={{16,0},{32,16},{48,32},{64,48},{80,64},{96,80},{112,96},{128,112},... | collective-permute-start | bytes 786440 | tf_op jit(solution)/shard_map/ppermute | solution.py:512
  16.5 6.6 %collective-permute-start.2 = (f32[4,48,128]{2,1,0:T(8,128)S(1)}, f32[4,48,128]{2,1,0:T(8,128)S(1)}, u32[]{:S(2)}, u32[]{:S(2)}) collective-permute-start(f32[4,48,128]{2,1,0:T(8,128)S(1)} %get-tuple-element.29), channel_id=1, source_target_pairs={{0,32},{16,48},{32,64},{48,80},{64,96},{80,112},{96,128},{112,144}... | collective-permute-start | bytes 294920 | tf_op jit(solution)/shard_map/ppermute | solution.py:512
  20.5 7.3 %collective-permute-start.5 = (f32[4,48,128]{2,1,0:T(8,128)S(1)}, f32[4,48,128]{2,1,0:T(8,128)S(1)}, u32[]{:S(2)}, u32[]{:S(2)}) collective-permute-start(f32[4,48,128]{2,1,0:T(8,128)S(1)} %get-tuple-element.33), channel_id=1, source_target_pairs={{32,0},{48,16},{64,32},{80,48},{96,64},{112,80},{128,96},{144,112}... | collective-permute-start | bytes 294920 | tf_op jit(solution)/shard_map/ppermute | solution.py:512
  32.8 22.9 %all-to-all-start = ((f32[16,16,128]{2,1,0:T(8,128)}), f32[16,16,128]{2,1,0:T(8,128)S(1)}, u32[]{:S(2)}, u32[]{:S(2)}) async-start(f32[16,16,128]{2,1,0:T(8,128)} %get-tuple-element.34), calls=%async_computation | async-start | bytes 262144 | tf_op jit(solution)/shard_map/all_to_all | solution.py:580
  46.5 3.1 %collective-permute-start.6 = (f32[2,16,128]{2,1,0:T(8,128)S(1)}, f32[2,16,128]{2,1,0:T(8,128)S(1)}, u32[]{:S(2)}, u32[]{:S(2)}) collective-permute-start(f32[2,16,128]{2,1,0:T(8,128)S(1)} %get-tuple-element.35.ends_ref), channel_id=1, source_target_pairs={{0,1},{1,0},{2,3},{3,2},{4,5},{5,4},{6,7},{7,6},{8,9},{9,8},{10,11... | collective-permute-start | bytes 49160 | tf_op jit(solution)/shard_map/ppermute | solution.py:524
  67.7 7.8 %collective-permute-start.8 = (f32[4,112,128]{2,1,0:T(8,128)S(1)}, f32[4,112,128]{2,1,0:T(8,128)S(1)}, u32[]{:S(2)}, u32[]{:S(2)}) collective-permute-start(f32[4,112,128]{2,1,0:T(8,128)S(1)} %all_to_all.10.mid_ref), channel_id=1, source_target_pairs={{0,128},{129,1},{64,192},{193,65},{128,256},{257,129},{192,320},{3... | collective-permute-start | bytes 688136 | tf_op jit(solution)/shard_map/ppermute | solution.py:520
  69.0 13.3 %collective-permute-start.7 = (f32[4,112,128]{2,1,0:T(8,128)S(1)}, f32[4,112,128]{2,1,0:T(8,128)S(1)}, u32[]{:S(2)}, u32[]{:S(2)}) collective-permute-start(f32[4,112,128]{2,1,0:T(8,128)S(1)} %all_to_all.10.mid_ref), channel_id=1, source_target_pairs={{0,64},{65,1},{64,128},{129,65},{128,192},{193,129},{192,256},{257... | collective-permute-start | bytes 688136 | tf_op jit(solution)/shard_map/ppermute | solution.py:520
  75.5 10.3 %collective-permute-start.10 = (f32[4,112,128]{2,1,0:T(8,128)S(1)}, f32[4,112,128]{2,1,0:T(8,128)S(1)}, u32[]{:S(2)}, u32[]{:S(2)}) collective-permute-start(f32[4,112,128]{2,1,0:T(8,128)S(1)} %collective-permute-done.8.took2_ref), channel_id=1, source_target_pairs={{0,1},{1,0},{2,3},{3,2},{4,5},{5,4},{6,7},{7,6},{8,9},{9,8},{10,11... | collective-permute-start | bytes 688136 | tf_op jit(solution)/shard_map/ppermute | solution.py:524
  82.3 4.6 %collective-permute-start.9 = (f32[4,112,128]{2,1,0:T(8,128)S(1)}, f32[4,112,128]{2,1,0:T(8,128)S(1)}, u32[]{:S(2)}, u32[]{:S(2)}) collective-permute-start(f32[4,112,128]{2,1,0:T(8,128)S(1)} %collective-permute-done.7.took1_ref), channel_id=1, source_target_pairs={{0,1},{1,0},{2,3},{3,2},{4,5},{5,4},{6,7},{7,6},{8,9},{9,8},{10,11... | collective-permute-start | bytes 688136 | tf_op jit(solution)/shard_map/ppermute | solution.py:524

commit v5 on v4

--- a/solution.py
+++ b/solution.py
@@ -13,6 +13,7 @@
 PLANES = 4 + 2 * REACH
 WINDOW = 8
 SPAN = 20
+CORE = 12
 KEEP = 0.2
 OMEGA = 0.8
 
@@ -334,7 +335,11 @@
         inside = jnp.where((block >= 0) & (block < count), 1.0, 0.0).astype(F32)
         value = got_ref[jnp.clip(block, 0, count - 1), pl.ds(0, 8)] * inside
         for which in range(4):
-            chunk[pl.ds(SPAN * which + 2 * step, 2)] = value[2 * which : 2 * which + 2]
+            if 2 <= step < 8:
+                at = CORE * which + 2 * step - 4
+            else:
+                at = 4 * CORE + (SPAN - CORE) * which + (2 * step if step < 2 else 2 * step - CORE)
+            chunk[pl.ds(at, 2)] = value[2 * which : 2 * which + 2]
     body = chunk[...]
     size = out_ref.shape[0]
     first = (core == 0).astype(F32)
@@ -348,7 +353,7 @@
 
 
 def down_kernel(
-    spot_ref, took1_ref, took2_ref, mid_ref, gave1_ref, gave2_ref, rows_ref, fx, fy, fz, w, s, v2,
+    spot_ref, took1_ref, took2_ref, mid_ref, gave_ref, rows_ref, fx, fy, fz, w, s, v2,
     fxm, fym, fzm, wm, sm, vm, root,
     out_ref,
     parts, state, ends, field, third, total,
@@ -362,6 +367,8 @@
 
     lower_core = spot_ref[5] == 0
     block = mid_ref.shape[0]
+    gave1_ref = gave_ref.at[:, pl.ds(0, 4 * SPAN + 32)]
+    gave2_ref = gave_ref.at[:, pl.ds(4 * SPAN + 32, 4 * CORE)]
     sources = (
         (took2_ref, gave2_ref), (took1_ref, gave1_ref), (mid_ref, None), (gave1_ref, took1_ref), (gave2_ref, took2_ref)
     )
@@ -375,12 +382,18 @@
                     value = jnp.where(lower_core, value, two[plane, pl.ds(first, rows)])
                 return value
 
+            blank = jnp.zeros((4, LANES), F32)
             for which in range(4):
-                value = jnp.where(row < SPAN, read(SPAN * which, ROWS), 0.0)
+                below = above = blank
+                if 0 < number < 4:
+                    outer = read(4 * CORE + (SPAN - CORE) * which, SPAN - CORE)
+                    below, above = outer[:4], outer[4:]
+                value = jnp.concatenate([below, read(CORE * which, CORE), above, blank], axis=0)
                 parts[which, at] = value
                 if which == 0:
                     state[0, at] = value
-            ends[at] = jnp.where(lower_core, read(4 * SPAN, 16), read(4 * SPAN + 16, 16))
+            if 0 < number < 4:
+                ends[at] = jnp.where(lower_core, read(4 * SPAN, 16), read(4 * SPAN + 16, 16))
 
     for turn in range(1, WINDOW):
         old = (turn - 1) % 2
@@ -584,12 +597,14 @@
         window_kernel, [SMEM] + [VMEM] * 3, [window], [room(4 * SPAN, LANES)], spot, rows, ends, other
     )
     planes = lax.all_to_all(planes, "xa", 0, 0, tiled=True)
+    planes, middle_rows = lax.optimization_barrier((planes, planes[:, : 4 * CORE]))
     took1 = parted(planes, 1)
-    took2 = parted(planes, 2)
-    blocks = [took1, took2, planes, swapped(took1), swapped(took2)]
+    took2 = parted(middle_rows, 2)
+    gave = swapped(jnp.concatenate([took1, took2], axis=1))
+    blocks = [took1, took2, planes, gave]
     (correction,) = call(
         down_kernel,
-        [SMEM] + [VMEM] * 19,
+        [SMEM] + [VMEM] * 18,
         [(4, 8, 4 * LANES)],
         [
             room(4, 5 * block, ROWS, LANES), room(2, 5 * block, ROWS, LANES), room(5 * block, 16, LANES),

time: 89.7 us -> 88.5 us (0.987)
  starting transfers between devices: 47.1 us -> 44.7 us
  waiting for transfers between devices: 21.2 us -> 22.4 us
    ppermute x3 -> x2, starting transfers between devices: 12.3 us -> 9.93 us  [swapped(): return lax.ppermute(value, 'ca', [(0, 1), (1, 0)])]
    ppermute x2, waiting for transfers between devices: 5.17 us -> 6.23 us  [parted(): return lax.ppermute(value, ('ya', 'ca'), pairs)]
    ppermute x3 -> x2, waiting for transfers between devices: 2.13 us -> 2.28 us  [swapped(): return lax.ppermute(value, 'ca', [(0, 1), (1, 0)])]
  transfers between devices with their start and end apart: 12 -> 11, of which waited for: 7 -> 7; matrix products, arithmetic and copies ran while one was open for 0% -> 0% of each run, Pallas kernels for 0% -> 0%
where the time goes in v5:
time: 88.5 us; the launch traced here: 88 us
  starting transfers between devices  44.7 us (51%)
  waiting for transfers between devices  22.4 us (25%)
  blocking collectives  11.5 us (13%)
  Pallas kernels  9.15 us (10%)
    ppermute x6, starting transfers between devices, shifted(): return lax.ppermute(value, axis, pairs)  18.5 us
    all_to_all x1, starting transfers between devices, shards(): rows = lax.all_to_all(chunk, GY, 0, 0, tiled=True)  13.7 us
    all_to_all x1, blocking collectives, shards(): planes = lax.all_to_all(planes, 'xa', 0, 0, tiled=True)  11.5 us
    ppermute x2, starting transfers between devices, swapped(): return lax.ppermute(value, 'ca', [(0, 1), (1, 0)])  9.93 us
    pallas_call x5, Pallas kernels, call(): pl.pallas_call(kernel, in_specs=specs, out_specs=[VMEM] * len(outs), out_...  9.15 us
    ppermute x6, waiting for transfers between devices, shifted(): return lax.ppermute(value, axis, pairs)  7.78 us
    ppermute x2, waiting for transfers between devices, parted(): return lax.ppermute(value, ('ya', 'ca'), pairs)  6.23 us
    all_to_all x1, waiting for transfers between devices, shards(): rows = lax.all_to_all(chunk, GY, 0, 0, tiled=True)  6.1 us
  transfers between devices with their start and end apart: 11, of which 7 were waited for; matrix products, arithmetic and copies ran while one was open for 0% of the time, Pallas kernels for 0%

profile of v5, /device:TPU:1, one launch (start us, length us, event | category | flops | bytes accessed | tf_op | source)
XLA Modules:
  0.0 88.0 jit_solution(18186413142383443398)
XLA Ops:
  0.0 1.2 %shard_map.37 = (f32[4,2,4,8,128]{4,3,2,1,0:T(8,128)S(1)}, f32[8,128]{1,0:T(8,128)S(1)}) custom-call(f32[3]{0:T(128)} %table_hbm.1, s32[4,8,512]{2,1,0:T(8,128)} %labels_hbm.1, f32[4,8,512]{2,1,0:T(8,128)} %source_hbm.1), custom_call_target="tpu_custom_call" | custom-call | tf_op jit(solution)/shard_map/pallas_call | solution.py:509
  1.2 8.8 %collective-permute-start.1 = (f32[4,2,4,8,128]{4,3,2,1,0:T(8,128)S(1)}, f32[4,2,4,8,128]{4,3,2,1,0:T(8,128)S(1)}, u32[]{:S(2)}, u32[]{:S(2)}) collective-permute-start(f32[4,2,4,8,128]{4,3,2,1,0:T(8,128)S(1)} %get-tuple-element.30.own_ref), channel_id=1, source_target_pairs={{1,0},{2,1},{3,2},{4,3},{5,4},{6,5},{7,6},{8,7},{9,8},{10,9},{11,1... | collective-permute-start | bytes 393224 | tf_op jit(solution)/shard_map/ppermute | solution.py:525
  10.0 1.9 %collective-permute-start = (f32[4,2,4,8,128]{4,3,2,1,0:T(8,128)S(1)}, f32[4,2,4,8,128]{4,3,2,1,0:T(8,128)S(1)}, u32[]{:S(2)}, u32[]{:S(2)}) collective-permute-start(f32[4,2,4,8,128]{4,3,2,1,0:T(8,128)S(1)} %get-tuple-element.30.own_ref), channel_id=1, source_target_pairs={{0,1},{1,2},{2,3},{3,4},{4,5},{5,6},{6,7},{7,8},{8,9},{9,10},{10,1... | collective-permute-start | bytes 393224 | tf_op jit(solution)/shard_map/ppermute | solution.py:525
  11.9 0.0 collective-permute-done.1.high_ref
  11.9 1.9 %collective-permute-done.low_ref = f32[4,2,4,8,128]{4,3,2,1,0:T(8,128)S(1)} collective-permute-done((f32[4,2,4,8,128]{4,3,2,1,0:T(8,128)S(1)}, f32[4,2,4,8,128]{4,3,2,1,0:T(8,128)S(1)}, u32[]{:S(2)}, u32[]{:S(2)}) %collective-permute-start) | collective-permute-done | bytes 131104 | tf_op jit(solution)/shard_map/ppermute | solution.py:525
  13.8 0.1 shard_map.38
  13.9 1.3 %collective-permute-start.3 = (f32[4,128,128]{2,1,0:T(8,128)S(1)}, f32[4,128,128]{2,1,0:T(8,128)S(1)}, u32[]{:S(2)}, u32[]{:S(2)}) collective-permute-start(f32[4,128,128]{2,1,0:T(8,128)S(1)} %get-tuple-element.32), channel_id=1, source_target_pairs={{0,16},{16,32},{32,48},{48,64},{64,80},{80,96},{96,112},{112,128},... | collective-permute-start | bytes 786440 | tf_op jit(solution)/shard_map/ppermute | solution.py:525
  15.2 1.3 %collective-permute-start.4 = (f32[4,128,128]{2,1,0:T(8,128)S(1)}, f32[4,128,128]{2,1,0:T(8,128)S(1)}, u32[]{:S(2)}, u32[]{:S(2)}) collective-permute-start(f32[4,128,128]{2,1,0:T(8,128)S(1)} %get-tuple-element.34), channel_id=1, source_target_pairs={{16,0},{32,16},{48,32},{64,48},{80,64},{96,80},{112,96},{128,112},... | collective-permute-start | bytes 786440 | tf_op jit(solution)/shard_map/ppermute | solution.py:525
  16.5 3.9 %collective-permute-start.2 = (f32[4,48,128]{2,1,0:T(8,128)S(1)}, f32[4,48,128]{2,1,0:T(8,128)S(1)}, u32[]{:S(2)}, u32[]{:S(2)}) collective-permute-start(f32[4,48,128]{2,1,0:T(8,128)S(1)} %get-tuple-element.31), channel_id=1, source_target_pairs={{0,32},{16,48},{32,64},{48,80},{64,96},{80,112},{96,128},{112,144}... | collective-permute-start | bytes 294920 | tf_op jit(solution)/shard_map/ppermute | solution.py:525
  20.5 1.3 %collective-permute-start.5 = (f32[4,48,128]{2,1,0:T(8,128)S(1)}, f32[4,48,128]{2,1,0:T(8,128)S(1)}, u32[]{:S(2)}, u32[]{:S(2)}) collective-permute-start(f32[4,48,128]{2,1,0:T(8,128)S(1)} %get-tuple-element.35), channel_id=1, source_target_pairs={{32,0},{48,16},{64,32},{80,48},{96,64},{112,80},{128,96},{144,112}... | collective-permute-start | bytes 294920 | tf_op jit(solution)/shard_map/ppermute | solution.py:525
  21.8 0.1 stack.19.spot_ref
  21.9 1.3 %collective-permute-done.2.low2_ref = f32[4,48,128]{2,1,0:T(8,128)S(1)} collective-permute-done((f32[4,48,128]{2,1,0:T(8,128)S(1)}, f32[4,48,128]{2,1,0:T(8,128)S(1)}, u32[]{:S(2)}, u32[]{:S(2)}) %collective-permute-start.2) | collective-permute-done | bytes 98336 | tf_op jit(solution)/shard_map/ppermute | solution.py:525
  23.1 4.6 %collective-permute-done.5.high2_ref = f32[4,48,128]{2,1,0:T(8,128)S(1)} collective-permute-done((f32[4,48,128]{2,1,0:T(8,128)S(1)}, f32[4,48,128]{2,1,0:T(8,128)S(1)}, u32[]{:S(2)}, u32[]{:S(2)}) %collective-permute-start.5) | collective-permute-done | bytes 98336 | tf_op jit(solution)/shard_map/ppermute | solution.py:525
  27.7 0.0 collective-permute-done.3.low1_ref
  27.7 0.0 collective-permute-done.4.high1_ref
  27.7 5.1 %shard_map.39 = (f32[16,16,128]{2,1,0:T(8,128)}, f32[2,16,128]{2,1,0:T(8,128)S(1)}, f32[5,4,8,128]{3,2,1,0:T(8,128)S(1)}, f32[4,4,24,128]{3,2,1,0:T(8,128)S(1)},...) custom-call(s32[6]{0:T(128)S(1)} %stack.19.spot_ref, ...), custom_call_target="tpu_custom_call" | custom-call | tf_op jit(solution)/shard_map/pallas_call | solution.py:509
  32.8 13.7 %all-to-all-start = ((f32[16,16,128]{2,1,0:T(8,128)}), f32[16,16,128]{2,1,0:T(8,128)S(1)}, u32[]{:S(2)}, u32[]{:S(2)}) async-start(f32[16,16,128]{2,1,0:T(8,128)} %get-tuple-element.36), calls=%async_computation | async-start | bytes 262144 | tf_op jit(solution)/shard_map/all_to_all | solution.py:593
  46.5 2.0 %collective-permute-start.6 = (f32[2,16,128]{2,1,0:T(8,128)S(1)}, f32[2,16,128]{2,1,0:T(8,128)S(1)}, u32[]{:S(2)}, u32[]{:S(2)}) collective-permute-start(f32[2,16,128]{2,1,0:T(8,128)S(1)} %get-tuple-element.37.ends_ref), channel_id=1, source_target_pairs={{0,1},{1,0},{2,3},{3,2},{4,5},{5,4},{6,7},{7,6},{8,9},{9,8},{10,11... | collective-permute-start | bytes 49160 | tf_op jit(solution)/shard_map/ppermute | solution.py:537
  48.5 1.0 %collective-permute-done.6.other_ref = f32[2,16,128]{2,1,0:T(8,128)S(1)} collective-permute-done((f32[2,16,128]{2,1,0:T(8,128)S(1)}, f32[2,16,128]{2,1,0:T(8,128)S(1)}, u32[]{:S(2)}, u32[]{:S(2)}) %collective-permute-start.6) | collective-permute-done | bytes 16416 | tf_op jit(solution)/shard_map/ppermute | solution.py:537
  49.5 6.1 %all-to-all-done.got_ref.rows_ref = f32[16,16,128]{2,1,0:T(8,128)S(1)} async-done(((f32[16,16,128]{2,1,0:T(8,128)}), f32[16,16,128]{2,1,0:T(8,128)S(1)}, u32[]{:S(2)}, u32[]{:S(2)}) %all-to-all-start) | async-done | bytes 131104 | tf_op jit(solution)/shard_map/all_to_all | solution.py:593
  55.6 0.6 shard_map.40
  56.3 11.5 %all_to_all.10.mid_ref = f32[4,112,128]{2,1,0:T(8,128)S(1)} all-to-all(f32[4,112,128]{2,1,0:T(8,128)S(1)} %shard_map.40), channel_id=1, replica_groups=mesh['ya'=8,'xa'=4,'za'=8,'ca'=2] {'xa'}, dimensions={0} | all-to-all | bytes 458752 | tf_op jit(solution)/shard_map/all_to_all | solution.py:599
  67.7 1.3 %collective-permute-start.7 = (f32[4,112,128]{2,1,0:T(8,128)S(1)}, f32[4,112,128]{2,1,0:T(8,128)S(1)}, u32[]{:S(2)}, u32[]{:S(2)}) collective-permute-start(f32[4,112,128]{2,1,0:T(8,128)S(1)} %all_to_all.10.mid_ref), channel_id=1, source_target_pairs={{0,64},{65,1},{64,128},{129,65},{128,192},{193,129},{192,256},{257... | collective-permute-start | bytes 688136 | tf_op jit(solution)/shard_map/ppermute | solution.py:533
  69.0 1.3 %collective-permute-start.8 = (f32[4,48,128]{2,1,0:T(8,128)S(1)}, f32[4,48,128]{2,1,0:T(8,128)S(1)}, u32[]{:S(2)}, u32[]{:S(2)}) collective-permute-start(f32[4,48,128]{2,1,0:T(8,128)S(1)} %slice.4), channel_id=1, source_target_pairs={{0,128},{129,1},{64,192},{193,65},{128,256},{257,129},{192,320},{3... | collective-permute-start | bytes 294920 | tf_op jit(solution)/shard_map/ppermute | solution.py:533
  70.3 6.2 %collective-permute-done.8.took2_ref = f32[4,48,128]{2,1,0:T(8,128)S(1)} collective-permute-done((f32[4,48,128]{2,1,0:T(8,128)S(1)}, f32[4,48,128]{2,1,0:T(8,128)S(1)}, u32[]{:S(2)}, u32[]{:S(2)}) %collective-permute-start.8) | collective-permute-done | bytes 98336 | tf_op jit(solution)/shard_map/ppermute | solution.py:533
  76.6 0.0 collective-permute-done.7.took1_ref
  76.6 7.9 %collective-permute-start.9 = (f32[4,160,128]{2,1,0:T(8,128)S(1)}, f32[4,160,128]{2,1,0:T(8,128)S(1)}, u32[]{:S(2)}, u32[]{:S(2)}) collective-permute-start(f32[4,160,128]{2,1,0:T(8,128)S(1)} %pad_maximum_fusion), channel_id=1, source_target_pairs={{0,1},{1,0},{2,3},{3,2},{4,5},{5,4},{6,7},{7,6},{8,9},{9,8},{10,11... | collective-permute-start | bytes 983048 | tf_op jit(solution)/shard_map/ppermute | solution.py:537
  84.5 1.2 %collective-permute-done.9.gave_ref = f32[4,160,128]{2,1,0:T(8,128)S(1)} collective-permute-done((f32[4,160,128]{2,1,0:T(8,128)S(1)}, f32[4,160,128]{2,1,0:T(8,128)S(1)}, u32[]{:S(2)}, u32[]{:S(2)}) %collective-permute-start.9) | collective-permute-done | bytes 327712 | tf_op jit(solution)/shard_map/ppermute | solution.py:537
  85.8 2.2 %shard_map.41 = f32[4,8,512]{2,1,0:T(8,128)} custom-call(s32[6]{0:T(128)S(1)} %stack.19.spot_ref, f32[4,112,128]{2,1,0:T(8,128)S(1)} %collective-permute-done.7.took1_ref, f32[4,48,128]{2,1,0:T(8,128)S(1)} %collective-permute-done.8.took2_ref, f32[4,112,128]{2,1,0:T(8,128)S(1)} %all_to_all.10.mid_ref, f32[4,160,128]{2,1,0:T(8,128)S(1)} %collective-permute-done.9.gave_ref, ...), custom_call_target="tpu_custom_call" | custom-call | tf_op jit(solution)/shard_map/pallas_call | solution.py:509
  (2 shorter events, 0.0 us)
Async XLA Ops:
  1.2 10.7 %collective-permute-start.1 = (f32[4,2,4,8,128]{4,3,2,1,0:T(8,128)S(1)}, f32[4,2,4,8,128]{4,3,2,1,0:T(8,128)S(1)}, u32[]{:S(2)}, u32[]{:S(2)}) collective-permute-start(f32[4,2,4,8,128]{4,3,2,1,0:T(8,128)S(1)} %get-tuple-element.30.own_ref), channel_id=1, source_target_pairs={{1,0},{2,1},{3,2},{4,3},{5,4},{6,5},{7,6},{8,7},{9,8},{10,9},{11,1... | collective-permute-start | bytes 393224 | tf_op jit(solution)/shard_map/ppermute | solution.py:525
  10.0 3.9 %collective-permute-start = (f32[4,2,4,8,128]{4,3,2,1,0:T(8,128)S(1)}, f32[4,2,4,8,128]{4,3,2,1,0:T(8,128)S(1)}, u32[]{:S(2)}, u32[]{:S(2)}) collective-permute-start(f32[4,2,4,8,128]{4,3,2,1,0:T(8,128)S(1)} %get-tuple-element.30.own_ref), channel_id=1, source_target_pairs={{0,1},{1,2},{2,3},{3,4},{4,5},{5,6},{6,7},{7,8},{8,9},{9,10},{10,1... | collective-permute-start | bytes 393224 | tf_op jit(solution)/shard_map/ppermute | solution.py:525
  13.9 13.8 %collective-permute-start.3 = (f32[4,128,128]{2,1,0:T(8,128)S(1)}, f32[4,128,128]{2,1,0:T(8,128)S(1)}, u32[]{:S(2)}, u32[]{:S(2)}) collective-permute-start(f32[4,128,128]{2,1,0:T(8,128)S(1)} %get-tuple-element.32), channel_id=1, source_target_pairs={{0,16},{16,32},{32,48},{48,64},{64,80},{80,96},{96,112},{112,128},... | collective-permute-start | bytes 786440 | tf_op jit(solution)/shard_map/ppermute | solution.py:525
  15.2 12.5 %collective-permute-start.4 = (f32[4,128,128]{2,1,0:T(8,128)S(1)}, f32[4,128,128]{2,1,0:T(8,128)S(1)}, u32[]{:S(2)}, u32[]{:S(2)}) collective-permute-start(f32[4,128,128]{2,1,0:T(8,128)S(1)} %get-tuple-element.34), channel_id=1, source_target_pairs={{16,0},{32,16},{48,32},{64,48},{80,64},{96,80},{112,96},{128,112},... | collective-permute-start | bytes 786440 | tf_op jit(solution)/shard_map/ppermute | solution.py:525
  16.5 6.6 %collective-permute-start.2 = (f32[4,48,128]{2,1,0:T(8,128)S(1)}, f32[4,48,128]{2,1,0:T(8,128)S(1)}, u32[]{:S(2)}, u32[]{:S(2)}) collective-permute-start(f32[4,48,128]{2,1,0:T(8,128)S(1)} %get-tuple-element.31), channel_id=1, source_target_pairs={{0,32},{16,48},{32,64},{48,80},{64,96},{80,112},{96,128},{112,144}... | collective-permute-start | bytes 294920 | tf_op jit(solution)/shard_map/ppermute | solution.py:525
  20.5 7.3 %collective-permute-start.5 = (f32[4,48,128]{2,1,0:T(8,128)S(1)}, f32[4,48,128]{2,1,0:T(8,128)S(1)}, u32[]{:S(2)}, u32[]{:S(2)}) collective-permute-start(f32[4,48,128]{2,1,0:T(8,128)S(1)} %get-tuple-element.35), channel_id=1, source_target_pairs={{32,0},{48,16},{64,32},{80,48},{96,64},{112,80},{128,96},{144,112}... | collective-permute-start | bytes 294920 | tf_op jit(solution)/shard_map/ppermute | solution.py:525
  32.8 22.9 %all-to-all-start = ((f32[16,16,128]{2,1,0:T(8,128)}), f32[16,16,128]{2,1,0:T(8,128)S(1)}, u32[]{:S(2)}, u32[]{:S(2)}) async-start(f32[16,16,128]{2,1,0:T(8,128)} %get-tuple-element.36), calls=%async_computation | async-start | bytes 262144 | tf_op jit(solution)/shard_map/all_to_all | solution.py:593
  46.5 3.1 %collective-permute-start.6 = (f32[2,16,128]{2,1,0:T(8,128)S(1)}, f32[2,16,128]{2,1,0:T(8,128)S(1)}, u32[]{:S(2)}, u32[]{:S(2)}) collective-permute-start(f32[2,16,128]{2,1,0:T(8,128)S(1)} %get-tuple-element.37.ends_ref), channel_id=1, source_target_pairs={{0,1},{1,0},{2,3},{3,2},{4,5},{5,4},{6,7},{7,6},{8,9},{9,8},{10,11... | collective-permute-start | bytes 49160 | tf_op jit(solution)/shard_map/ppermute | solution.py:537
  67.7 8.8 %collective-permute-start.7 = (f32[4,112,128]{2,1,0:T(8,128)S(1)}, f32[4,112,128]{2,1,0:T(8,128)S(1)}, u32[]{:S(2)}, u32[]{:S(2)}) collective-permute-start(f32[4,112,128]{2,1,0:T(8,128)S(1)} %all_to_all.10.mid_ref), channel_id=1, source_target_pairs={{0,64},{65,1},{64,128},{129,65},{128,192},{193,129},{192,256},{257... | collective-permute-start | bytes 688136 | tf_op jit(solution)/shard_map/ppermute | solution.py:533
  69.0 7.5 %collective-permute-start.8 = (f32[4,48,128]{2,1,0:T(8,128)S(1)}, f32[4,48,128]{2,1,0:T(8,128)S(1)}, u32[]{:S(2)}, u32[]{:S(2)}) collective-permute-start(f32[4,48,128]{2,1,0:T(8,128)S(1)} %slice.4), channel_id=1, source_target_pairs={{0,128},{129,1},{64,192},{193,65},{128,256},{257,129},{192,320},{3... | collective-permute-start | bytes 294920 | tf_op jit(solution)/shard_map/ppermute | solution.py:533
  76.6 9.2 %collective-permute-start.9 = (f32[4,160,128]{2,1,0:T(8,128)S(1)}, f32[4,160,128]{2,1,0:T(8,128)S(1)}, u32[]{:S(2)}, u32[]{:S(2)}) collective-permute-start(f32[4,160,128]{2,1,0:T(8,128)S(1)} %pad_maximum_fusion), channel_id=1, source_target_pairs={{0,1},{1,0},{2,3},{3,2},{4,5},{5,4},{6,7},{7,6},{8,9},{9,8},{10,11... | collective-permute-start | bytes 983048 | tf_op jit(solution)/shard_map/ppermute | solution.py:537

commit v6 on v5

--- a/solution.py
+++ b/solution.py
@@ -88,18 +88,6 @@
                 out = pl.ds(offset, rows)
                 down_ref[residue, out] = all_ref[ahead, which, residue, pl.ds(row, rows)]
                 up_ref[residue, out] = all_ref[3 - ahead, which, residue, pl.ds(row, rows)]
-
-
-def fine_sum(fx_up, fx_low, fy, fz, v_up, v_low, v):
-    lane = iota((ROWS, LANES), 1)
-    total = fx_up * v_up + fx_low * v_low
-    total = total + fy * row_roll(v, -1) + row_roll(fy * v, 1)
-    zv = fz * v
-    last = jnp.where(lane == LANES - 1, 0.0, lane_roll(v[0], -1))
-    first = jnp.where(lane == 0, 0.0, lane_roll(zv[3], 1))
-    lower = [first, fz[0] * v[0], fz[1] * v[1], fz[2] * v[2]]
-    upper = [fz[0] * v[1], fz[1] * v[2], fz[2] * v[3], fz[3] * last]
-    return total + jnp.stack([lower[r] + upper[r] for r in range(4)])
 
 
 def middle_sum(fx_up, fx_low, fy, fz, v_up, v_low, v):
@@ -179,35 +167,51 @@
         return jnp.concatenate(parts, axis=0).reshape(key.shape)
 
     def faces(p, carry):
-        here = code[p]
-        fx[p] = look(here + code[p + 1])
-        fy[p] = look(here + row_roll(here, -1))
-        beyond = jnp.where(lane == LANES - 1, 0, lane_roll(here[0], -1))
-        after = jnp.stack([here[1], here[2], here[3], beyond])
-        fz_here = look(here + after)
-        fz[p] = fz_here
-        zlow[p] = jnp.where(lane == 0, look(here[0]), lane_roll(fz_here[3], 1))
+        here = [code[p, r] for r in range(4)]
+        after = here[1:] + [jnp.where(lane == LANES - 1, 0, lane_roll(here[0], -1))]
+        for r in range(4):
+            fx[p, r] = look(here[r] + code[p + 1, r])
+            fy[p, r] = look(here[r] + row_roll(here[r], -1))
+            across = look(here[r] + after[r])
+            fz[p, r] = across
+        zlow[p] = jnp.where(lane == 0, look(here[0]), lane_roll(across, 1))
         return carry
 
     lax.fori_loop(0, PLANES - 1, faces, 0, unroll=True)
 
     def start(p, carry):
-        fy_here = fy[p]
-        fz_here = fz[p]
-        lower = jnp.stack([zlow[p], fz_here[0], fz_here[1], fz_here[2]])
-        total = fx[p] + fx[p - 1] + fy_here + row_roll(fy_here, 1) + fz_here + lower
-        diag[p] = total
-        w = (OMEGA * planemask(x0 - REACH + p) * rowmask) / total
-        weight[p] = w
-        first[p] = w * source[p]
+        mask = (OMEGA * planemask(x0 - REACH + p)) * rowmask
+        lower = zlow[p]
+        for r in range(4):
+            fy_here = fy[p, r]
+            upper = fz[p, r]
+            total = fx[p, r] + fx[p - 1, r] + fy_here + row_roll(fy_here, 1) + upper + lower
+            lower = upper
+            diag[p, r] = total
+            w = mask / total
+            weight[p, r] = w
+            first[p, r] = w * source[p, r]
         return carry
 
     lax.fori_loop(1, PLANES - 1, start, 0, unroll=True)
 
+    def image(field, p):
+        v = [field[p, r] for r in range(4)]
+        along = [fz[p, r] * v[r] for r in range(4)]
+        below = [jnp.where(lane == 0, 0.0, lane_roll(along[3], 1))] + along[:3]
+        above = v[1:] + [jnp.where(lane == LANES - 1, 0.0, lane_roll(v[0], -1))]
+        sums = []
+        for r in range(4):
+            fy_here = fy[p, r]
+            total = fx[p, r] * field[p + 1, r] + fx[p - 1, r] * field[p - 1, r]
+            total = total + fy_here * row_roll(v[r], -1) + row_roll(fy_here * v[r], 1)
+            sums.append(total + (below[r] + fz[p, r] * above[r]))
+        return v, sums
+
     def sweep(p, carry):
-        v = first[p]
-        image = fine_sum(fx[p], fx[p - 1], fy[p], fz[p], first[p + 1], first[p - 1], v)
-        second[p] = KEEP * v + weight[p] * (source[p] + image)
+        v, sums = image(first, p)
+        for r in range(4):
+            second[p, r] = KEEP * v[r] + weight[p, r] * (source[p, r] + sums[r])
         return carry
 
     lax.fori_loop(2, PLANES - 2, sweep, 0, unroll=True)
@@ -216,9 +220,8 @@
         return jnp.stack([value[0] + value[1], value[2] + value[3]])
 
     def residual(p):
-        v = second[p]
-        image = fine_sum(fx[p], fx[p - 1], fy[p], fz[p], second[p + 1], second[p - 1], v)
-        return source[p] - diag[p] * v + image
+        v, sums = image(second, p)
+        return jnp.stack([source[p, r] - diag[p, r] * v[r] + sums[r] for r in range(4)])
 
     def coarse_face(k, carry):
         fxm[k] = both_rows(halves(fx[2 + 2 * k]), 1)
@@ -250,8 +253,8 @@
 
     def middle_sweep(k, carry):
         v = firstm[k]
-        image = middle_sum(fxm[k], fxm[k - 1], fym[k], fzm[k], firstm[k + 1], firstm[k - 1], v)
-        secondm[k] = KEEP * v + weightm[k] * (sourcem[k] + image)
+        near = middle_sum(fxm[k], fxm[k - 1], fym[k], fzm[k], firstm[k + 1], firstm[k - 1], v)
+        secondm[k] = KEEP * v + weightm[k] * (sourcem[k] + near)
         return carry
 
     lax.fori_loop(2, 6, middle_sweep, 0, unroll=True)
@@ -259,8 +262,8 @@
     coarse_source = jnp.zeros((ROWS, LANES), F32)
     for k in (3, 4):
         v = secondm[k]
-        image = middle_sum(fxm[k], fxm[k - 1], fym[k], fzm[k], secondm[k + 1], secondm[k - 1], v)
-        left = sourcem[k] - diagm[k] * v + image
+        near = middle_sum(fxm[k], fxm[k - 1], fym[k], fzm[k], secondm[k + 1], secondm[k - 1], v)
+        left = sourcem[k] - diagm[k] * v + near
         coarse_source = coarse_source + left[0] + left[1]
     coarse_source = both_rows(coarse_source, 2)
 

time: 88.5 us -> 88.1 us (level)
  no operation moved by 1% of the time
where the time goes in v6:
time: 88.1 us; the launch traced here: 87.6 us
  starting transfers between devices  44.7 us (51%)
  waiting for transfers between devices  22.4 us (25%)
  blocking collectives  11.5 us (13%)
  Pallas kernels  8.72 us (10%)
    ppermute x6, starting transfers between devices, shifted(): return lax.ppermute(value, axis, pairs)  18.5 us
    all_to_all x1, starting transfers between devices, shards(): rows = lax.all_to_all(chunk, GY, 0, 0, tiled=True)  13.7 us
    all_to_all x1, blocking collectives, shards(): planes = lax.all_to_all(planes, 'xa', 0, 0, tiled=True)  11.5 us
    ppermute x2, starting transfers between devices, swapped(): return lax.ppermute(value, 'ca', [(0, 1), (1, 0)])  9.93 us
    pallas_call x5, Pallas kernels, call(): pl.pallas_call(kernel, in_specs=specs, out_specs=[VMEM] * len(outs), out_...  8.72 us
    ppermute x6, waiting for transfers between devices, shifted(): return lax.ppermute(value, axis, pairs)  7.78 us
    ppermute x2, waiting for transfers between devices, parted(): return lax.ppermute(value, ('ya', 'ca'), pairs)  6.23 us
    all_to_all x1, waiting for transfers between devices, shards(): rows = lax.all_to_all(chunk, GY, 0, 0, tiled=True)  6.1 us
  transfers between devices with their start and end apart: 11, of which 7 were waited for; matrix products, arithmetic and copies ran while one was open for 0% of the time, Pallas kernels for 0%

profile of v6, /device:TPU:1, one launch (start us, length us, event | category | flops | bytes accessed | tf_op | source)
XLA Modules:
  0.0 87.6 jit_solution(17263695274439697620)
XLA Ops:
  0.0 1.2 %shard_map.37 = (f32[4,2,4,8,128]{4,3,2,1,0:T(8,128)S(1)}, f32[8,128]{1,0:T(8,128)S(1)}) custom-call(f32[3]{0:T(128)} %table_hbm.1, s32[4,8,512]{2,1,0:T(8,128)} %labels_hbm.1, f32[4,8,512]{2,1,0:T(8,128)} %source_hbm.1), custom_call_target="tpu_custom_call" | custom-call | tf_op jit(solution)/shard_map/pallas_call | solution.py:512
  1.2 8.8 %collective-permute-start.1 = (f32[4,2,4,8,128]{4,3,2,1,0:T(8,128)S(1)}, f32[4,2,4,8,128]{4,3,2,1,0:T(8,128)S(1)}, u32[]{:S(2)}, u32[]{:S(2)}) collective-permute-start(f32[4,2,4,8,128]{4,3,2,1,0:T(8,128)S(1)} %get-tuple-element.30.own_ref), channel_id=1, source_target_pairs={{1,0},{2,1},{3,2},{4,3},{5,4},{6,5},{7,6},{8,7},{9,8},{10,9},{11,1... | collective-permute-start | bytes 393224 | tf_op jit(solution)/shard_map/ppermute | solution.py:528
  10.0 1.9 %collective-permute-start = (f32[4,2,4,8,128]{4,3,2,1,0:T(8,128)S(1)}, f32[4,2,4,8,128]{4,3,2,1,0:T(8,128)S(1)}, u32[]{:S(2)}, u32[]{:S(2)}) collective-permute-start(f32[4,2,4,8,128]{4,3,2,1,0:T(8,128)S(1)} %get-tuple-element.30.own_ref), channel_id=1, source_target_pairs={{0,1},{1,2},{2,3},{3,4},{4,5},{5,6},{6,7},{7,8},{8,9},{9,10},{10,1... | collective-permute-start | bytes 393224 | tf_op jit(solution)/shard_map/ppermute | solution.py:528
  11.9 0.0 collective-permute-done.1.high_ref
  11.9 1.9 %collective-permute-done.low_ref = f32[4,2,4,8,128]{4,3,2,1,0:T(8,128)S(1)} collective-permute-done((f32[4,2,4,8,128]{4,3,2,1,0:T(8,128)S(1)}, f32[4,2,4,8,128]{4,3,2,1,0:T(8,128)S(1)}, u32[]{:S(2)}, u32[]{:S(2)}) %collective-permute-start) | collective-permute-done | bytes 131104 | tf_op jit(solution)/shard_map/ppermute | solution.py:528
  13.8 0.1 shard_map.38
  13.9 1.3 %collective-permute-start.3 = (f32[4,128,128]{2,1,0:T(8,128)S(1)}, f32[4,128,128]{2,1,0:T(8,128)S(1)}, u32[]{:S(2)}, u32[]{:S(2)}) collective-permute-start(f32[4,128,128]{2,1,0:T(8,128)S(1)} %get-tuple-element.32), channel_id=1, source_target_pairs={{0,16},{16,32},{32,48},{48,64},{64,80},{80,96},{96,112},{112,128},... | collective-permute-start | bytes 786440 | tf_op jit(solution)/shard_map/ppermute | solution.py:528
  15.2 1.3 %collective-permute-start.4 = (f32[4,128,128]{2,1,0:T(8,128)S(1)}, f32[4,128,128]{2,1,0:T(8,128)S(1)}, u32[]{:S(2)}, u32[]{:S(2)}) collective-permute-start(f32[4,128,128]{2,1,0:T(8,128)S(1)} %get-tuple-element.34), channel_id=1, source_target_pairs={{16,0},{32,16},{48,32},{64,48},{80,64},{96,80},{112,96},{128,112},... | collective-permute-start | bytes 786440 | tf_op jit(solution)/shard_map/ppermute | solution.py:528
  16.5 3.9 %collective-permute-start.2 = (f32[4,48,128]{2,1,0:T(8,128)S(1)}, f32[4,48,128]{2,1,0:T(8,128)S(1)}, u32[]{:S(2)}, u32[]{:S(2)}) collective-permute-start(f32[4,48,128]{2,1,0:T(8,128)S(1)} %get-tuple-element.31), channel_id=1, source_target_pairs={{0,32},{16,48},{32,64},{48,80},{64,96},{80,112},{96,128},{112,144}... | collective-permute-start | bytes 294920 | tf_op jit(solution)/shard_map/ppermute | solution.py:528
  20.5 1.3 %collective-permute-start.5 = (f32[4,48,128]{2,1,0:T(8,128)S(1)}, f32[4,48,128]{2,1,0:T(8,128)S(1)}, u32[]{:S(2)}, u32[]{:S(2)}) collective-permute-start(f32[4,48,128]{2,1,0:T(8,128)S(1)} %get-tuple-element.35), channel_id=1, source_target_pairs={{32,0},{48,16},{64,32},{80,48},{96,64},{112,80},{128,96},{144,112}... | collective-permute-start | bytes 294920 | tf_op jit(solution)/shard_map/ppermute | solution.py:528
  21.8 0.1 stack.19.spot_ref
  21.9 1.3 %collective-permute-done.2.low2_ref = f32[4,48,128]{2,1,0:T(8,128)S(1)} collective-permute-done((f32[4,48,128]{2,1,0:T(8,128)S(1)}, f32[4,48,128]{2,1,0:T(8,128)S(1)}, u32[]{:S(2)}, u32[]{:S(2)}) %collective-permute-start.2) | collective-permute-done | bytes 98336 | tf_op jit(solution)/shard_map/ppermute | solution.py:528
  23.1 4.6 %collective-permute-done.5.high2_ref = f32[4,48,128]{2,1,0:T(8,128)S(1)} collective-permute-done((f32[4,48,128]{2,1,0:T(8,128)S(1)}, f32[4,48,128]{2,1,0:T(8,128)S(1)}, u32[]{:S(2)}, u32[]{:S(2)}) %collective-permute-start.5) | collective-permute-done | bytes 98336 | tf_op jit(solution)/shard_map/ppermute | solution.py:528
  27.7 0.0 collective-permute-done.3.low1_ref
  27.7 0.0 collective-permute-done.4.high1_ref
  27.7 4.6 %shard_map.39 = (f32[16,16,128]{2,1,0:T(8,128)}, f32[2,16,128]{2,1,0:T(8,128)S(1)}, f32[5,4,8,128]{3,2,1,0:T(8,128)S(1)}, f32[4,4,24,128]{3,2,1,0:T(8,128)S(1)},...) custom-call(s32[6]{0:T(128)S(1)} %stack.19.spot_ref, ...), custom_call_target="tpu_custom_call" | custom-call | tf_op jit(solution)/shard_map/pallas_call | solution.py:512
  32.4 13.7 %all-to-all-start = ((f32[16,16,128]{2,1,0:T(8,128)}), f32[16,16,128]{2,1,0:T(8,128)S(1)}, u32[]{:S(2)}, u32[]{:S(2)}) async-start(f32[16,16,128]{2,1,0:T(8,128)} %get-tuple-element.36), calls=%async_computation | async-start | bytes 262144 | tf_op jit(solution)/shard_map/all_to_all | solution.py:596
  46.0 2.0 %collective-permute-start.6 = (f32[2,16,128]{2,1,0:T(8,128)S(1)}, f32[2,16,128]{2,1,0:T(8,128)S(1)}, u32[]{:S(2)}, u32[]{:S(2)}) collective-permute-start(f32[2,16,128]{2,1,0:T(8,128)S(1)} %get-tuple-element.37.ends_ref), channel_id=1, source_target_pairs={{0,1},{1,0},{2,3},{3,2},{4,5},{5,4},{6,7},{7,6},{8,9},{9,8},{10,11... | collective-permute-start | bytes 49160 | tf_op jit(solution)/shard_map/ppermute | solution.py:540
  48.1 1.0 %collective-permute-done.6.other_ref = f32[2,16,128]{2,1,0:T(8,128)S(1)} collective-permute-done((f32[2,16,128]{2,1,0:T(8,128)S(1)}, f32[2,16,128]{2,1,0:T(8,128)S(1)}, u32[]{:S(2)}, u32[]{:S(2)}) %collective-permute-start.6) | collective-permute-done | bytes 16416 | tf_op jit(solution)/shard_map/ppermute | solution.py:540
  49.1 6.1 %all-to-all-done.got_ref.rows_ref = f32[16,16,128]{2,1,0:T(8,128)S(1)} async-done(((f32[16,16,128]{2,1,0:T(8,128)}), f32[16,16,128]{2,1,0:T(8,128)S(1)}, u32[]{:S(2)}, u32[]{:S(2)}) %all-to-all-start) | async-done | bytes 131104 | tf_op jit(solution)/shard_map/all_to_all | solution.py:596
  55.2 0.6 shard_map.40
  55.8 11.5 %all_to_all.10.mid_ref = f32[4,112,128]{2,1,0:T(8,128)S(1)} all-to-all(f32[4,112,128]{2,1,0:T(8,128)S(1)} %shard_map.40), channel_id=1, replica_groups=mesh['ya'=8,'xa'=4,'za'=8,'ca'=2] {'xa'}, dimensions={0} | all-to-all | bytes 458752 | tf_op jit(solution)/shard_map/all_to_all | solution.py:602
  67.3 1.3 %collective-permute-start.7 = (f32[4,112,128]{2,1,0:T(8,128)S(1)}, f32[4,112,128]{2,1,0:T(8,128)S(1)}, u32[]{:S(2)}, u32[]{:S(2)}) collective-permute-start(f32[4,112,128]{2,1,0:T(8,128)S(1)} %all_to_all.10.mid_ref), channel_id=1, source_target_pairs={{0,64},{65,1},{64,128},{129,65},{128,192},{193,129},{192,256},{257... | collective-permute-start | bytes 688136 | tf_op jit(solution)/shard_map/ppermute | solution.py:536
  68.6 1.3 %collective-permute-start.8 = (f32[4,48,128]{2,1,0:T(8,128)S(1)}, f32[4,48,128]{2,1,0:T(8,128)S(1)}, u32[]{:S(2)}, u32[]{:S(2)}) collective-permute-start(f32[4,48,128]{2,1,0:T(8,128)S(1)} %slice.4), channel_id=1, source_target_pairs={{0,128},{129,1},{64,192},{193,65},{128,256},{257,129},{192,320},{3... | collective-permute-start | bytes 294920 | tf_op jit(solution)/shard_map/ppermute | solution.py:536
  69.9 6.2 %collective-permute-done.8.took2_ref = f32[4,48,128]{2,1,0:T(8,128)S(1)} collective-permute-done((f32[4,48,128]{2,1,0:T(8,128)S(1)}, f32[4,48,128]{2,1,0:T(8,128)S(1)}, u32[]{:S(2)}, u32[]{:S(2)}) %collective-permute-start.8) | collective-permute-done | bytes 98336 | tf_op jit(solution)/shard_map/ppermute | solution.py:536
  76.1 0.0 collective-permute-done.7.took1_ref
  76.2 7.9 %collective-permute-start.9 = (f32[4,160,128]{2,1,0:T(8,128)S(1)}, f32[4,160,128]{2,1,0:T(8,128)S(1)}, u32[]{:S(2)}, u32[]{:S(2)}) collective-permute-start(f32[4,160,128]{2,1,0:T(8,128)S(1)} %pad_maximum_fusion), channel_id=1, source_target_pairs={{0,1},{1,0},{2,3},{3,2},{4,5},{5,4},{6,7},{7,6},{8,9},{9,8},{10,11... | collective-permute-start | bytes 983048 | tf_op jit(solution)/shard_map/ppermute | solution.py:540
  84.1 1.2 %collective-permute-done.9.gave_ref = f32[4,160,128]{2,1,0:T(8,128)S(1)} collective-permute-done((f32[4,160,128]{2,1,0:T(8,128)S(1)}, f32[4,160,128]{2,1,0:T(8,128)S(1)}, u32[]{:S(2)}, u32[]{:S(2)}) %collective-permute-start.9) | collective-permute-done | bytes 327712 | tf_op jit(solution)/shard_map/ppermute | solution.py:540
  85.3 2.2 %shard_map.41 = f32[4,8,512]{2,1,0:T(8,128)} custom-call(s32[6]{0:T(128)S(1)} %stack.19.spot_ref, f32[4,112,128]{2,1,0:T(8,128)S(1)} %collective-permute-done.7.took1_ref, f32[4,48,128]{2,1,0:T(8,128)S(1)} %collective-permute-done.8.took2_ref, f32[4,112,128]{2,1,0:T(8,128)S(1)} %all_to_all.10.mid_ref, f32[4,160,128]{2,1,0:T(8,128)S(1)} %collective-permute-done.9.gave_ref, ...), custom_call_target="tpu_custom_call" | custom-call | tf_op jit(solution)/shard_map/pallas_call | solution.py:512
  (2 shorter events, 0.0 us)
Async XLA Ops:
  1.2 10.7 %collective-permute-start.1 = (f32[4,2,4,8,128]{4,3,2,1,0:T(8,128)S(1)}, f32[4,2,4,8,128]{4,3,2,1,0:T(8,128)S(1)}, u32[]{:S(2)}, u32[]{:S(2)}) collective-permute-start(f32[4,2,4,8,128]{4,3,2,1,0:T(8,128)S(1)} %get-tuple-element.30.own_ref), channel_id=1, source_target_pairs={{1,0},{2,1},{3,2},{4,3},{5,4},{6,5},{7,6},{8,7},{9,8},{10,9},{11,1... | collective-permute-start | bytes 393224 | tf_op jit(solution)/shard_map/ppermute | solution.py:528
  10.0 3.9 %collective-permute-start = (f32[4,2,4,8,128]{4,3,2,1,0:T(8,128)S(1)}, f32[4,2,4,8,128]{4,3,2,1,0:T(8,128)S(1)}, u32[]{:S(2)}, u32[]{:S(2)}) collective-permute-start(f32[4,2,4,8,128]{4,3,2,1,0:T(8,128)S(1)} %get-tuple-element.30.own_ref), channel_id=1, source_target_pairs={{0,1},{1,2},{2,3},{3,4},{4,5},{5,6},{6,7},{7,8},{8,9},{9,10},{10,1... | collective-permute-start | bytes 393224 | tf_op jit(solution)/shard_map/ppermute | solution.py:528
  13.9 13.8 %collective-permute-start.3 = (f32[4,128,128]{2,1,0:T(8,128)S(1)}, f32[4,128,128]{2,1,0:T(8,128)S(1)}, u32[]{:S(2)}, u32[]{:S(2)}) collective-permute-start(f32[4,128,128]{2,1,0:T(8,128)S(1)} %get-tuple-element.32), channel_id=1, source_target_pairs={{0,16},{16,32},{32,48},{48,64},{64,80},{80,96},{96,112},{112,128},... | collective-permute-start | bytes 786440 | tf_op jit(solution)/shard_map/ppermute | solution.py:528
  15.2 12.5 %collective-permute-start.4 = (f32[4,128,128]{2,1,0:T(8,128)S(1)}, f32[4,128,128]{2,1,0:T(8,128)S(1)}, u32[]{:S(2)}, u32[]{:S(2)}) collective-permute-start(f32[4,128,128]{2,1,0:T(8,128)S(1)} %get-tuple-element.34), channel_id=1, source_target_pairs={{16,0},{32,16},{48,32},{64,48},{80,64},{96,80},{112,96},{128,112},... | collective-permute-start | bytes 786440 | tf_op jit(solution)/shard_map/ppermute | solution.py:528
  16.5 6.6 %collective-permute-start.2 = (f32[4,48,128]{2,1,0:T(8,128)S(1)}, f32[4,48,128]{2,1,0:T(8,128)S(1)}, u32[]{:S(2)}, u32[]{:S(2)}) collective-permute-start(f32[4,48,128]{2,1,0:T(8,128)S(1)} %get-tuple-element.31), channel_id=1, source_target_pairs={{0,32},{16,48},{32,64},{48,80},{64,96},{80,112},{96,128},{112,144}... | collective-permute-start | bytes 294920 | tf_op jit(solution)/shard_map/ppermute | solution.py:528
  20.5 7.3 %collective-permute-start.5 = (f32[4,48,128]{2,1,0:T(8,128)S(1)}, f32[4,48,128]{2,1,0:T(8,128)S(1)}, u32[]{:S(2)}, u32[]{:S(2)}) collective-permute-start(f32[4,48,128]{2,1,0:T(8,128)S(1)} %get-tuple-element.35), channel_id=1, source_target_pairs={{32,0},{48,16},{64,32},{80,48},{96,64},{112,80},{128,96},{144,112}... | collective-permute-start | bytes 294920 | tf_op jit(solution)/shard_map/ppermute | solution.py:528
  32.4 22.9 %all-to-all-start = ((f32[16,16,128]{2,1,0:T(8,128)}), f32[16,16,128]{2,1,0:T(8,128)S(1)}, u32[]{:S(2)}, u32[]{:S(2)}) async-start(f32[16,16,128]{2,1,0:T(8,128)} %get-tuple-element.36), calls=%async_computation | async-start | bytes 262144 | tf_op jit(solution)/shard_map/all_to_all | solution.py:596
  46.0 3.1 %collective-permute-start.6 = (f32[2,16,128]{2,1,0:T(8,128)S(1)}, f32[2,16,128]{2,1,0:T(8,128)S(1)}, u32[]{:S(2)}, u32[]{:S(2)}) collective-permute-start(f32[2,16,128]{2,1,0:T(8,128)S(1)} %get-tuple-element.37.ends_ref), channel_id=1, source_target_pairs={{0,1},{1,0},{2,3},{3,2},{4,5},{5,4},{6,7},{7,6},{8,9},{9,8},{10,11... | collective-permute-start | bytes 49160 | tf_op jit(solution)/shard_map/ppermute | solution.py:540
  67.3 8.8 %collective-permute-start.7 = (f32[4,112,128]{2,1,0:T(8,128)S(1)}, f32[4,112,128]{2,1,0:T(8,128)S(1)}, u32[]{:S(2)}, u32[]{:S(2)}) collective-permute-start(f32[4,112,128]{2,1,0:T(8,128)S(1)} %all_to_all.10.mid_ref), channel_id=1, source_target_pairs={{0,64},{65,1},{64,128},{129,65},{128,192},{193,129},{192,256},{257... | collective-permute-start | bytes 688136 | tf_op jit(solution)/shard_map/ppermute | solution.py:536
  68.6 7.5 %collective-permute-start.8 = (f32[4,48,128]{2,1,0:T(8,128)S(1)}, f32[4,48,128]{2,1,0:T(8,128)S(1)}, u32[]{:S(2)}, u32[]{:S(2)}) collective-permute-start(f32[4,48,128]{2,1,0:T(8,128)S(1)} %slice.4), channel_id=1, source_target_pairs={{0,128},{129,1},{64,192},{193,65},{128,256},{257,129},{192,320},{3... | collective-permute-start | bytes 294920 | tf_op jit(solution)/shard_map/ppermute | solution.py:536
  76.2 9.2 %collective-permute-start.9 = (f32[4,160,128]{2,1,0:T(8,128)S(1)}, f32[4,160,128]{2,1,0:T(8,128)S(1)}, u32[]{:S(2)}, u32[]{:S(2)}) collective-permute-start(f32[4,160,128]{2,1,0:T(8,128)S(1)} %pad_maximum_fusion), channel_id=1, source_target_pairs={{0,1},{1,0},{2,3},{3,2},{4,5},{5,4},{6,7},{7,6},{8,9},{9,8},{10,11... | collective-permute-start | bytes 983048 | tf_op jit(solution)/shard_map/ppermute | solution.py:540

commit v7 on v6

--- a/solution.py
+++ b/solution.py
@@ -125,7 +125,7 @@
 
 def up_kernel(
     spot_ref, pairs_ref, low2_ref, low1_ref, own_ref, high1_ref, high2_ref,
-    chunk_ref, ends_ref, fx_out, fy_out, fz_out, w_out, s_out, v_out,
+    chunk_ref, ends_ref, edge_ref, fx_out, fy_out, fz_out, w_out, s_out, v_out,
     fxm_out, fym_out, fzm_out, wm_out, sm_out, vm_out, root_out,
     code, source, fx, fy, fz, zlow, diag, weight, first, second,
     fxm, fym, fzm, zlowm, diagm, weightm, sourcem, firstm, secondm,
@@ -136,8 +136,13 @@
     ny = 8 * spot_ref[3]
     table = pairs_ref[...]
     blank = jnp.zeros((4, ROWS, LANES), F32)
+
+    def in_grid(value, row):
+        y = y0 - 8 + row + iota(value.shape, value.ndim - 2)
+        return jnp.where((y >= 0) & (y < ny), value.astype(jnp.int32), 0)
+
     for k in range(4):
-        code[REACH + k] = own_ref[k, 0].astype(jnp.int32)
+        code[REACH + k] = in_grid(own_ref[k, 0], 0)
         source[REACH + k] = own_ref[k, 1]
     for distance in range(1, REACH + 1):
         for p in (REACH - distance, REACH + 3 + distance):
@@ -149,7 +154,7 @@
                 for residue in range(4):
                     value = ref[residue, pl.ds(offset, rows)]
                     if which == 0:
-                        code[p, residue, pl.ds(row, rows)] = value.astype(jnp.int32)
+                        code[p, residue, pl.ds(row, rows)] = in_grid(value, row)
                     else:
                         source[p, residue, pl.ds(row, rows)] = value
 
@@ -295,18 +300,27 @@
     for value in (OMEGA * root * coarse_source, cx, cy, cz):
         lines.append(value[8:9])
         lines.append(value[12:13])
-    for at_row in (10, 12):
-        for k in (3, 4):
-            for half in range(2):
-                lines.append(secondm[k, half, at_row : at_row + 1])
     chunk = jnp.concatenate(lines, axis=0)
     for peer in range(chunk_ref.shape[0]):
         chunk_ref[peer] = chunk
+    first_core = spot_ref[5] == 0
+
+    def edges(sibling):
+        rows = []
+        for k in (3, 4):
+            for half in range(2):
+                low = secondm[k, half, 10:11]
+                high = secondm[k, half, 12:13]
+                rows.append(jnp.where(first_core == sibling, high, low))
+        return rows
+
+    edge_ref[...] = jnp.concatenate(edges(False) + [jnp.zeros((4, LANES), F32)], axis=0)
+    inside_chip = edges(True)
     for k, other in ((3, 4), (4, 3)):
         lines = [secondm[k, half, 8 + 2 * m : 9 + 2 * m] for half in range(2) for m in range(4)]
         lines += [secondm[other, half, at_row : at_row + 1] for at_row in (6, 16) for half in range(2)]
         lines += [root[at_row : at_row + 1] for at_row in (4, 16)]
-        lines += [jnp.zeros((2, LANES), F32)]
+        lines += inside_chip[2 * (k - 3) : 2 * (k - 2)]
         ends_ref[k - 3] = jnp.concatenate(lines, axis=0)
 
     own_rows = pl.ds(8, 8)
@@ -356,14 +370,12 @@
 
 
 def down_kernel(
-    spot_ref, took1_ref, took2_ref, mid_ref, gave_ref, rows_ref, fx, fy, fz, w, s, v2,
+    spot_ref, took1_ref, took2_ref, mid_ref, gave_ref, other_ref, edge_ref, fx, fy, fz, w, s, v2,
     fxm, fym, fzm, wm, sm, vm, root,
     out_ref,
     parts, state, ends, field, third, total,
 ):
-    mine_y = spot_ref[1]
     place = spot_ref[4]
-    count_y = rows_ref.shape[0]
     width = 2 * WINDOW + 1
     lane = iota((ROWS, LANES), 1)
     row = iota((ROWS, LANES), 0)
@@ -453,16 +465,14 @@
     field[5] = line_block(place + WINDOW + 1) + spread[2]
     field[1] = corners(vm[0], place + WINDOW - 1) + spread[0]
     field[4] = corners(vm[3], place + WINDOW + 1) + spread[2]
-    left = jnp.where(mine_y > 0, 1.0, 0.0).astype(F32)
-    right = jnp.where(mine_y < count_y - 1, 1.0, 0.0).astype(F32)
-    left_spot = jnp.maximum(mine_y - 1, 0)
-    right_spot = jnp.minimum(mine_y + 1, count_y - 1)
     for k in range(2):
         halves = []
         for half in range(2):
             value = vm[1 + k, half]
-            lower = rows_ref[left_spot, pl.ds(12 + 2 * k + half, 1)] * left
-            upper = rows_ref[right_spot, pl.ds(8 + 2 * k + half, 1)] * right
+            sibling = other_ref[k, pl.ds(14 + half, 1)]
+            beyond = edge_ref[pl.ds(2 * k + half, 1)]
+            lower = jnp.where(lower_core, beyond, sibling)
+            upper = jnp.where(lower_core, sibling, beyond)
             halves.append(swap_rows(swap_rows(value, lower, 4, 6), upper, 18, 20))
         field[2 + k] = jnp.stack(halves) + spread[1]
 
@@ -536,6 +546,14 @@
     return lax.ppermute(value, ("ya", "ca"), pairs)
 
 
+def shifted_chip(value):
+    pairs = []
+    for i in range(lax.axis_size("za") - 1):
+        pairs.append((2 * i + 1, 2 * i + 2))
+        pairs.append((2 * i + 2, 2 * i + 1))
+    return lax.ppermute(value, GY, pairs)
+
+
 def swapped(value):
     return lax.ppermute(value, "ca", [(0, 1), (1, 0)])
 
@@ -562,8 +580,9 @@
         ],
         *(pltpu.with_memory_space_constraint(value, pltpu.HBM) for value in (conduct_table, labels, right_side)),
     )
-    low = shifted(own, GY, 1)
-    high = shifted(own, GY, -1)
+    ring = [(i, (i + 1) % ny) for i in range(ny)]
+    low = lax.ppermute(own, GY, ring)
+    high = lax.ppermute(own, GY, [(b, a) for a, b in ring])
     near = (4, NEAR_ROWS, LANES)
     far = (4, FAR_ROWS, LANES)
     wide, up1, down1, up2, down2 = call(
@@ -578,7 +597,7 @@
         up_kernel,
         [SMEM] + [VMEM] * 6,
         [
-            (ny, 16, LANES), (2, 16, LANES),
+            (ny, 8, LANES), (2, 16, LANES), (8, LANES),
             (5,) + tile, (4,) + fine, (4,) + tile, (4,) + tile, (4,) + tile, (6,) + fine,
             (5,) + mid, (4,) + mid, (4,) + mid, (4,) + mid, (4,) + mid, (4,) + mid,
             (3, ROWS, LANES),
@@ -592,7 +611,7 @@
         + [room(8, *mid)] * 5,
         spot, pairs, low2, low1, wide, high1, high2,
     )
-    chunk, ends = outs[:2]
+    chunk, ends, edge = outs[:3]
     rows = lax.all_to_all(chunk, GY, 0, 0, tiled=True)
     other = swapped(ends)
     window = (block, 4 * SPAN + 32, LANES)
@@ -603,17 +622,18 @@
     planes, middle_rows = lax.optimization_barrier((planes, planes[:, : 4 * CORE]))
     took1 = parted(planes, 1)
     took2 = parted(middle_rows, 2)
+    took1, took2, edge = lax.optimization_barrier((took1, took2, shifted_chip(edge)))
     gave = swapped(jnp.concatenate([took1, took2], axis=1))
     blocks = [took1, took2, planes, gave]
     (correction,) = call(
         down_kernel,
-        [SMEM] + [VMEM] * 18,
+        [SMEM] + [VMEM] * 19,
         [(4, 8, 4 * LANES)],
         [
             room(4, 5 * block, ROWS, LANES), room(2, 5 * block, ROWS, LANES), room(5 * block, 16, LANES),
             room(6, *mid), room(4, *mid), room(6, *fine),
         ],
-        spot, *blocks, rows, *outs[2:],
+        spot, *blocks, other, edge, *outs[3:],
     )
     return correction
 

time: 88.1 us -> 85.8 us (0.974)
  waiting for transfers between devices: 22.4 us -> 18.4 us
  starting transfers between devices: 44.7 us -> 47.1 us
    ppermute x0 -> x3, starting transfers between devices: none -> 19.5 us  [the longest x1 12.6 us: shifted_chip(): return lax.ppermute(value, GY, pairs)]
    ppermute x6 -> x4, starting transfers between devices: 18.5 us -> 11.2 us  [shifted(): return lax.ppermute(value, axis, pairs)]
    ppermute x2, waiting for transfers between devices: 6.23 us -> 0.01 us  [parted(): return lax.ppermute(value, ('ya', 'ca'), pairs)]
    ppermute x2, starting transfers between devices: 9.93 us -> 4.05 us  [swapped(): return lax.ppermute(value, 'ca', [(0, 1), (1, 0)])]
    ppermute x0 -> x3, waiting for transfers between devices: none -> 5.22 us  [the longest x1 2.96 us: shards(): low = lax.ppermute(own, GY, ring)]
    all_to_all x1, starting transfers between devices: 13.7 us -> 9.76 us  [shards(): rows = lax.all_to_all(chunk, GY, 0, 0, tiled=True)]
    ppermute x6 -> x4, waiting for transfers between devices: 7.78 us -> 5.87 us  [shifted(): return lax.ppermute(value, axis, pairs)]
    all_to_all x1, waiting for transfers between devices: 6.1 us -> 4.77 us  [shards(): rows = lax.all_to_all(chunk, GY, 0, 0, tiled=True)]
  transfers between devices with their start and end apart: 11 -> 12, of which waited for: 7 -> 8; matrix products, arithmetic and copies ran while one was open for 0% -> 0% of each run, Pallas kernels for 0% -> 0%
where the time goes in v7:
time: 85.8 us; the launch traced here: 85.4 us
  starting transfers between devices  47.1 us (55%)
  waiting for transfers between devices  18.4 us (21%)
  blocking collectives  10.9 us (13%)
  Pallas kernels  8.72 us (10%)
    ppermute x1, starting transfers between devices, shifted_chip(): return lax.ppermute(value, GY, pairs)  12.6 us
    ppermute x4, starting transfers between devices, shifted(): return lax.ppermute(value, axis, pairs)  11.2 us
    all_to_all x1, blocking collectives, shards(): planes = lax.all_to_all(planes, 'xa', 0, 0, tiled=True)  10.9 us
    all_to_all x1, starting transfers between devices, shards(): rows = lax.all_to_all(chunk, GY, 0, 0, tiled=True)  9.76 us
    pallas_call x5, Pallas kernels, call(): pl.pallas_call(kernel, in_specs=specs, out_specs=[VMEM] * len(outs), out_...  8.72 us
    ppermute x1, starting transfers between devices, shards(): high = lax.ppermute(own, GY, [(b, a) for a, b in ring])  6.89 us
    ppermute x4, waiting for transfers between devices, shifted(): return lax.ppermute(value, axis, pairs)  5.87 us
    all_to_all x1, waiting for transfers between devices, shards(): rows = lax.all_to_all(chunk, GY, 0, 0, tiled=True)  4.77 us
  transfers between devices with their start and end apart: 12, of which 8 were waited for; matrix products, arithmetic and copies ran while one was open for 0% of the time, Pallas kernels for 0%

profile of v7, /device:TPU:1, one launch (start us, length us, event | category | flops | bytes accessed | tf_op | source)
XLA Modules:
  0.0 85.4 jit_solution(16580279648876675121)
XLA Ops:
  0.0 1.2 %shard_map.37 = (f32[4,2,4,8,128]{4,3,2,1,0:T(8,128)S(1)}, f32[8,128]{1,0:T(8,128)S(1)}) custom-call(f32[3]{0:T(128)} %table_hbm.1, s32[4,8,512]{2,1,0:T(8,128)} %labels_hbm.1, f32[4,8,512]{2,1,0:T(8,128)} %source_hbm.1), custom_call_target="tpu_custom_call" | custom-call | tf_op jit(solution)/shard_map/pallas_call | solution.py:522
  1.2 6.9 %collective-permute-start.1 = (f32[4,2,4,8,128]{4,3,2,1,0:T(8,128)S(1)}, f32[4,2,4,8,128]{4,3,2,1,0:T(8,128)S(1)}, u32[]{:S(2)}, u32[]{:S(2)}) collective-permute-start(f32[4,2,4,8,128]{4,3,2,1,0:T(8,128)S(1)} %get-tuple-element.34.own_ref), channel_id=1, source_target_pairs={{1,0},{2,1},{3,2},{4,3},{5,4},{6,5},{7,6},{8,7},{9,8},{10,9},{11,1... | collective-permute-start | bytes 393224 | tf_op jit(solution)/shard_map/ppermute | solution.py:585
  8.1 0.0 collective-permute-start
  8.1 1.0 %collective-permute-done.1.high_ref = f32[4,2,4,8,128]{4,3,2,1,0:T(8,128)S(1)} collective-permute-done((f32[4,2,4,8,128]{4,3,2,1,0:T(8,128)S(1)}, f32[4,2,4,8,128]{4,3,2,1,0:T(8,128)S(1)}, u32[]{:S(2)}, u32[]{:S(2)}) %collective-permute-start.1) | collective-permute-done | bytes 131104 | tf_op jit(solution)/shard_map/ppermute | solution.py:585
  9.1 3.0 %collective-permute-done.low_ref = f32[4,2,4,8,128]{4,3,2,1,0:T(8,128)S(1)} collective-permute-done((f32[4,2,4,8,128]{4,3,2,1,0:T(8,128)S(1)}, f32[4,2,4,8,128]{4,3,2,1,0:T(8,128)S(1)}, u32[]{:S(2)}, u32[]{:S(2)}) %collective-permute-start) | collective-permute-done | bytes 131104 | tf_op jit(solution)/shard_map/ppermute | solution.py:584
  12.0 0.1 shard_map.38
  12.1 3.1 %collective-permute-start.3 = (f32[4,128,128]{2,1,0:T(8,128)S(1)}, f32[4,128,128]{2,1,0:T(8,128)S(1)}, u32[]{:S(2)}, u32[]{:S(2)}) collective-permute-start(f32[4,128,128]{2,1,0:T(8,128)S(1)} %get-tuple-element.36), channel_id=1, source_target_pairs={{0,16},{16,32},{32,48},{48,64},{64,80},{80,96},{96,112},{112,128},... | collective-permute-start | bytes 786440 | tf_op jit(solution)/shard_map/ppermute | solution.py:538
  15.2 1.3 %collective-permute-start.4 = (f32[4,128,128]{2,1,0:T(8,128)S(1)}, f32[4,128,128]{2,1,0:T(8,128)S(1)}, u32[]{:S(2)}, u32[]{:S(2)}) collective-permute-start(f32[4,128,128]{2,1,0:T(8,128)S(1)} %get-tuple-element.38), channel_id=1, source_target_pairs={{16,0},{32,16},{48,32},{64,48},{80,64},{96,80},{112,96},{128,112},... | collective-permute-start | bytes 786440 | tf_op jit(solution)/shard_map/ppermute | solution.py:538
  16.5 5.5 %collective-permute-start.2 = (f32[4,48,128]{2,1,0:T(8,128)S(1)}, f32[4,48,128]{2,1,0:T(8,128)S(1)}, u32[]{:S(2)}, u32[]{:S(2)}) collective-permute-start(f32[4,48,128]{2,1,0:T(8,128)S(1)} %get-tuple-element.35), channel_id=1, source_target_pairs={{0,32},{16,48},{32,64},{48,80},{64,96},{80,112},{96,128},{112,144}... | collective-permute-start | bytes 294920 | tf_op jit(solution)/shard_map/ppermute | solution.py:538
  22.1 1.3 %collective-permute-start.5 = (f32[4,48,128]{2,1,0:T(8,128)S(1)}, f32[4,48,128]{2,1,0:T(8,128)S(1)}, u32[]{:S(2)}, u32[]{:S(2)}) collective-permute-start(f32[4,48,128]{2,1,0:T(8,128)S(1)} %get-tuple-element.39), channel_id=1, source_target_pairs={{32,0},{48,16},{64,32},{80,48},{96,64},{112,80},{128,96},{144,112}... | collective-permute-start | bytes 294920 | tf_op jit(solution)/shard_map/ppermute | solution.py:538
  23.4 0.1 stack.19.spot_ref
  23.5 1.3 %collective-permute-done.2.low2_ref = f32[4,48,128]{2,1,0:T(8,128)S(1)} collective-permute-done((f32[4,48,128]{2,1,0:T(8,128)S(1)}, f32[4,48,128]{2,1,0:T(8,128)S(1)}, u32[]{:S(2)}, u32[]{:S(2)}) %collective-permute-start.2) | collective-permute-done | bytes 98336 | tf_op jit(solution)/shard_map/ppermute | solution.py:538
  24.7 4.6 %collective-permute-done.5.high2_ref = f32[4,48,128]{2,1,0:T(8,128)S(1)} collective-permute-done((f32[4,48,128]{2,1,0:T(8,128)S(1)}, f32[4,48,128]{2,1,0:T(8,128)S(1)}, u32[]{:S(2)}, u32[]{:S(2)}) %collective-permute-start.5) | collective-permute-done | bytes 98336 | tf_op jit(solution)/shard_map/ppermute | solution.py:538
  29.3 0.0 collective-permute-done.3.low1_ref
  29.3 0.0 collective-permute-done.4.high1_ref
  29.3 4.6 %shard_map.39 = (f32[16,8,128]{2,1,0:T(8,128)}, f32[2,16,128]{2,1,0:T(8,128)S(1)}, f32[8,128]{1,0:T(8,128)S(1)}, f32[5,4,8,128]{3,2,1,0:T(8,128)S(1)}, f32[4,4,2...) custom-call(s32[6]{0:T(128)S(1)} %stack.19.spot_ref, ...), custom_call_target="tpu_custom_call" | custom-call | tf_op jit(solution)/shard_map/pallas_call | solution.py:522
  34.0 9.8 %all-to-all-start = ((f32[16,8,128]{2,1,0:T(8,128)}), f32[16,8,128]{2,1,0:T(8,128)S(1)}, u32[]{:S(2)}, u32[]{:S(2)}) async-start(f32[16,8,128]{2,1,0:T(8,128)} %get-tuple-element.40), calls=%async_computation | async-start | bytes 131072 | tf_op jit(solution)/shard_map/all_to_all | solution.py:615
  43.7 2.1 %collective-permute-start.6 = (f32[2,16,128]{2,1,0:T(8,128)S(1)}, f32[2,16,128]{2,1,0:T(8,128)S(1)}, u32[]{:S(2)}, u32[]{:S(2)}) collective-permute-start(f32[2,16,128]{2,1,0:T(8,128)S(1)} %get-tuple-element.41.ends_ref), channel_id=1, source_target_pairs={{0,1},{1,0},{2,3},{3,2},{4,5},{5,4},{6,7},{7,6},{8,9},{9,8},{10,11... | collective-permute-start | bytes 49160 | tf_op jit(solution)/shard_map/ppermute | solution.py:558
  45.8 0.9 %collective-permute-done.6.other_ref = f32[2,16,128]{2,1,0:T(8,128)S(1)} collective-permute-done((f32[2,16,128]{2,1,0:T(8,128)S(1)}, f32[2,16,128]{2,1,0:T(8,128)S(1)}, u32[]{:S(2)}, u32[]{:S(2)}) %collective-permute-start.6) | collective-permute-done | bytes 16416 | tf_op jit(solution)/shard_map/ppermute | solution.py:558
  46.8 4.8 %all-to-all-done.got_ref = f32[16,8,128]{2,1,0:T(8,128)S(1)} async-done(((f32[16,8,128]{2,1,0:T(8,128)}), f32[16,8,128]{2,1,0:T(8,128)S(1)}, u32[]{:S(2)}, u32[]{:S(2)}) %all-to-all-start) | async-done | bytes 65568 | tf_op jit(solution)/shard_map/all_to_all | solution.py:615
  51.6 0.6 shard_map.40
  52.2 10.9 %all_to_all.10.mid_ref = f32[4,112,128]{2,1,0:T(8,128)S(1)} all-to-all(f32[4,112,128]{2,1,0:T(8,128)S(1)} %shard_map.40), channel_id=1, replica_groups=mesh['ya'=8,'xa'=4,'za'=8,'ca'=2] {'xa'}, dimensions={0} | all-to-all | bytes 458752 | tf_op jit(solution)/shard_map/all_to_all | solution.py:621
  63.1 1.3 %collective-permute-start.7 = (f32[4,112,128]{2,1,0:T(8,128)S(1)}, f32[4,112,128]{2,1,0:T(8,128)S(1)}, u32[]{:S(2)}, u32[]{:S(2)}) collective-permute-start(f32[4,112,128]{2,1,0:T(8,128)S(1)} %all_to_all.10.mid_ref), channel_id=1, source_target_pairs={{0,64},{65,1},{64,128},{129,65},{128,192},{193,129},{192,256},{257... | collective-permute-start | bytes 688136 | tf_op jit(solution)/shard_map/ppermute | solution.py:546
  64.4 1.3 %collective-permute-start.8 = (f32[4,48,128]{2,1,0:T(8,128)S(1)}, f32[4,48,128]{2,1,0:T(8,128)S(1)}, u32[]{:S(2)}, u32[]{:S(2)}) collective-permute-start(f32[4,48,128]{2,1,0:T(8,128)S(1)} %slice.4), channel_id=1, source_target_pairs={{0,128},{129,1},{64,192},{193,65},{128,256},{257,129},{192,320},{3... | collective-permute-start | bytes 294920 | tf_op jit(solution)/shard_map/ppermute | solution.py:546
  65.7 12.6 %collective-permute-start.9 = (f32[8,128]{1,0:T(8,128)S(1)}, f32[8,128]{1,0:T(8,128)S(1)}, u32[]{:S(2)}, u32[]{:S(2)}) collective-permute-start(f32[8,128]{1,0:T(8,128)S(1)} %get-tuple-element.44), channel_id=1, source_target_pairs={{1,2},{2,1},{3,4},{4,3},{5,6},{6,5},{7,8},{8,7},{9,10},{10,9},{11,... | collective-permute-start | bytes 12296 | tf_op jit(solution)/shard_map/ppermute | solution.py:554
  78.3 1.3 %collective-permute-done.9.edge_ref = f32[8,128]{1,0:T(8,128)S(1)} collective-permute-done((f32[8,128]{1,0:T(8,128)S(1)}, f32[8,128]{1,0:T(8,128)S(1)}, u32[]{:S(2)}, u32[]{:S(2)}) %collective-permute-start.9) | collective-permute-done | bytes 4128 | tf_op jit(solution)/shard_map/ppermute | solution.py:554
  79.6 0.0 collective-permute-done.8.took2_ref
  79.6 0.0 collective-permute-done.7.took1_ref
  79.6 1.9 %collective-permute-start.10 = (f32[4,160,128]{2,1,0:T(8,128)S(1)}, f32[4,160,128]{2,1,0:T(8,128)S(1)}, u32[]{:S(2)}, u32[]{:S(2)}) collective-permute-start(f32[4,160,128]{2,1,0:T(8,128)S(1)} %pad_maximum_fusion), channel_id=1, source_target_pairs={{0,1},{1,0},{2,3},{3,2},{4,5},{5,4},{6,7},{7,6},{8,9},{9,8},{10,11... | collective-permute-start | bytes 983048 | tf_op jit(solution)/shard_map/ppermute | solution.py:558
  81.6 1.6 %collective-permute-done.10.gave_ref = f32[4,160,128]{2,1,0:T(8,128)S(1)} collective-permute-done((f32[4,160,128]{2,1,0:T(8,128)S(1)}, f32[4,160,128]{2,1,0:T(8,128)S(1)}, u32[]{:S(2)}, u32[]{:S(2)}) %collective-permute-start.10) | collective-permute-done | bytes 327712 | tf_op jit(solution)/shard_map/ppermute | solution.py:558
  83.1 2.2 %shard_map.41 = f32[4,8,512]{2,1,0:T(8,128)} custom-call(s32[6]{0:T(128)S(1)} %stack.19.spot_ref, f32[4,112,128]{2,1,0:T(8,128)S(1)} %collective-permute-done.7.took1_ref, f32[4,48,128]{2,1,0:T(8,128)S(1)} %collective-permute-done.8.took2_ref, f32[4,112,128]{2,1,0:T(8,128)S(1)} %all_to_all.10.mid_ref, f32[4,160,128]{2,1,0:T(8,128)S(1)} %collective-permute-done.10.gave_ref, ...), custom_call_target="tpu_custom_call" | custom-call | tf_op jit(solution)/shard_map/pallas_call | solution.py:522
  (2 shorter events, 0.0 us)
Async XLA Ops:
  1.2 7.9 %collective-permute-start.1 = (f32[4,2,4,8,128]{4,3,2,1,0:T(8,128)S(1)}, f32[4,2,4,8,128]{4,3,2,1,0:T(8,128)S(1)}, u32[]{:S(2)}, u32[]{:S(2)}) collective-permute-start(f32[4,2,4,8,128]{4,3,2,1,0:T(8,128)S(1)} %get-tuple-element.34.own_ref), channel_id=1, source_target_pairs={{1,0},{2,1},{3,2},{4,3},{5,4},{6,5},{7,6},{8,7},{9,8},{10,9},{11,1... | collective-permute-start | bytes 393224 | tf_op jit(solution)/shard_map/ppermute | solution.py:585
  8.1 3.9 %collective-permute-start = (f32[4,2,4,8,128]{4,3,2,1,0:T(8,128)S(1)}, f32[4,2,4,8,128]{4,3,2,1,0:T(8,128)S(1)}, u32[]{:S(2)}, u32[]{:S(2)}) collective-permute-start(f32[4,2,4,8,128]{4,3,2,1,0:T(8,128)S(1)} %get-tuple-element.34.own_ref), channel_id=1, source_target_pairs={{0,1},{1,2},{2,3},{3,4},{4,5},{5,6},{6,7},{7,8},{8,9},{9,10},{10,1... | collective-permute-start | bytes 393224 | tf_op jit(solution)/shard_map/ppermute | solution.py:584
  12.1 17.2 %collective-permute-start.3 = (f32[4,128,128]{2,1,0:T(8,128)S(1)}, f32[4,128,128]{2,1,0:T(8,128)S(1)}, u32[]{:S(2)}, u32[]{:S(2)}) collective-permute-start(f32[4,128,128]{2,1,0:T(8,128)S(1)} %get-tuple-element.36), channel_id=1, source_target_pairs={{0,16},{16,32},{32,48},{48,64},{64,80},{80,96},{96,112},{112,128},... | collective-permute-start | bytes 786440 | tf_op jit(solution)/shard_map/ppermute | solution.py:538
  15.2 14.1 %collective-permute-start.4 = (f32[4,128,128]{2,1,0:T(8,128)S(1)}, f32[4,128,128]{2,1,0:T(8,128)S(1)}, u32[]{:S(2)}, u32[]{:S(2)}) collective-permute-start(f32[4,128,128]{2,1,0:T(8,128)S(1)} %get-tuple-element.38), channel_id=1, source_target_pairs={{16,0},{32,16},{48,32},{64,48},{80,64},{96,80},{112,96},{128,112},... | collective-permute-start | bytes 786440 | tf_op jit(solution)/shard_map/ppermute | solution.py:538
  16.5 8.2 %collective-permute-start.2 = (f32[4,48,128]{2,1,0:T(8,128)S(1)}, f32[4,48,128]{2,1,0:T(8,128)S(1)}, u32[]{:S(2)}, u32[]{:S(2)}) collective-permute-start(f32[4,48,128]{2,1,0:T(8,128)S(1)} %get-tuple-element.35), channel_id=1, source_target_pairs={{0,32},{16,48},{32,64},{48,80},{64,96},{80,112},{96,128},{112,144}... | collective-permute-start | bytes 294920 | tf_op jit(solution)/shard_map/ppermute | solution.py:538
  22.1 7.3 %collective-permute-start.5 = (f32[4,48,128]{2,1,0:T(8,128)S(1)}, f32[4,48,128]{2,1,0:T(8,128)S(1)}, u32[]{:S(2)}, u32[]{:S(2)}) collective-permute-start(f32[4,48,128]{2,1,0:T(8,128)S(1)} %get-tuple-element.39), channel_id=1, source_target_pairs={{32,0},{48,16},{64,32},{80,48},{96,64},{112,80},{128,96},{144,112}... | collective-permute-start | bytes 294920 | tf_op jit(solution)/shard_map/ppermute | solution.py:538
  34.0 17.6 %all-to-all-start = ((f32[16,8,128]{2,1,0:T(8,128)}), f32[16,8,128]{2,1,0:T(8,128)S(1)}, u32[]{:S(2)}, u32[]{:S(2)}) async-start(f32[16,8,128]{2,1,0:T(8,128)} %get-tuple-element.40), calls=%async_computation | async-start | bytes 131072 | tf_op jit(solution)/shard_map/all_to_all | solution.py:615
  43.7 3.1 %collective-permute-start.6 = (f32[2,16,128]{2,1,0:T(8,128)S(1)}, f32[2,16,128]{2,1,0:T(8,128)S(1)}, u32[]{:S(2)}, u32[]{:S(2)}) collective-permute-start(f32[2,16,128]{2,1,0:T(8,128)S(1)} %get-tuple-element.41.ends_ref), channel_id=1, source_target_pairs={{0,1},{1,0},{2,3},{3,2},{4,5},{5,4},{6,7},{7,6},{8,9},{9,8},{10,11... | collective-permute-start | bytes 49160 | tf_op jit(solution)/shard_map/ppermute | solution.py:558
  63.1 16.5 %collective-permute-start.7 = (f32[4,112,128]{2,1,0:T(8,128)S(1)}, f32[4,112,128]{2,1,0:T(8,128)S(1)}, u32[]{:S(2)}, u32[]{:S(2)}) collective-permute-start(f32[4,112,128]{2,1,0:T(8,128)S(1)} %all_to_all.10.mid_ref), channel_id=1, source_target_pairs={{0,64},{65,1},{64,128},{129,65},{128,192},{193,129},{192,256},{257... | collective-permute-start | bytes 688136 | tf_op jit(solution)/shard_map/ppermute | solution.py:546
  64.4 15.2 %collective-permute-start.8 = (f32[4,48,128]{2,1,0:T(8,128)S(1)}, f32[4,48,128]{2,1,0:T(8,128)S(1)}, u32[]{:S(2)}, u32[]{:S(2)}) collective-permute-start(f32[4,48,128]{2,1,0:T(8,128)S(1)} %slice.4), channel_id=1, source_target_pairs={{0,128},{129,1},{64,192},{193,65},{128,256},{257,129},{192,320},{3... | collective-permute-start | bytes 294920 | tf_op jit(solution)/shard_map/ppermute | solution.py:546
  65.7 13.9 %collective-permute-start.9 = (f32[8,128]{1,0:T(8,128)S(1)}, f32[8,128]{1,0:T(8,128)S(1)}, u32[]{:S(2)}, u32[]{:S(2)}) collective-permute-start(f32[8,128]{1,0:T(8,128)S(1)} %get-tuple-element.44), channel_id=1, source_target_pairs={{1,2},{2,1},{3,4},{4,3},{5,6},{6,5},{7,8},{8,7},{9,10},{10,9},{11,... | collective-permute-start | bytes 12296 | tf_op jit(solution)/shard_map/ppermute | solution.py:554
  79.6 3.5 %collective-permute-start.10 = (f32[4,160,128]{2,1,0:T(8,128)S(1)}, f32[4,160,128]{2,1,0:T(8,128)S(1)}, u32[]{:S(2)}, u32[]{:S(2)}) collective-permute-start(f32[4,160,128]{2,1,0:T(8,128)S(1)} %pad_maximum_fusion), channel_id=1, source_target_pairs={{0,1},{1,0},{2,3},{3,2},{4,5},{5,4},{6,7},{7,6},{8,9},{9,8},{10,11... | collective-permute-start | bytes 983048 | tf_op jit(solution)/shard_map/ppermute | solution.py:558

commit v8 on v7

--- a/solution.py
+++ b/solution.py
@@ -547,11 +547,13 @@
 
 
 def shifted_chip(value):
-    pairs = []
-    for i in range(lax.axis_size("za") - 1):
-        pairs.append((2 * i + 1, 2 * i + 2))
-        pairs.append((2 * i + 2, 2 * i + 1))
-    return lax.ppermute(value, GY, pairs)
+    count = lax.axis_size(GY)
+    ring = [(i, (i + 1) % count) for i in range(count)]
+    low = lax.ppermute(value, GY, ring)
+    high = lax.ppermute(value, GY, [(b, a) for a, b in ring])
+    place = lax.axis_index(GY)
+    kept = jnp.where(lax.axis_index("ca") == 0, low, high)
+    return jnp.where((place > 0) & (place < count - 1), kept, 0.0)
 
 
 def swapped(value):

time: 85.8 us -> 85.3 us (level)
  starting transfers between devices: 47.1 us -> 38.7 us
  waiting for transfers between devices: 18.4 us -> 25.8 us
    ppermute x2, waiting for transfers between devices: 0.01 us -> 9.04 us  [parted(): return lax.ppermute(value, ('ya', 'ca'), pairs)]
    ppermute x1 -> x2, starting transfers between devices: 12.6 us -> 3.93 us  [the longest x1 3.79 us: shifted_chip(): high = lax.ppermute(value, GY, [(b, a) for a, b in ring])]
    ppermute x1 -> x2, waiting for transfers between devices: 1.28 us -> 0.01 us  [the longest x1 0.01 us: shifted_chip(): low = lax.ppermute(value, GY, ring)]
  transfers between devices with their start and end apart: 12 -> 13, of which waited for: 8 -> 8; matrix products, arithmetic and copies ran while one was open for 0% -> 0% of each run, Pallas kernels for 0% -> 0%
where the time goes in v8:
time: 85.3 us; the launch traced here: 84.5 us
  starting transfers between devices  38.7 us (45%)
  waiting for transfers between devices  25.8 us (30%)
  blocking collectives  10.9 us (13%)
  Pallas kernels  8.72 us (10%)
    ppermute x4, starting transfers between devices, shifted(): return lax.ppermute(value, axis, pairs)  11.2 us
    all_to_all x1, blocking collectives, shards(): planes = lax.all_to_all(planes, 'xa', 0, 0, tiled=True)  10.9 us
    all_to_all x1, starting transfers between devices, shards(): rows = lax.all_to_all(chunk, GY, 0, 0, tiled=True)  9.76 us
    ppermute x2, waiting for transfers between devices, parted(): return lax.ppermute(value, ('ya', 'ca'), pairs)  9.04 us
    pallas_call x5, Pallas kernels, call(): pl.pallas_call(kernel, in_specs=specs, out_specs=[VMEM] * len(outs), out_...  8.72 us
    ppermute x1, starting transfers between devices, shards(): high = lax.ppermute(own, GY, [(b, a) for a, b in ring])  6.89 us
    ppermute x4, waiting for transfers between devices, shifted(): return lax.ppermute(value, axis, pairs)  5.87 us
    all_to_all x1, waiting for transfers between devices, shards(): rows = lax.all_to_all(chunk, GY, 0, 0, tiled=True)  4.77 us
  transfers between devices with their start and end apart: 13, of which 8 were waited for; matrix products, arithmetic and copies ran while one was open for 0% of the time, Pallas kernels for 0%

profile of v8, /device:TPU:1, one launch (start us, length us, event | category | flops | bytes accessed | tf_op | source)
XLA Modules:
  0.0 84.5 jit_solution(12203571349509051492)
XLA Ops:
  0.0 1.2 %shard_map.37 = (f32[4,2,4,8,128]{4,3,2,1,0:T(8,128)S(1)}, f32[8,128]{1,0:T(8,128)S(1)}) custom-call(f32[3]{0:T(128)} %table_hbm.1, s32[4,8,512]{2,1,0:T(8,128)} %labels_hbm.1, f32[4,8,512]{2,1,0:T(8,128)} %source_hbm.1), custom_call_target="tpu_custom_call" | custom-call | tf_op jit(solution)/shard_map/pallas_call | solution.py:522
  1.2 6.9 %collective-permute-start.1 = (f32[4,2,4,8,128]{4,3,2,1,0:T(8,128)S(1)}, f32[4,2,4,8,128]{4,3,2,1,0:T(8,128)S(1)}, u32[]{:S(2)}, u32[]{:S(2)}) collective-permute-start(f32[4,2,4,8,128]{4,3,2,1,0:T(8,128)S(1)} %get-tuple-element.34.own_ref), channel_id=1, source_target_pairs={{1,0},{2,1},{3,2},{4,3},{5,4},{6,5},{7,6},{8,7},{9,8},{10,9},{11,1... | collective-permute-start | bytes 393224 | tf_op jit(solution)/shard_map/ppermute | solution.py:587
  8.1 0.0 collective-permute-start
  8.1 1.0 %collective-permute-done.1.high_ref = f32[4,2,4,8,128]{4,3,2,1,0:T(8,128)S(1)} collective-permute-done((f32[4,2,4,8,128]{4,3,2,1,0:T(8,128)S(1)}, f32[4,2,4,8,128]{4,3,2,1,0:T(8,128)S(1)}, u32[]{:S(2)}, u32[]{:S(2)}) %collective-permute-start.1) | collective-permute-done | bytes 131104 | tf_op jit(solution)/shard_map/ppermute | solution.py:587
  9.1 3.0 %collective-permute-done.low_ref = f32[4,2,4,8,128]{4,3,2,1,0:T(8,128)S(1)} collective-permute-done((f32[4,2,4,8,128]{4,3,2,1,0:T(8,128)S(1)}, f32[4,2,4,8,128]{4,3,2,1,0:T(8,128)S(1)}, u32[]{:S(2)}, u32[]{:S(2)}) %collective-permute-start) | collective-permute-done | bytes 131104 | tf_op jit(solution)/shard_map/ppermute | solution.py:586
  12.0 0.1 shard_map.38
  12.1 3.1 %collective-permute-start.3 = (f32[4,128,128]{2,1,0:T(8,128)S(1)}, f32[4,128,128]{2,1,0:T(8,128)S(1)}, u32[]{:S(2)}, u32[]{:S(2)}) collective-permute-start(f32[4,128,128]{2,1,0:T(8,128)S(1)} %get-tuple-element.36), channel_id=1, source_target_pairs={{0,16},{16,32},{32,48},{48,64},{64,80},{80,96},{96,112},{112,128},... | collective-permute-start | bytes 786440 | tf_op jit(solution)/shard_map/ppermute | solution.py:538
  15.2 1.3 %collective-permute-start.4 = (f32[4,128,128]{2,1,0:T(8,128)S(1)}, f32[4,128,128]{2,1,0:T(8,128)S(1)}, u32[]{:S(2)}, u32[]{:S(2)}) collective-permute-start(f32[4,128,128]{2,1,0:T(8,128)S(1)} %get-tuple-element.38), channel_id=1, source_target_pairs={{16,0},{32,16},{48,32},{64,48},{80,64},{96,80},{112,96},{128,112},... | collective-permute-start | bytes 786440 | tf_op jit(solution)/shard_map/ppermute | solution.py:538
  16.5 5.5 %collective-permute-start.2 = (f32[4,48,128]{2,1,0:T(8,128)S(1)}, f32[4,48,128]{2,1,0:T(8,128)S(1)}, u32[]{:S(2)}, u32[]{:S(2)}) collective-permute-start(f32[4,48,128]{2,1,0:T(8,128)S(1)} %get-tuple-element.35), channel_id=1, source_target_pairs={{0,32},{16,48},{32,64},{48,80},{64,96},{80,112},{96,128},{112,144}... | collective-permute-start | bytes 294920 | tf_op jit(solution)/shard_map/ppermute | solution.py:538
  22.1 1.3 %collective-permute-start.5 = (f32[4,48,128]{2,1,0:T(8,128)S(1)}, f32[4,48,128]{2,1,0:T(8,128)S(1)}, u32[]{:S(2)}, u32[]{:S(2)}) collective-permute-start(f32[4,48,128]{2,1,0:T(8,128)S(1)} %get-tuple-element.39), channel_id=1, source_target_pairs={{32,0},{48,16},{64,32},{80,48},{96,64},{112,80},{128,96},{144,112}... | collective-permute-start | bytes 294920 | tf_op jit(solution)/shard_map/ppermute | solution.py:538
  23.4 0.1 stack.19.spot_ref
  23.5 1.3 %collective-permute-done.2.low2_ref = f32[4,48,128]{2,1,0:T(8,128)S(1)} collective-permute-done((f32[4,48,128]{2,1,0:T(8,128)S(1)}, f32[4,48,128]{2,1,0:T(8,128)S(1)}, u32[]{:S(2)}, u32[]{:S(2)}) %collective-permute-start.2) | collective-permute-done | bytes 98336 | tf_op jit(solution)/shard_map/ppermute | solution.py:538
  24.7 4.6 %collective-permute-done.5.high2_ref = f32[4,48,128]{2,1,0:T(8,128)S(1)} collective-permute-done((f32[4,48,128]{2,1,0:T(8,128)S(1)}, f32[4,48,128]{2,1,0:T(8,128)S(1)}, u32[]{:S(2)}, u32[]{:S(2)}) %collective-permute-start.5) | collective-permute-done | bytes 98336 | tf_op jit(solution)/shard_map/ppermute | solution.py:538
  29.3 0.0 collective-permute-done.3.low1_ref
  29.3 0.0 collective-permute-done.4.high1_ref
  29.3 4.6 %shard_map.39 = (f32[16,8,128]{2,1,0:T(8,128)}, f32[2,16,128]{2,1,0:T(8,128)S(1)}, f32[8,128]{1,0:T(8,128)S(1)}, f32[5,4,8,128]{3,2,1,0:T(8,128)S(1)}, f32[4,4,2...) custom-call(s32[6]{0:T(128)S(1)} %stack.19.spot_ref, ...), custom_call_target="tpu_custom_call" | custom-call | tf_op jit(solution)/shard_map/pallas_call | solution.py:522
  34.0 9.8 %all-to-all-start = ((f32[16,8,128]{2,1,0:T(8,128)}), f32[16,8,128]{2,1,0:T(8,128)S(1)}, u32[]{:S(2)}, u32[]{:S(2)}) async-start(f32[16,8,128]{2,1,0:T(8,128)} %get-tuple-element.40), calls=%async_computation | async-start | bytes 131072 | tf_op jit(solution)/shard_map/all_to_all | solution.py:617
  43.7 2.1 %collective-permute-start.6 = (f32[2,16,128]{2,1,0:T(8,128)S(1)}, f32[2,16,128]{2,1,0:T(8,128)S(1)}, u32[]{:S(2)}, u32[]{:S(2)}) collective-permute-start(f32[2,16,128]{2,1,0:T(8,128)S(1)} %get-tuple-element.41.ends_ref), channel_id=1, source_target_pairs={{0,1},{1,0},{2,3},{3,2},{4,5},{5,4},{6,7},{7,6},{8,9},{9,8},{10,11... | collective-permute-start | bytes 49160 | tf_op jit(solution)/shard_map/ppermute | solution.py:560
  45.8 0.9 %collective-permute-done.6.other_ref = f32[2,16,128]{2,1,0:T(8,128)S(1)} collective-permute-done((f32[2,16,128]{2,1,0:T(8,128)S(1)}, f32[2,16,128]{2,1,0:T(8,128)S(1)}, u32[]{:S(2)}, u32[]{:S(2)}) %collective-permute-start.6) | collective-permute-done | bytes 16416 | tf_op jit(solution)/shard_map/ppermute | solution.py:560
  46.8 4.8 %all-to-all-done.got_ref = f32[16,8,128]{2,1,0:T(8,128)S(1)} async-done(((f32[16,8,128]{2,1,0:T(8,128)}), f32[16,8,128]{2,1,0:T(8,128)S(1)}, u32[]{:S(2)}, u32[]{:S(2)}) %all-to-all-start) | async-done | bytes 65568 | tf_op jit(solution)/shard_map/all_to_all | solution.py:617
  51.6 0.6 shard_map.40
  52.2 10.9 %all_to_all.10.mid_ref = f32[4,112,128]{2,1,0:T(8,128)S(1)} all-to-all(f32[4,112,128]{2,1,0:T(8,128)S(1)} %shard_map.40), channel_id=1, replica_groups=mesh['ya'=8,'xa'=4,'za'=8,'ca'=2] {'xa'}, dimensions={0} | all-to-all | bytes 458752 | tf_op jit(solution)/shard_map/all_to_all | solution.py:623
  63.1 1.3 %collective-permute-start.7 = (f32[4,112,128]{2,1,0:T(8,128)S(1)}, f32[4,112,128]{2,1,0:T(8,128)S(1)}, u32[]{:S(2)}, u32[]{:S(2)}) collective-permute-start(f32[4,112,128]{2,1,0:T(8,128)S(1)} %all_to_all.10.mid_ref), channel_id=1, source_target_pairs={{0,64},{65,1},{64,128},{129,65},{128,192},{193,129},{192,256},{257... | collective-permute-start | bytes 688136 | tf_op jit(solution)/shard_map/ppermute | solution.py:546
  64.4 3.8 %collective-permute-start.10 = (f32[8,128]{1,0:T(8,128)S(1)}, f32[8,128]{1,0:T(8,128)S(1)}, u32[]{:S(2)}, u32[]{:S(2)}) collective-permute-start(f32[8,128]{1,0:T(8,128)S(1)} %get-tuple-element.44), channel_id=1, source_target_pairs={{1,0},{2,1},{3,2},{4,3},{5,4},{6,5},{7,6},{8,7},{9,8},{10,9},{11,1... | collective-permute-start | bytes 12296 | tf_op jit(solution)/shard_map/ppermute | solution.py:553
  68.2 0.1 collective-permute-start.9
  68.3 1.3 %collective-permute-start.8 = (f32[4,48,128]{2,1,0:T(8,128)S(1)}, f32[4,48,128]{2,1,0:T(8,128)S(1)}, u32[]{:S(2)}, u32[]{:S(2)}) collective-permute-start(f32[4,48,128]{2,1,0:T(8,128)S(1)} %slice.4), channel_id=1, source_target_pairs={{0,128},{129,1},{64,192},{193,65},{128,256},{257,129},{192,320},{3... | collective-permute-start | bytes 294920 | tf_op jit(solution)/shard_map/ppermute | solution.py:546
  69.6 0.0 collective-permute-done.10
  69.6 0.0 collective-permute-done.9
  69.6 9.0 %collective-permute-done.8.took2_ref = f32[4,48,128]{2,1,0:T(8,128)S(1)} collective-permute-done((f32[4,48,128]{2,1,0:T(8,128)S(1)}, f32[4,48,128]{2,1,0:T(8,128)S(1)}, u32[]{:S(2)}, u32[]{:S(2)}) %collective-permute-start.8) | collective-permute-done | bytes 98336 | tf_op jit(solution)/shard_map/ppermute | solution.py:546
  78.7 0.0 collective-permute-done.7.took1_ref
  78.7 2.2 %collective-permute-start.11 = (f32[4,160,128]{2,1,0:T(8,128)S(1)}, f32[4,160,128]{2,1,0:T(8,128)S(1)}, u32[]{:S(2)}, u32[]{:S(2)}) collective-permute-start(f32[4,160,128]{2,1,0:T(8,128)S(1)} %pad_maximum_fusion), channel_id=1, source_target_pairs={{0,1},{1,0},{2,3},{3,2},{4,5},{5,4},{6,7},{7,6},{8,9},{9,8},{10,11... | collective-permute-start | bytes 983048 | tf_op jit(solution)/shard_map/ppermute | solution.py:560
  80.9 1.3 %collective-permute-done.11.gave_ref = f32[4,160,128]{2,1,0:T(8,128)S(1)} collective-permute-done((f32[4,160,128]{2,1,0:T(8,128)S(1)}, f32[4,160,128]{2,1,0:T(8,128)S(1)}, u32[]{:S(2)}, u32[]{:S(2)}) %collective-permute-start.11) | collective-permute-done | bytes 327712 | tf_op jit(solution)/shard_map/ppermute | solution.py:560
  82.2 2.2 %shard_map.41 = f32[4,8,512]{2,1,0:T(8,128)} custom-call(s32[6]{0:T(128)S(1)} %stack.19.spot_ref, f32[4,112,128]{2,1,0:T(8,128)S(1)} %collective-permute-done.7.took1_ref, f32[4,48,128]{2,1,0:T(8,128)S(1)} %collective-permute-done.8.took2_ref, f32[4,112,128]{2,1,0:T(8,128)S(1)} %all_to_all.10.mid_ref, f32[4,160,128]{2,1,0:T(8,128)S(1)} %collective-permute-done.11.gave_ref, ...), custom_call_target="tpu_custom_call" | custom-call | tf_op jit(solution)/shard_map/pallas_call | solution.py:522
  (3 shorter events, 0.0 us)
Async XLA Ops:
  1.2 7.9 %collective-permute-start.1 = (f32[4,2,4,8,128]{4,3,2,1,0:T(8,128)S(1)}, f32[4,2,4,8,128]{4,3,2,1,0:T(8,128)S(1)}, u32[]{:S(2)}, u32[]{:S(2)}) collective-permute-start(f32[4,2,4,8,128]{4,3,2,1,0:T(8,128)S(1)} %get-tuple-element.34.own_ref), channel_id=1, source_target_pairs={{1,0},{2,1},{3,2},{4,3},{5,4},{6,5},{7,6},{8,7},{9,8},{10,9},{11,1... | collective-permute-start | bytes 393224 | tf_op jit(solution)/shard_map/ppermute | solution.py:587
  8.1 3.9 %collective-permute-start = (f32[4,2,4,8,128]{4,3,2,1,0:T(8,128)S(1)}, f32[4,2,4,8,128]{4,3,2,1,0:T(8,128)S(1)}, u32[]{:S(2)}, u32[]{:S(2)}) collective-permute-start(f32[4,2,4,8,128]{4,3,2,1,0:T(8,128)S(1)} %get-tuple-element.34.own_ref), channel_id=1, source_target_pairs={{0,1},{1,2},{2,3},{3,4},{4,5},{5,6},{6,7},{7,8},{8,9},{9,10},{10,1... | collective-permute-start | bytes 393224 | tf_op jit(solution)/shard_map/ppermute | solution.py:586
  12.1 17.2 %collective-permute-start.3 = (f32[4,128,128]{2,1,0:T(8,128)S(1)}, f32[4,128,128]{2,1,0:T(8,128)S(1)}, u32[]{:S(2)}, u32[]{:S(2)}) collective-permute-start(f32[4,128,128]{2,1,0:T(8,128)S(1)} %get-tuple-element.36), channel_id=1, source_target_pairs={{0,16},{16,32},{32,48},{48,64},{64,80},{80,96},{96,112},{112,128},... | collective-permute-start | bytes 786440 | tf_op jit(solution)/shard_map/ppermute | solution.py:538
  15.2 14.1 %collective-permute-start.4 = (f32[4,128,128]{2,1,0:T(8,128)S(1)}, f32[4,128,128]{2,1,0:T(8,128)S(1)}, u32[]{:S(2)}, u32[]{:S(2)}) collective-permute-start(f32[4,128,128]{2,1,0:T(8,128)S(1)} %get-tuple-element.38), channel_id=1, source_target_pairs={{16,0},{32,16},{48,32},{64,48},{80,64},{96,80},{112,96},{128,112},... | collective-permute-start | bytes 786440 | tf_op jit(solution)/shard_map/ppermute | solution.py:538
  16.5 8.2 %collective-permute-start.2 = (f32[4,48,128]{2,1,0:T(8,128)S(1)}, f32[4,48,128]{2,1,0:T(8,128)S(1)}, u32[]{:S(2)}, u32[]{:S(2)}) collective-permute-start(f32[4,48,128]{2,1,0:T(8,128)S(1)} %get-tuple-element.35), channel_id=1, source_target_pairs={{0,32},{16,48},{32,64},{48,80},{64,96},{80,112},{96,128},{112,144}... | collective-permute-start | bytes 294920 | tf_op jit(solution)/shard_map/ppermute | solution.py:538
  22.1 7.3 %collective-permute-start.5 = (f32[4,48,128]{2,1,0:T(8,128)S(1)}, f32[4,48,128]{2,1,0:T(8,128)S(1)}, u32[]{:S(2)}, u32[]{:S(2)}) collective-permute-start(f32[4,48,128]{2,1,0:T(8,128)S(1)} %get-tuple-element.39), channel_id=1, source_target_pairs={{32,0},{48,16},{64,32},{80,48},{96,64},{112,80},{128,96},{144,112}... | collective-permute-start | bytes 294920 | tf_op jit(solution)/shard_map/ppermute | solution.py:538
  34.0 17.6 %all-to-all-start = ((f32[16,8,128]{2,1,0:T(8,128)}), f32[16,8,128]{2,1,0:T(8,128)S(1)}, u32[]{:S(2)}, u32[]{:S(2)}) async-start(f32[16,8,128]{2,1,0:T(8,128)} %get-tuple-element.40), calls=%async_computation | async-start | bytes 131072 | tf_op jit(solution)/shard_map/all_to_all | solution.py:617
  43.7 3.1 %collective-permute-start.6 = (f32[2,16,128]{2,1,0:T(8,128)S(1)}, f32[2,16,128]{2,1,0:T(8,128)S(1)}, u32[]{:S(2)}, u32[]{:S(2)}) collective-permute-start(f32[2,16,128]{2,1,0:T(8,128)S(1)} %get-tuple-element.41.ends_ref), channel_id=1, source_target_pairs={{0,1},{1,0},{2,3},{3,2},{4,5},{5,4},{6,7},{7,6},{8,9},{9,8},{10,11... | collective-permute-start | bytes 49160 | tf_op jit(solution)/shard_map/ppermute | solution.py:560
  63.1 15.6 %collective-permute-start.7 = (f32[4,112,128]{2,1,0:T(8,128)S(1)}, f32[4,112,128]{2,1,0:T(8,128)S(1)}, u32[]{:S(2)}, u32[]{:S(2)}) collective-permute-start(f32[4,112,128]{2,1,0:T(8,128)S(1)} %all_to_all.10.mid_ref), channel_id=1, source_target_pairs={{0,64},{65,1},{64,128},{129,65},{128,192},{193,129},{192,256},{257... | collective-permute-start | bytes 688136 | tf_op jit(solution)/shard_map/ppermute | solution.py:546
  64.4 5.2 %collective-permute-start.10 = (f32[8,128]{1,0:T(8,128)S(1)}, f32[8,128]{1,0:T(8,128)S(1)}, u32[]{:S(2)}, u32[]{:S(2)}) collective-permute-start(f32[8,128]{1,0:T(8,128)S(1)} %get-tuple-element.44), channel_id=1, source_target_pairs={{1,0},{2,1},{3,2},{4,3},{5,4},{6,5},{7,6},{8,7},{9,8},{10,9},{11,1... | collective-permute-start | bytes 12296 | tf_op jit(solution)/shard_map/ppermute | solution.py:553
  68.2 1.4 %collective-permute-start.9 = (f32[8,128]{1,0:T(8,128)S(1)}, f32[8,128]{1,0:T(8,128)S(1)}, u32[]{:S(2)}, u32[]{:S(2)}) collective-permute-start(f32[8,128]{1,0:T(8,128)S(1)} %get-tuple-element.44), channel_id=1, source_target_pairs={{0,1},{1,2},{2,3},{3,4},{4,5},{5,6},{6,7},{7,8},{8,9},{9,10},{10,1... | collective-permute-start | bytes 12296 | tf_op jit(solution)/shard_map/ppermute | solution.py:552
  68.3 10.4 %collective-permute-start.8 = (f32[4,48,128]{2,1,0:T(8,128)S(1)}, f32[4,48,128]{2,1,0:T(8,128)S(1)}, u32[]{:S(2)}, u32[]{:S(2)}) collective-permute-start(f32[4,48,128]{2,1,0:T(8,128)S(1)} %slice.4), channel_id=1, source_target_pairs={{0,128},{129,1},{64,192},{193,65},{128,256},{257,129},{192,320},{3... | collective-permute-start | bytes 294920 | tf_op jit(solution)/shard_map/ppermute | solution.py:546
  78.7 3.5 %collective-permute-start.11 = (f32[4,160,128]{2,1,0:T(8,128)S(1)}, f32[4,160,128]{2,1,0:T(8,128)S(1)}, u32[]{:S(2)}, u32[]{:S(2)}) collective-permute-start(f32[4,160,128]{2,1,0:T(8,128)S(1)} %pad_maximum_fusion), channel_id=1, source_target_pairs={{0,1},{1,0},{2,3},{3,2},{4,5},{5,4},{6,7},{7,6},{8,9},{9,8},{10,11... | collective-permute-start | bytes 983048 | tf_op jit(solution)/shard_map/ppermute | solution.py:560
